TPU v7x, 32 devices: a whole 2x2x4 slice. The times are simulated.
32 devices in a mesh: slot: 4 (over z), pb: 8 (over y, x, core).
Axes of the slice: x: 2, y: 2, z: 4, core: 2. Of those that a mesh axis runs over, the one named last changes fastest.
Arguments:
- inputs: bfloat16 [8, 4, 64, 1024], P('pb', 'slot'), may hold values from -6 to 6
- memory: bfloat16 [8, 4, 128, 1024], P('pb', 'slot'), may hold values from -6 to 6
- attn_weight: bfloat16 [1024, 6, 1024], P('pb'), may hold values from -0.1875 to 0.1875
- attn_out: bfloat16 [1024, 2, 1024], P('pb'), may hold values from -0.75 to 0.75
- ffn_in: bfloat16 [1024, 4096], P('pb'), may hold values from -0.1875 to 0.1875
- ffn_out: bfloat16 [4096, 1024], P('pb'), may hold values from -0.09375 to 0.09375
- attn_bias: float32 [1024, 6], replicated, may hold values from -3 to 3
- norm_gain: float32 [1024, 3], replicated, may hold values from 0.5 to 1.5
- norm_bias: float32 [1024, 3], replicated, may hold values from -2 to 2
- bias_in: float32 [4096], replicated, may hold values from -3 to 3
- bias_out: float32 [1024], replicated, may hold values from -2 to 2
- embedding: bfloat16 [32768, 1024], P('pb'), may hold values from -0.375 to 0.375
- targets: int32 [8, 64], replicated, may hold values from 0 to 32767
- slot_counts: int32 [8], replicated, may hold values from 2 to 4
- pad_mask: int32 [8, 64], P('pb'), may hold values 0 or 1
- log_prior: float32 [8, 4], P('pb', 'slot'), may hold values from -4 to 4
Outputs:
- token_logprob: float32 [8, 64], P('pb')
- grad_inputs: float32 [8, 4, 64, 1024], P('pb', 'slot')
- grad_memory: float32 [8, 4, 128, 1024], P('pb', 'slot')
- grad_log_prior: float32 [8, 4], P('pb', 'slot')
- grad_attn_weight: float32 [1024, 6, 1024], P(('slot', 'pb'))
- grad_attn_out: float32 [1024, 2, 1024], P(('slot', 'pb'))
- grad_ffn_in: float32 [1024, 4096], P(('slot', 'pb'))
- grad_ffn_out: float32 [4096, 1024], P(('slot', 'pb'))
- grad_attn_bias: float32 [1024, 6], P(('slot', 'pb'))
- grad_norm_gain: float32 [1024, 3], P(('slot', 'pb'))
- grad_norm_bias: float32 [1024, 3], P(('slot', 'pb'))
- grad_bias_in: float32 [4096], P(('slot', 'pb'))
- grad_bias_out: float32 [1024], P(('slot', 'pb'))
- grad_embedding: float32 [32768, 1024], P('pb')
Inputs may be any that keep to these rules, and one draw needn't show every extreme that they name: Slots 0 to slot_counts[q] - 1 of question q hold passages; the others are padding.
All inputs are finite; a program needn't handle non-finite values. No bound on the sum of `pad_mask` on one device may be relied on, other than what follows from the above.
Results may differ from a plain program's by a relative error of at most 0.029.
Values may be sent and summed in bfloat16 or wider, within the bound.
No kernel may reach another device: no remote copies, remote signals or barrier semaphores. Data moves between devices by JAX's collectives and lax.ppermute only.
A program may use at most 320 MiB of HBM per device.

v0:
```python
import functools

import jax
import jax.numpy as jnp
from jax import lax
from jax.experimental import pallas as pl
from jax.experimental.pallas import tpu as pltpu
from jax.sharding import PartitionSpec as P

HEAD = 64
CHIPS = 4
CORES = 2
TEAM = CHIPS * CORES
SLOTS = 4
BF = jnp.bfloat16
F32 = jnp.float32
TOKENS = 512
VOCAB_TILE = 512


def from_chip(x, k):
    pairs = []
    for i in range(lax.axis_size("pb")):
        place = i % TEAM
        pairs.append((i, i - place + ((place // CORES) ^ k) * CORES + place % CORES))
    return lax.ppermute(x, "pb", pairs)


def from_core(x):
    return lax.ppermute(x, "pb", [(i, i ^ 1) for i in range(lax.axis_size("pb"))])


def across_slot(x, k):
    return lax.ppermute(x, "slot", [(i, i ^ k) for i in range(lax.axis_size("slot"))])


def same_place_groups():
    size = lax.axis_size("pb")
    return [[g * TEAM + j for g in range(size // TEAM)] for j in range(TEAM)]


def team_groups():
    size = lax.axis_size("pb")
    return [[g * TEAM + j for j in range(TEAM)] for g in range(size // TEAM)]


def others(x):
    return [from_chip(x, k) for k in range(1, CHIPS)]


def tie(*values):
    return list(lax.optimization_barrier(values))


def across_slots(x):
    return lax.all_to_all(x, "slot", 0, 0, tiled=True)


def at(x, index):
    return lax.dynamic_index_in_dim(x, index, 0, False)


NN = (((1,), (0,)), ((), ()))
NT = (((1,), (1,)), ((), ()))
TN = (((0,), (0,)), ((), ()))


def dot(a, b, dims=NN):
    return lax.dot_general(a, b, dims, preferred_element_type=F32)


def place():
    j = lax.axis_index("pb") % TEAM
    return j // CORES, j % CORES


def rows_at(start, size, unit):
    return pl.ds(pl.multiple_of(start, unit), size)


MIB = 2**20


def limit(mib):
    return pltpu.CompilerParams(vmem_limit_bytes=min(60, mib) * MIB)


def work(us):
    return pl.CostEstimate(flops=int(us * 1e9), bytes_accessed=0, transcendentals=0)


def call(kernel, outs, *args, us=2.0, far=False, scratch=()):
    shapes = [jax.ShapeDtypeStruct(*o) for o in outs]
    held = sum(a.size * a.dtype.itemsize for a in (*args, *shapes))
    params = limit(8 + held * 5 // 4 // MIB)
    places = [pltpu.HBM(*o) for o in outs] if far else shapes
    results = pl.pallas_call(
        kernel, out_shape=places, scratch_shapes=scratch, compiler_params=params, cost_estimate=work(us)
    )(*args)
    return [in_hbm(r) for r in results] if far else results


def in_hbm(x):
    return pltpu.with_memory_space_constraint(x, pltpu.HBM)


def norm_rows(r, gain, shift):
    centered = r - jnp.mean(r, axis=-1, keepdims=True)
    inv = lax.rsqrt(jnp.mean(centered * centered, axis=-1, keepdims=True) + 1e-05)
    z = centered * inv
    return z * gain + shift, z, inv


def norm_back(dh, z, inv, gain):
    dz = dh * gain
    return (dz - jnp.mean(dz, axis=-1, keepdims=True) - z * jnp.mean(dz * z, axis=-1, keepdims=True)) * inv


def lane_head(shape, keys):
    return lax.broadcasted_iota(jnp.int32, shape, 1) // keys


def per_head(x):
    head = lane_head(x.shape, HEAD)
    return jnp.concatenate([jnp.where(head == h, x, jnp.zeros_like(x)) for h in range(x.shape[1] // HEAD)], axis=0)


def own_heads(big, keys):
    count = big.shape[1] // HEAD
    head = lane_head((keys, big.shape[1]), HEAD)
    total = jnp.zeros((keys, big.shape[1]), F32)
    for h in range(count):
        total = total + jnp.where(head == h, big[h * keys : (h + 1) * keys], 0.0)
    return total


def head_probs(q, kbig, keys, causal):
    s = dot(q, kbig, NT) * 0.125
    head = lane_head(s.shape, keys)
    count = s.shape[1] // keys
    if causal:
        query = lax.broadcasted_iota(jnp.int32, s.shape, 0)
        key = lax.broadcasted_iota(jnp.int32, s.shape, 1) % keys
        s = jnp.where(query >= key, s, -1e30)
    peak = jnp.zeros_like(s)
    for h in range(count):
        m = jnp.max(jnp.where(head == h, s, -3e38), axis=1, keepdims=True)
        peak = jnp.where(head == h, m, peak)
    e = jnp.exp(s - peak)
    return e / head_sums(e, head, count)


def head_sums(x, head, count):
    total = jnp.zeros_like(x)
    for h in range(count):
        total = jnp.where(head == h, jnp.sum(jnp.where(head == h, x, 0.0), axis=1, keepdims=True), total)
    return total


def attend(q, k, v, causal):
    probs = head_probs(q, per_head(k), k.shape[0], causal)
    return dot(probs.astype(BF), per_head(v)).astype(BF)


def attend_back(g, q, k, v, causal):
    keys = k.shape[0]
    kbig, vbig = per_head(k), per_head(v)
    probs = head_probs(q, kbig, keys, causal)
    dp = dot(g, vbig, NT)
    head = lane_head(dp.shape, keys)
    ds = (probs * (dp - head_sums(dp * probs, head, dp.shape[1] // keys))).astype(BF)
    dq = dot(ds, kbig) * 0.125
    dk = own_heads(dot(ds, q, TN), keys) * 0.125
    dv = own_heads(dot(probs.astype(BF), g, TN), keys)
    return dq.astype(BF), dk.astype(BF), dv.astype(BF)


def pack_kernel(count, first, *refs):
    *rows_in, w_ref, o0, o1, o2, o3 = refs
    outs = (o0, o1, o2, o3)
    chip, _ = place()
    rows, quarter = w_ref.shape[1], w_ref.shape[2] // CHIPS
    for k in range(CHIPS):
        top = 0
        for x_ref in rows_in:
            x = x_ref[...]
            for b in range(CHIPS):
                outs[k][top : top + x.shape[0], :] = x[:, b * quarter : (b + 1) * quarter]
                top += x.shape[0]
        for j in range(count):
            outs[k][top : top + rows, :] = w_ref[first + j, :, rows_at((chip ^ k) * quarter, quarter, 128)]
            top += rows


def natural_columns(own, pair, w_out, top, count):
    chip, core = place()
    rows = w_out.shape[0] // TEAM
    quarter = own[0].shape[1]
    for k in range(CHIPS):
        for refs, c in ((own, core), (pair, 1 - core)):
            start = (chip ^ k) * (CORES * rows) + c * rows
            for j in range(count):
                w_out[rows_at(start, rows, 16), j * quarter : (j + 1) * quarter] = refs[k][
                    top + j * rows : top + (j + 1) * rows, :
                ]


def half_columns(parts, out, top, count):
    chip, _ = place()
    rows = (parts[0].shape[0] - top) // count
    quarter = parts[0].shape[1]
    for k in range(CHIPS):
        for j in range(count):
            out[chip ^ k, :, j * quarter : (j + 1) * quarter] = parts[k][top + j * rows : top + (j + 1) * rows, :]


def whole_columns(mine, pair, out):
    _, core = place()
    rows = mine.shape[1]
    for b in range(CHIPS):
        for part, c in ((mine, core), (pair, 1 - core)):
            out[rows_at(b * CORES * rows + c * rows, rows, 16), :] = part[b]


def pair_rows(own, pair):
    _, core = place()
    a, b = own[...], pair[...]
    return jnp.concatenate([jnp.where(core == 0, a, b), jnp.where(core == 0, b, a)], axis=0)


def self_kernel(*refs):
    own, pair, (o_own, o_pair, vec) = refs[:4], refs[4:8], refs[8:11]
    x_out, w_out, q_out, k_out, v_out, o_out, wo_out, mine_out = refs[11:19]
    send = refs[19:]
    chip, _ = place()
    quarter = own[0].shape[1]
    length = x_out.shape[0] // CHIPS
    natural_columns(own, pair, w_out, CHIPS * length, 3)
    for k in range(CHIPS):
        for b in range(CHIPS):
            x_out[k * length : (k + 1) * length, b * quarter : (b + 1) * quarter] = own[k][b * length : (b + 1) * length, :]
    for j in range(2):
        wo_out[j] = pair_rows(o_own.at[j], o_pair.at[j])
    lanes = rows_at(chip * quarter, quarter, 128)
    y = dot(x_out[...], w_out[...])
    q = (y[:, :quarter] + vec[0:1, lanes]).astype(BF)
    k = y[:, quarter : 2 * quarter].astype(BF)
    v = (y[:, 2 * quarter :] + vec[1:2, lanes]).astype(BF)
    q_out[...], k_out[...], v_out[...] = q, k, v

    def pair(i, carry):
        for j in range(2):
            s = rows_at((2 * i + j) * length, length, 16)
            o_out[s, :] = attend(q_out[s, :], k_out[s, :], v_out[s, :], True)
        return carry

    lax.fori_loop(0, CHIPS // 2, pair, 0)
    split_rows(dot(o_out[...], wo_out[0]), mine_out, send)


def half_kernel(*refs):
    half_columns(refs[:4], refs[4], 0, 3)


def memory_kernel(*refs):
    mem, own, pair, vec, (m_out, w_out, k_out, v_out) = refs[:4], refs[4:8], refs[8:12], refs[12], refs[13:]
    chip, _ = place()
    quarter = k_out.shape[1]
    natural_columns(own, pair, w_out, own[0].shape[0] - 3 * w_out.shape[0] // TEAM, 3)
    m_out[...] = stack_rows(mem)
    y = dot(m_out[...], w_out[:, quarter:])
    k_out[...] = y[:, :quarter].astype(BF)
    v_out[...] = (y[:, quarter:] + vec[4:5, rows_at(chip * quarter, quarter, 128)]).astype(BF)


def norm_kernel(rows, *refs):
    base, mine, r1, r2, r3, vec, h_out, low_out, z_out, inv_out = refs
    y = mine[...] + r1[...].astype(F32) + r2[...].astype(F32) + r3[...].astype(F32)
    r = base[...].astype(F32) + y + vec[rows[0] : rows[0] + 1, :]
    h, z, inv = norm_rows(r, vec[rows[1] : rows[1] + 1, :], vec[rows[2] : rows[2] + 1, :])
    h_out[...] = h
    low_out[...] = h.astype(BF)
    z_out[...] = z
    inv_out[...] = inv


def cross_kernel(*refs):
    parts, (wo, w_cols, keys, values, vec), (low_out, q_out, o_out, mine_out), send = refs[:4], refs[4:9], refs[9:13], refs[13:]
    chip, _ = place()
    quarter = keys.shape[1]
    length = parts[0].shape[0]
    memory = keys.shape[0] // CHIPS
    low = stack_rows(parts)
    low_out[...] = low
    q = (dot(low, w_cols[:, :quarter]) + vec[3:4, rows_at(chip * quarter, quarter, 128)]).astype(BF)
    q_out[...] = q

    def pair(i, carry):
        for j in range(2):
            s, t = rows_at((2 * i + j) * length, length, 16), rows_at((2 * i + j) * memory, memory, 16)
            o_out[s, :] = attend(q_out[s, :], keys[t, :], values[t, :], False)
        return carry

    lax.fori_loop(0, CHIPS // 2, pair, 0)
    split_rows(dot(o_out[...], wo[1]), mine_out, send)


def gelu_parts(u):
    phi = 0.5 * (1.0 + lax.erf(u * 0.7071067811865476))
    return phi


def up_half_kernel(*refs):
    half_columns(refs[:4], refs[4], 0, 1)


def ffn_kernel(*refs):
    parts, (up_mine, up_pair, down_own, down_pair, vec) = refs[:4], refs[4:9]
    low_out, u_out, a_out, up_out, down_out, mine_out = refs[9:15]
    send = refs[15:]
    chip, _ = place()
    whole_columns(up_mine, up_pair, up_out)
    down_out[...] = pair_rows(down_own, down_pair)
    low = stack_rows(parts)
    low_out[...] = low
    u = dot(low, up_out[...]) + vec[pl.ds(13 + chip, 1), :]
    u_out[...] = u
    a_out[...] = (u * gelu_parts(u)).astype(BF)
    split_rows(dot(a_out[...], down_out[...]), mine_out, send)


def stack_kernel(r0, r1, r2, r3, out, spread_out):
    n = r0.shape[0]
    for k, part in enumerate((r0, r1, r2, r3)):
        out[k * n : (k + 1) * n, :] = part[...]
        for slot in range(SLOTS):
            spread_out[slot, k * n : (k + 1) * n, :] = part[...]


def logits_kernel(length, h0_ref, h1_ref, ids_ref, own_ref, e_ref, l_ref, pay_ref, h_ref, m_ref, s_ref, p_ref):
    i = pl.program_id(0)
    half = h0_ref.shape[0]

    @pl.when(i == 0)
    def _():
        h_ref[:half, :] = h0_ref[...]
        h_ref[half:, :] = h1_ref[...]
        m_ref[...] = jnp.full_like(m_ref, -3e38)
        s_ref[...] = jnp.zeros_like(s_ref)
        p_ref[...] = jnp.zeros_like(p_ref)

    x = dot(e_ref[...], h_ref[...], NT)
    l_ref[...] = x
    entry = lax.broadcasted_iota(jnp.int32, x.shape, 0) + i * x.shape[0]
    peak = jnp.maximum(m_ref[0:1, :], jnp.max(x, axis=0, keepdims=True))
    total = s_ref[0:1, :] * jnp.exp(m_ref[0:1, :] - peak) + jnp.sum(jnp.exp(x - peak), axis=0, keepdims=True)
    pick = p_ref[0:1, :] + jnp.sum(jnp.where(entry == ids_ref[...], x, 0.0), axis=0, keepdims=True)
    m_ref[0:1, :], s_ref[0:1, :], p_ref[0:1, :] = peak, total, pick

    @pl.when(i == pl.num_programs(0) - 1)
    def _():
        pay_ref[...] = jnp.zeros_like(pay_ref)
        pay_ref[pay_ref.shape[0] - 8 : pay_ref.shape[0] - 7, :] = own_ref[...]
        norm = peak + jnp.log(total)
        lane = lax.broadcasted_iota(jnp.int32, (1, 2 * length), 1)
        chip, core = place()
        for n in range(2 * half // (2 * length)):
            s = slice(n * 2 * length, (n + 1) * 2 * length)
            d, rest = divmod(2 * n * length, half)
            first = rest // length
            team, k = first // CHIPS, first % CHIPS
            rows = (
                jnp.where(lane < length, norm[:, s], pltpu.roll(pick[:, s], length, 1)),
                jnp.where(lane < length, pltpu.roll(norm[:, s], length, 1), pick[:, s]),
            )
            for j in range(2):
                q = team * TEAM + (chip ^ (k + j)) * CORES + (core ^ d)
                pay_ref[pl.ds(q, 1), :] = rows[j]


def logits(held, pair, ids, own_row, embedding, length, questions):
    half, vocab, width = held.shape[0], embedding.shape[0], embedding.shape[1]
    tile = min(2 * VOCAB_TILE, vocab)
    stat = pltpu.VMEM((8, 2 * half), F32)
    whole = pl.BlockSpec(memory_space=pltpu.VMEM)
    return pl.pallas_call(
        functools.partial(logits_kernel, length),
        grid=(vocab // tile,),
        in_specs=[whole, whole, whole, whole, pl.BlockSpec((tile, width), lambda i: (i, 0))],
        out_specs=[
            pl.BlockSpec((tile, 2 * half), lambda i: (i, 0)),
            pl.BlockSpec((questions + 8, 2 * length), lambda i: (0, 0)),
        ],
        out_shape=[
            pltpu.HBM((vocab, 2 * half), F32),
            jax.ShapeDtypeStruct((questions + 8, 2 * length), F32),
        ],
        scratch_shapes=[pltpu.VMEM((2 * half, width), BF), stat, stat, stat],
        compiler_params=limit(14 + 24 * half * tile // MIB),
        cost_estimate=work(10),
    )(held, pair, ids, own_row, embedding)


def merge_kernel(length, all_ref, counts_ref, ids_ref, rows_out, own_out, logp_out, prior_out, n_ref, g_ref):
    n_slot, n_pb = n_ref.shape[0], n_ref.shape[1]
    chip, core = place()
    me, slot = lax.axis_index("pb"), lax.axis_index("slot")
    lane = lax.broadcasted_iota(jnp.int32, (1, 2 * length), 1)
    logps, priors = [], None
    for s in range(n_slot):
        blocks = [all_ref[s * n_pb + j, :n_pb, :] for j in range(n_pb)]
        peak = blocks[0]
        for b in blocks[1:]:
            peak = jnp.maximum(peak, b)
        total = jnp.zeros_like(peak)
        pick = jnp.zeros_like(peak)
        for b in blocks:
            total = total + jnp.exp(b - peak)
            pick = pick + b
        norm = peak + jnp.log(total)
        n_ref[s] = norm
        own = jnp.concatenate([all_ref[s * n_pb + j, n_pb : n_pb + 1, :] for j in range(n_pb)], axis=0)
        mask = own
        prior = pltpu.roll(own, length, 1)
        logp = pltpu.roll(pick, length, 1) - norm + prior
        logps.append(jnp.where(counts_ref[...] > s, logp, -1e30))
    top = logps[0]
    for p in logps[1:]:
        top = jnp.maximum(top, p)
    total = jnp.zeros_like(top)
    for p in logps:
        total = total + jnp.exp(p - top)
    merged = top + jnp.log(total)
    for s in range(n_slot):
        g_ref[s] = jnp.where(counts_ref[...] > s, -mask * jnp.exp(logps[s] - merged), 0.0)
    n_rows = n_ref.shape[1]
    row = lax.broadcasted_iota(jnp.int32, merged.shape, 0)
    logp_out[...] = jnp.sum(jnp.where(row == me, merged, 0.0), axis=0, keepdims=True)
    own_grad = jnp.where(lane < length, g_ref[slot, pl.ds(me, 1), :], 0.0)
    prior_out[...] = jnp.sum(own_grad, axis=1, keepdims=True)
    rows_out[...] = jnp.zeros_like(rows_out)
    half = rows_out.shape[3]
    for s in range(n_slot):
        for d in range(CORES):
            for n in range(half // (2 * length)):
                team, c = (2 * n) // CHIPS, (2 * n) % CHIPS
                q = [team * TEAM + (chip ^ (c + j)) * CORES + (core ^ d) for j in range(2)]
                t = slice(n * 2 * length, (n + 1) * 2 * length)
                for r, (first, second) in enumerate(
                    (
                        (n_ref[s, pl.ds(q[0], 1), :], n_ref[s, pl.ds(q[1], 1), :]),
                        (g_ref[s, pl.ds(q[0], 1), :], g_ref[s, pl.ds(q[1], 1), :]),
                        (ids_ref[pl.ds(q[0], 1), :], ids_ref[pl.ds(q[1], 1), :]),
                    )
                ):
                    rows_out[s, d, r : r + 1, t] = jnp.where(lane < length, first, pltpu.roll(second, length, 1))
    own_out[0] = rows_out[slot]


def merge(everyone, counts, ids, length, n_slot, n_pb, half):
    held = pltpu.VMEM((n_slot, n_pb, 2 * length), F32)
    return pl.pallas_call(
        functools.partial(merge_kernel, length),
        out_shape=[
            jax.ShapeDtypeStruct((n_slot, CORES, 8, half), F32),
            jax.ShapeDtypeStruct((1, CORES, 8, half), F32),
            jax.ShapeDtypeStruct((1, 2 * length), F32),
            jax.ShapeDtypeStruct((1, 1), F32),
        ],
        scratch_shapes=[held, held],
        compiler_params=limit(16 + 2 * everyone.size * 4 // MIB),
        cost_estimate=work(2),
    )(everyone, counts, ids)


def logit_gradient(x, rows, first):
    entry = (lax.broadcasted_iota(jnp.int32, x.shape, 0) + first).astype(F32)
    hit = jnp.where(entry == rows[2:3, :], 1.0, 0.0)
    return (rows[1:2, :] * (hit - jnp.exp(x - rows[0:1, :]))).astype(BF)


def state_grad_kernel(l_ref, rows_ref, e_ref, own_ref, pair_ref, d_ref, acc_ref):
    i = pl.program_id(0)
    half = own_ref.shape[0]

    @pl.when(i == 0)
    def _():
        acc_ref[...] = jnp.zeros_like(acc_ref)

    tile = l_ref.shape[0]
    d = [logit_gradient(l_ref[:, c * half : (c + 1) * half], rows_ref[0, c], i * tile) for c in range(CORES)]
    d_ref[...] = jnp.concatenate(d, axis=1)
    acc_ref[...] += dot(d_ref[...], e_ref[...], TN)

    @pl.when(i == pl.num_programs(0) - 1)
    def _():
        own_ref[...] = acc_ref[:half, :].astype(own_ref.dtype)
        pair_ref[...] = acc_ref[half:, :].astype(BF)


def state_grad(scores, rows, embedding, own_type):
    vocab, count = scores.shape
    width = embedding.shape[1]
    half = count // CORES
    tile = min(2 * VOCAB_TILE, vocab)
    last = pl.BlockSpec((half, width), lambda i: (0, 0))
    return pl.pallas_call(
        state_grad_kernel,
        grid=(vocab // tile,),
        in_specs=[
            pl.BlockSpec((tile, count), lambda i: (i, 0)),
            pl.BlockSpec((1,) + rows.shape[1:], lambda i: (0, 0, 0, 0)),
            pl.BlockSpec((tile, width), lambda i: (i, 0)),
        ],
        out_specs=[last, last, pl.BlockSpec((tile, count), lambda i: (i, 0))],
        out_shape=[
            jax.ShapeDtypeStruct((half, width), own_type),
            jax.ShapeDtypeStruct((half, width), BF),
            pltpu.HBM((vocab, count), BF),
        ],
        scratch_shapes=[pltpu.VMEM((count, width), F32)],
        compiler_params=limit(16 + 20 * half * tile // MIB + count * width * 4 // MIB),
        cost_estimate=work(11),
    )(in_hbm(scores), rows, embedding)


def own_embedding_kernel(d_ref, own_ref, pair_ref, *refs):
    half = own_ref.shape[0]
    refs[-1][...] = dot(d_ref[:, :half], own_ref[...]) + dot(d_ref[:, half:], pair_ref[...])


def own_embedding(d, own, pair, held, piece, count):
    vocab, tokens = d.shape
    tile = min(VOCAB_TILE, vocab // count)
    steps = vocab // count // tile
    ahead = [] if held is None else [held]
    whole = pl.BlockSpec(memory_space=pltpu.VMEM)
    shape = (vocab, own.shape[1])
    return pl.pallas_call(
        own_embedding_kernel,
        grid=(steps,),
        in_specs=[pl.BlockSpec((tile, tokens), lambda i: (piece * steps + i, 0)), whole, whole]
        + [pl.BlockSpec(memory_space=pl.ANY)] * len(ahead),
        out_specs=pl.BlockSpec((tile, shape[1]), lambda i: (piece * steps + i, 0)),
        out_shape=pltpu.HBM(shape, F32),
        input_output_aliases={3: 0} if ahead else {},
        compiler_params=limit(14),
        cost_estimate=work(1),
    )(d, own, pair, *ahead)


def embedding_kernel(base, rows_ref, own_ref, pair_ref, e_ref, held_ref, o_ref):
    first = base + pl.program_id(0) * e_ref.shape[0]
    slot = lax.axis_index("slot")
    o_ref[...] = held_ref[...]

    def other(k, carry):
        n = slot ^ k
        for top in range(0, own_ref.shape[1], TOKENS // CORES):
            t = slice(top, top + TOKENS // CORES)
            h = jnp.concatenate([own_ref[n, t, :], pair_ref[n, t, :]], axis=0)
            rows = jnp.concatenate([rows_ref[n, 0, :, t], rows_ref[n, 1, :, t]], axis=1)
            o_ref[...] += dot(logit_gradient(dot(e_ref[...], h, NT), rows, first), h)
        return carry

    lax.fori_loop(1, own_ref.shape[0], other, 0)


def embedding_piece(rows, states, embedding, held, first, size):
    width = embedding.shape[1]
    tile = min(VOCAB_TILE, size)
    steps = size // tile
    whole = pl.BlockSpec(memory_space=pltpu.VMEM)
    block = pl.BlockSpec((tile, width), lambda i: (first // tile + i, 0))
    return pl.pallas_call(
        functools.partial(embedding_kernel, first),
        grid=(steps,),
        in_specs=[whole, whole, whole, block, block],
        out_specs=block,
        out_shape=pltpu.HBM(embedding.shape, F32),
        input_output_aliases={4: 0},
        compiler_params=limit(24),
        cost_estimate=work(3 * size / 1024),
    )(rows, *states, embedding, held)


def add_kernel(mine, got, own_out, *send):
    length = own_out.shape[0]
    for k in range(CHIPS):
        s = slice(k * length, (k + 1) * length)
        y = mine[s, :] + got[s, :].astype(F32)
        if k == 0:
            own_out[...] = y
        else:
            send[k - 1][...] = y.astype(BF)


def norm_back_kernel(row, has_base, *refs):
    base = refs[0] if has_base else None
    mine, r1, r2, r3, z, inv, vec, dr_out, e_out, sums_out = refs[1 if has_base else 0 :]
    dh = mine[...] + r1[...].astype(F32) + r2[...].astype(F32) + r3[...].astype(F32)
    if has_base:
        dh = dh + base[...]
    dr = norm_back(dh, z[...], inv[...], vec[6 + row : 7 + row, :])
    e = dr.astype(BF)
    dr_out[...] = dr
    e_out[...] = e
    sums_out[...] = jnp.zeros_like(sums_out)
    sums_out[0:1, :] = jnp.sum(dh * z[...], axis=0, keepdims=True)
    sums_out[1:2, :] = jnp.sum(dh, axis=0, keepdims=True)
    sums_out[2:3, :] = jnp.sum(e.astype(F32), axis=0, keepdims=True)


def stack_rows(parts):
    return jnp.concatenate([p[...] for p in parts], axis=0)


def split_rows(y, mine_out, send):
    length = mine_out.shape[0]
    mine_out[...] = y[:length]
    for k in range(1, CHIPS):
        send[k - 1][...] = y[k * length : (k + 1) * length].astype(BF)


def column_sum(y):
    return jnp.sum(y.astype(F32), axis=0, keepdims=True)


def ffn_back_kernel(*refs):
    parts, (u_ref, up, down), (e_out, du_out, sum_out, mine_out), send = refs[:4], refs[4:7], refs[7:11], refs[11:]
    e = stack_rows(parts)
    e_out[...] = e
    da = dot(e, down[...], NT).astype(BF).astype(F32)
    u = u_ref[...]
    slope = gelu_parts(u) + u * (jnp.exp(-0.5 * u * u) * 0.3989422804014327)
    du = (da * slope).astype(BF)
    du_out[...] = du
    sum_out[...] = column_sum(du)
    split_rows(dot(du, up[...], NT), mine_out, send)


def pick_core(g, mine_out, other_out, top):
    _, core = place()
    lo, hi = g[:, :, 0], g[:, :, 1]
    n = lo.shape[1] * lo.shape[2]
    mine = jnp.where(core == 0, lo, hi).reshape(CHIPS, n, g.shape[-1])
    other = jnp.where(core == 0, hi, lo).reshape(CHIPS, n, g.shape[-1])
    mine_out[:, top : top + n, :] = mine.astype(BF)
    other_out[:, top : top + n, :] = other.astype(BF)


def place_columns(g, mine_out, other_out, top):
    unit = g.shape[0] // (CHIPS * CHIPS * CORES)
    pick_core(g.reshape(CHIPS, CHIPS, CORES, unit, g.shape[1]), mine_out, other_out, top)


def place_rows(g, mine_out, other_out, top):
    unit = g.shape[0] // (CHIPS * CORES)
    pick_core(g.reshape(CHIPS, 1, CORES, unit, g.shape[1]), mine_out, other_out, top)


def place_row_blocks(g, mine_out, other_out, top, lanes):
    unit = g.shape[0] // (CHIPS * CORES)
    for b in range(g.shape[1] // lanes):
        place_rows(g[:, b * lanes : (b + 1) * lanes], mine_out, other_out, top + b * unit)


def ffn_grads_kernel(low, du, a, e, mine_out, other_out):
    g = dot(low[...], du[...], TN)
    place_columns(g, mine_out, other_out, 0)
    g2 = dot(a[...], e[...], TN)
    place_rows(g2, mine_out, other_out, g.shape[0] // (CHIPS * CORES))


def cross_back_kernel(*refs):
    parts, (w_mine, w_cols, q_ref, k_ref, v_ref) = refs[:4], refs[4:9]
    (e_out, dq_out, dk_out, dv_out, mine_out), send, g_ref = refs[9:14], refs[14:-1], refs[-1]
    quarter = q_ref.shape[1]
    length, memory = q_ref.shape[0] // CHIPS, k_ref.shape[0] // CHIPS
    e = stack_rows(parts)
    e_out[...] = e
    g = dot(e, w_mine[1], NT).astype(BF)
    g_ref[...] = g

    def pair(i, carry):
        for j in range(2):
            s, t = rows_at((2 * i + j) * length, length, 16), rows_at((2 * i + j) * memory, memory, 16)
            dq_out[s, :], dk_out[t, :], dv_out[t, :] = attend_back(
                g_ref[s, :], q_ref[s, :], k_ref[t, :], v_ref[t, :], False
            )
        return carry

    lax.fori_loop(0, CHIPS // 2, pair, 0)
    split_rows(dot(dq_out[...], w_cols[:, :quarter], NT), mine_out, send)


def cross_grads_kernel(low, dq, m, dk, dv, o, e, mine_out, other_out, sums_out):
    n = low.shape[1] // (CHIPS * CORES)
    for j, (a, g) in enumerate(((low, dq), (m, dk), (m, dv))):
        place_columns(dot(a[...], g[...], TN), mine_out, other_out, j * n)
    place_row_blocks(dot(o[...], e[...], TN), mine_out, other_out, 3 * n, dq.shape[1])
    sums_out[...] = jnp.zeros_like(sums_out)
    sums_out[0:1, :] = column_sum(dq[...])
    sums_out[1:2, :] = column_sum(dv[...])


def self_back_kernel(*refs):
    parts, (w_mine, q_ref, k_ref, v_ref), (e_out, d_out, g_ref) = refs[:4], refs[4:8], refs[8:]
    quarter = q_ref.shape[1]
    length = q_ref.shape[0] // CHIPS
    e = stack_rows(parts)
    e_out[...] = e
    g = dot(e, w_mine[0], NT).astype(BF)
    g_ref[...] = g

    def pair(i, carry):
        for j in range(2):
            s = rows_at((2 * i + j) * length, length, 16)
            dq, dk, dv = attend_back(g_ref[s, :], q_ref[s, :], k_ref[s, :], v_ref[s, :], True)
            d_out[s, :quarter] = dq
            d_out[s, quarter : 2 * quarter] = dk
            d_out[s, 2 * quarter :] = dv
        return carry

    lax.fori_loop(0, CHIPS // 2, pair, 0)


SMALL = 16


def self_grads_kernel(x, d, o, e, c_sums, sum_in, one, two, three, mine_out, other_out):
    chip, core = place()
    quarter = d.shape[1] // 3
    n = x.shape[1] // (CHIPS * CORES)
    g = dot(x[...], d[...], TN)
    for j in range(3):
        place_columns(g[:, j * quarter : (j + 1) * quarter], mine_out, other_out, j * n)
    place_row_blocks(dot(o[...], e[...], TN), mine_out, other_out, 3 * n, quarter)

    def spread(row):
        zero = jnp.zeros_like(row)
        return jnp.concatenate([jnp.where(chip == b, row, zero) for b in range(CHIPS)], axis=1)

    rows = [
        spread(column_sum(d[:, :quarter])), spread(column_sum(d[:, 2 * quarter :])), one[2:3, :],
        spread(c_sums[0:1, :]), spread(c_sums[1:2, :]), two[2:3, :], one[0:1, :], two[0:1, :], three[0:1, :],
        one[1:2, :], two[1:2, :], three[1:2, :], three[2:3, :],
    ]
    v = jnp.concatenate(rows + [jnp.zeros((SMALL - len(rows), x.shape[1]), F32)], axis=0)
    unit = x.shape[1] // (CHIPS * CHIPS * CORES)
    wide = sum_in.shape[1] // (CHIPS * CORES)
    last = sum_in[...]
    top = 4 * n
    for out in (mine_out, other_out):
        out[:, top:, :] = jnp.zeros((CHIPS, 2 * SMALL, quarter), BF)
    for s in range(CHIPS):
        halves, ends = [], []
        for c in range(CORES):
            parts = [v[:, ((s * CHIPS + b) * CORES + c) * unit :][:, :unit] for b in range(CHIPS)]
            halves.append(jnp.concatenate(parts, axis=1))
            ends.append(last[:, (s * CORES + c) * wide :][:, :wide])
        for out, swap in ((mine_out, False), (other_out, True)):
            first = (core == 0) != swap
            out[s, top : top + SMALL, : CHIPS * unit] = jnp.where(first, halves[0], halves[1]).astype(BF)
            out[s, top + SMALL : top + SMALL + 1, :wide] = jnp.where(first, ends[0], ends[1]).astype(BF)


def input_back_kernel(d, w_self, dk, dv, w_cross, mine_out, *send):
    quarter = dk.shape[1]
    length, memory = d.shape[0] // CHIPS, dk.shape[0] // CHIPS
    y = dot(d[...], w_self[...], NT)
    m = dot(dk[...], w_cross[:, quarter : 2 * quarter], NT) + dot(dv[...], w_cross[:, 2 * quarter :], NT)
    for k, out in enumerate((mine_out, *send)):
        out[:length, :] = y[k * length : (k + 1) * length].astype(out.dtype)
        out[length:, :] = m[k * memory : (k + 1) * memory].astype(out.dtype)


def input_total_kernel(base, mine, r1, r2, r3, source_out, memory_out):
    length = base.shape[0]
    y = mine[...] + r1[...].astype(F32) + r2[...].astype(F32) + r3[...].astype(F32)
    source_out[...] = base[...] + y[:length]
    memory_out[...] = y[length:]


def core_sum_kernel(mine, got, out):
    for n in range(SLOTS):
        out[n] = (mine[n].astype(F32) + got[n].astype(F32)).astype(BF)


def column_pieces_kernel(count, got, *outs):
    *pieces, rest = outs
    chip, _ = place()
    unit = pieces[0].shape[0] // count
    y = sum(got[n].astype(F32) for n in range(SLOTS))
    top = count * CHIPS * unit
    rest[...] = y[top:].astype(BF)
    hold = y[:top].astype(BF).reshape(count, CHIPS, unit, y.shape[1])
    for k in range(CHIPS):
        for j in range(count):
            block = jnp.zeros((unit, y.shape[1]), BF)
            for b in range(CHIPS):
                block = jnp.where((chip ^ k) == b, hold[j, b], block)
            pieces[k][j * unit : (j + 1) * unit, :] = block


def attn_pieces_kernel(s_got, c_got, *outs):
    *pieces, rest = outs
    chip, _ = place()
    s = sum(s_got[n].astype(F32) for n in range(SLOTS)).astype(BF)
    c = sum(c_got[n].astype(F32) for n in range(SLOTS)).astype(BF)
    top = 3 * c.shape[0] // 4
    unit = top // (3 * CHIPS)
    both = [y[:top].reshape(3, CHIPS, unit, y.shape[1]) for y in (s, c)]
    for k in range(CHIPS):
        for m, y in enumerate(both):
            for j in range(3):
                block = jnp.zeros((unit, y.shape[3]), BF)
                for b in range(CHIPS):
                    block = jnp.where((chip ^ k) == b, y[j, b], block)
                pieces[k][(3 * m + j) * unit : (3 * m + j + 1) * unit, :] = block
        pieces[k][6 * unit :, :] = s[c.shape[0] : c.shape[0] + SMALL]
    n = c.shape[0] - top
    rest[:n, :] = s[top : top + n]
    rest[n : 2 * n, :] = c[top:]
    rest[2 * n :, :] = s[c.shape[0] + SMALL :]


def attn_out_kernel(p0, p1, p2, p3, out, bias_out, gain_out, shift_out, last_out):
    chip, _ = place()
    unit, quarter = out.shape[1], p0.shape[1]
    parts = (p0, p1, p2, p3)
    for k, p in enumerate(parts):
        lanes = rows_at((chip ^ k) * quarter, quarter, 128)
        for j in range(6):
            out[j, :, lanes] = p[j * unit : (j + 1) * unit, :].astype(F32)
    total = sum(p[6 * unit :, : CHIPS * unit].astype(F32) for p in parts)
    mine = jnp.zeros((SMALL, unit), F32)
    for b in range(CHIPS):
        mine = jnp.where(chip == b, total[:, b * unit : (b + 1) * unit], mine)
    columns = jnp.transpose(jnp.concatenate([mine, jnp.zeros((SMALL, 128 - unit), F32)], axis=1))
    bias_out[...] = columns[:unit, 0:6]
    gain_out[...] = columns[:unit, 6:9]
    shift_out[...] = columns[:unit, 9:12]
    last_out[...] = mine[12:13, :]


def rows_out_kernel(owned, f_owned, out, down_out, in_out):
    unit, quarter = out.shape[1], owned.shape[1]
    n = CHIPS * unit
    for m in range(2):
        for b in range(CHIPS):
            out[m, :, b * quarter : (b + 1) * quarter] = owned[m * n + b * unit : m * n + (b + 1) * unit, :].astype(F32)
    down_out[...] = f_owned[...].astype(F32)
    in_out[...] = owned[2 * n : 2 * n + 1, : in_out.shape[1]].astype(F32)


def up_out_kernel(p0, p1, p2, p3, out):
    chip, _ = place()
    quarter = p0.shape[1]
    for k, p in enumerate((p0, p1, p2, p3)):
        out[:, rows_at((chip ^ k) * quarter, quarter, 128)] = p[...].astype(F32)


def shards(
    inputs, memory, attn_weight, attn_out, ffn_in, ffn_out, attn_bias, norm_gain, norm_bias,
    bias_in, bias_out, embedding, targets, slot_counts, pad_mask, log_prior,
):
    n_pb, n_slot = lax.axis_size("pb"), lax.axis_size("slot")
    n_all = n_pb * n_slot
    teams = n_pb // TEAM
    me = lax.axis_index("pb")
    length, width = inputs.shape[2], inputs.shape[3]
    passage = memory.shape[2]
    quarter = width // CHIPS
    unit = width // (TEAM * n_slot)
    vocab_rows = embedding.shape[0]
    embedding = in_hbm(embedding)

    def team_rows(w):
        if teams == 1:
            return w
        w = lax.all_gather(w, "pb", axis=0, tiled=True)
        n = w.shape[0] // TEAM
        return lax.dynamic_slice_in_dim(w, (me % TEAM) * n, n)

    x, m = inputs[0, 0], memory[0, 0]
    attn_w = jnp.moveaxis(team_rows(attn_weight), 1, 0)
    out_w = jnp.moveaxis(team_rows(attn_out), 1, 0)
    up_w = team_rows(ffn_in)
    down_w = team_rows(ffn_out)
    rows = attn_w.shape[1]
    ff = up_w.shape[1] // CHIPS
    vec = jnp.concatenate(
        [attn_bias.T, norm_gain.T, norm_bias.T, bias_out[None], bias_in.reshape(CHIPS, -1)], axis=0
    )
    ids = (targets - me * vocab_rows).astype(jnp.int32)
    own_row = jnp.concatenate([pad_mask.astype(F32), jnp.broadcast_to(log_prior, (1, length))], axis=1)

    block = (length, width)
    every = (CHIPS * length, width)
    cols = (CHIPS * length, quarter)
    m_cols = (CHIPS * passage, quarter)
    sends = [(block, BF)] * 3

    def give(send):
        return [from_chip(send[k - 1], k) for k in range(1, CHIPS)]

    def give_far(send):
        return [in_hbm(r) for r in give(send)]

    far_call = functools.partial(call, far=True)

    first = call(functools.partial(pack_kernel, 6, 0), [((CHIPS * length + 6 * rows, quarter), BF)] * CHIPS, x, attn_w)
    got_first = [first[0]] + give(first[1:])
    got_first[1], vec = tie(got_first[1], vec)
    pair_first = [from_core(g) for g in got_first]
    out_pair = from_core(out_w)
    down_pair = from_core(down_w)
    third = list(call(functools.partial(pack_kernel, 1, 0), [((rows, ff), BF)] * CHIPS, up_w[None]))
    m_send, pair_first[3] = tie(m, pair_first[3])
    got_memory = [m, from_chip(m_send, 1), from_chip(m_send, 2)]

    x_all, w_self, queries, keys, values, mixed, w_out, mine, *send = call(
        self_kernel,
        [(every, BF), ((width, 3 * quarter), BF)] + [(cols, BF)] * 4 + [((2, quarter, width), BF), (block, F32)]
        + sends,
        *got_first, *pair_first, out_w, out_pair, vec,
    )
    got = give(send)
    got_memory[1], got_memory[2], *got = tie(got_memory[1], got_memory[2], *got)
    norm_outs = [(block, F32), (block, BF), (block, F32), ((length, 1), F32)]
    hidden_one, low_one, z_one, inv_one = call(
        functools.partial(norm_kernel, (2, 6, 9)), norm_outs, x, mine, *got, vec, us=1
    )
    got_low = [low_one] + others(low_one)
    m_send, got_memory[1] = tie(m, got_memory[1])
    got_memory.append(from_chip(m_send, 3))
    m_all, w_cross, cross_keys, cross_values = call(
        memory_kernel, [((CHIPS * passage, width), BF), ((width, 3 * quarter), BF)] + [(m_cols, BF)] * 2,
        *got_memory, *got_first, *pair_first, vec,
    )
    third[1], third[2], *got_low = tie(third[1], third[2], *got_low)
    got_third = [third[0], from_chip(third[1], 1), from_chip(third[2], 2)]
    low_one_all, cross_queries, cross_mixed, mine, *send = call(
        cross_kernel, [(every, BF), (cols, BF), (cols, BF), (block, F32)] + sends,
        *got_low, w_out, w_cross, cross_keys, cross_values, vec,
    )
    got = give(send)
    got_third[1], got_third[2], *got = tie(got_third[1], got_third[2], *got)
    hidden_two, low_two, z_two, inv_two = call(
        functools.partial(norm_kernel, (5, 7, 10)), norm_outs, hidden_one, mine, *got, vec, us=1
    )
    got_low = [low_two] + others(low_two)
    third[3], got_third[1] = tie(third[3], got_third[1])
    got_third.append(from_chip(third[3], 3))
    (up_half,) = call(up_half_kernel, [((CHIPS, rows, ff), BF)], *got_third)
    up_half_pair = from_core(up_half)
    low_two_all, upward, active, w_up, w_down, mine, *send = call(
        ffn_kernel,
        [(every, BF), ((CHIPS * length, ff), F32), ((CHIPS * length, ff), BF), ((width, ff), BF)]
        + [((ff, width), BF), (block, F32)]
        + sends,
        *got_low, up_half, up_half_pair, down_w, down_pair, vec,
    )
    got = give(send)
    _, final_low, z_three, inv_three = call(
        functools.partial(norm_kernel, (12, 8, 11)), norm_outs, hidden_two, mine, *got, vec, us=1
    )

    held, spread_held = call(
        stack_kernel, [(every, BF), ((n_slot,) + every, BF)], final_low, *others(final_low), us=1
    )
    pair = from_core(held)

    def all_teams(h):
        return lax.all_gather(h, "pb", axis_index_groups=same_place_groups(), axis=0, tiled=True) if teams > 1 else h

    half = teams * CHIPS * length
    chip, core = place()
    order = [
        t * TEAM + (chip ^ k) * CORES + (core ^ d) for d in range(CORES) for t in range(teams) for k in range(CHIPS)
    ]
    ids_row = jnp.concatenate([lax.dynamic_slice_in_dim(ids, q, 1) for q in order], axis=1)
    states = [all_teams(held), all_teams(pair)]
    scores, payload = logits(*states, ids_row, own_row, embedding, length, n_pb)
    everyone = lax.all_to_all(
        jnp.broadcast_to(payload[None], (n_all,) + payload.shape), ("slot", "pb"), 0, 0, tiled=True
    )
    ids_wide = jnp.pad(ids.astype(F32), ((0, 0), (0, length)))
    spread_held, everyone = tie(spread_held, everyone)
    all_held = across_slots(spread_held)
    token_rows, own_rows, token_logprob, prior_grad = merge(
        everyone, slot_counts.astype(jnp.int32)[:, None], ids_wide, length, n_slot, n_pb, half
    )
    def home(partial):
        if teams == 1:
            return partial
        return lax.psum_scatter(partial, "pb", axis_index_groups=same_place_groups(), scatter_dimension=0, tiled=True)

    own_part, for_pair, own_logits = state_grad(scores, own_rows, embedding, F32)
    own_logits = in_hbm(own_logits)
    own_part, got_pair = home(own_part), from_core(home(for_pair))
    mine, *send = call(add_kernel, [(block, F32)] + sends, own_part, got_pair, us=1)
    got = give(send)
    own_logits, send[0] = tie(own_logits, send[0])
    own_terms = own_embedding(own_logits, *states, None, 0, 2)
    own_terms, *got = tie(own_terms, *got)

    eighth = vocab_rows // 8
    parts = (1, 1, 1, 5)
    made = []

    def piece(*wait):
        n = len(made) - 1
        rows_in, *wait = tie(token_rows, *wait)
        first = sum(parts[:n]) * eighth
        made.append(embedding_piece(rows_in, states, embedding, made[-1], first, parts[n] * eighth))
        return wait

    def pieces(count, *wait):
        for _ in range(count):
            wait = piece(*wait)
        return list(wait)

    def then(*values):
        *values, made[-1] = tie(*values, made[-1])
        return values

    def settle(g):
        if teams == 1:
            return g
        g = lax.psum(g, "pb", axis_index_groups=same_place_groups())
        g = lax.all_gather(g, "pb", axis_index_groups=team_groups(), axis=0, tiled=True)
        n = g.shape[0] // n_pb
        return lax.dynamic_slice_in_dim(g, me * n, n)

    def to_owner(g):
        pairs = []
        for s in range(n_slot):
            for i in range(n_pb):
                t, b, c = i // TEAM, (i % TEAM) // CORES, i % CORES
                pairs.append((s * n_pb + i, b * n_pb + t * TEAM + s * CORES + c))
        return lax.ppermute(g, ("slot", "pb"), pairs)

    def column_pieces(count, got, n, cols):
        rest = got.shape[1] - count * CHIPS * n
        *piece, rest = call(
            functools.partial(column_pieces_kernel, count),
            [((count * n, cols), BF)] * CHIPS + [((rest, cols), BF)], got,
        )
        return [piece[0]] + give_far(piece[1:]), rest

    x_all, w_self, queries, keys, values, mixed, w_out, m_all, w_cross, cross_keys, cross_values = (
        in_hbm(v)
        for v in (x_all, w_self, queries, keys, values, mixed, w_out, m_all, w_cross, cross_keys, cross_values)
    )
    low_one_all, cross_queries, cross_mixed, low_two_all, upward, active, w_up, w_down = (
        in_hbm(v) for v in (low_one_all, cross_queries, cross_mixed, low_two_all, upward, active, w_up, w_down)
    )
    z_one, z_two, z_three = in_hbm(z_one), in_hbm(z_two), in_hbm(z_three)
    grads = [(block, F32), (block, BF), ((8, width), F32)]
    dr_three, e_three, sums_three = call(
        functools.partial(norm_back_kernel, 2, False), grads, mine, *got, z_three, inv_three, vec, us=1
    )
    got_e = others(e_three)
    own_logits, e_three = tie(own_logits, e_three)
    own_terms = own_embedding(own_logits, *states, own_terms, 1, 2)
    own_terms, *got_e = tie(own_terms, *got_e)
    made.append(own_terms)
    e_all, du, sum_in, mine, *send = call(
        ffn_back_kernel,
        [(every, BF), ((CHIPS * length, ff), BF), ((1, ff), F32), (block, F32)] + sends,
        e_three, *got_e, upward, w_up, w_down,
    )
    got = give_far(send)
    f_shape = (n_slot, CHIPS * unit + ff // TEAM, width)
    du, send[0] = tie(du, send[0])
    f_mine, f_other = call(ffn_grads_kernel, [(f_shape, BF)] * 2, low_two_all, du, active, e_all, us=3)
    f_other, all_held, *got = tie(f_other, all_held, *got)
    all_pair = from_core(all_held)
    dr_two, e_two, sums_two = far_call(
        functools.partial(norm_back_kernel, 1, True), grads, dr_three, mine, *got, z_two, inv_two, vec, us=1
    )
    got_e = give_far([e_two] * 3)
    f_got = from_core(f_other)
    f_got, all_pair, e_two = tie(f_got, all_pair, e_two)
    states = [jnp.stack([all_teams(h[n]) for n in range(n_slot)]) if teams > 1 else h for h in (all_held, all_pair)]
    (f_total,) = far_call(core_sum_kernel, [(f_shape, BF)], f_mine, f_got)
    f_got = across_slots(f_total)
    e_all_two, dqc, dkc, dvc, mine, *send = far_call(
        cross_back_kernel,
        [(every, BF), (cols, BF), (m_cols, BF), (m_cols, BF), (block, F32)] + sends,
        e_two, *got_e, w_out, w_cross, cross_queries, cross_keys, cross_values, us=5,
        scratch=[pltpu.VMEM(cols, BF)],
    )
    got = give_far(send)
    dqc, send[0] = tie(dqc, send[0])
    g_shape = (n_slot, 4 * CHIPS * unit, quarter)
    c_mine, c_other, c_sums = call(
        cross_grads_kernel, [(g_shape, BF)] * 2 + [((8, quarter), F32)],
        low_one_all, dqc, m_all, dkc, dvc, cross_mixed, e_all_two,
    )
    c_got = from_core(c_other)
    (c_mine,) = piece(c_mine)
    got = then(*got)
    dr_one, e_one, sums_one = far_call(
        functools.partial(norm_back_kernel, 0, True), grads, dr_two, mine, *got, z_one, inv_one, vec, us=1
    )
    got_e = give_far([e_one] * 3)
    c_got, e_one = tie(c_got, e_one)
    (c_total,) = far_call(core_sum_kernel, [(g_shape, BF)], c_mine, c_got)
    (c_total,) = piece(c_total)
    f_got, *got_e = then(f_got, *got_e)
    e_all_one, d_self = far_call(
        self_back_kernel, [(every, BF), ((CHIPS * length, 3 * quarter), BF)], e_one, *got_e, w_out, queries, keys, values, us=4,
        scratch=[pltpu.VMEM(cols, BF)],
    )
    c_total, d_self = tie(c_total, d_self)
    c_got = across_slots(c_total)
    s_shape = (n_slot, g_shape[1] + 2 * SMALL, quarter)
    s_mine, s_other = far_call(
        self_grads_kernel, [(s_shape, BF)] * 2, x_all, d_self, mixed, e_all_one, c_sums, sum_in, sums_one, sums_two, sums_three
    )
    s_got = from_core(s_other)
    f_got, s_mine = tie(f_got, s_mine)
    f_pieces, f_rest = column_pieces(1, f_got, unit, width)
    f_owned = to_owner(f_rest)
    d_self, f_rest = tie(d_self, f_rest)
    both = (length + passage, width)
    mine, *send = far_call(input_back_kernel, [(both, F32)] + [(both, BF)] * 3, d_self, w_self, dkc, dvc, w_cross, us=3)
    s_got, send[0] = tie(s_got, send[0])
    (s_total,) = far_call(core_sum_kernel, [(s_shape, BF)], s_mine, s_got)
    (s_total,) = pieces(1, s_total)
    c_got, *f_pieces = then(c_got, *f_pieces)
    s_total, send[0], c_got = tie(s_total, send[0], c_got)
    s_got = across_slots(s_total)
    got = give_far(send)
    (out_up,) = call(up_out_kernel, [((unit, up_w.shape[1]), F32)], *f_pieces, us=1)
    (out_up,) = pieces(len(parts) + 1 - len(made), out_up)
    s_got, *got = then(s_got, *got)
    *piece_parts, rest = call(
        attn_pieces_kernel,
        [((6 * unit + SMALL, quarter), BF)] * CHIPS + [((2 * CHIPS * unit + SMALL, quarter), BF)],
        s_got, c_got,
    )
    last = give(piece_parts[1:])
    owned = to_owner(rest)
    grad_source, grad_passage = call(
        input_total_kernel, [(block, F32), ((passage, width), F32)], dr_one, mine, *got, us=1
    )
    owned, grad_source, *last = tie(owned, grad_source, *last)
    out_attn, *vectors = call(
        attn_out_kernel,
        [((6, unit, width), F32), ((unit, 6), F32), ((unit, 3), F32), ((unit, 3), F32), ((1, unit), F32)],
        piece_parts[0], *last, us=1,
    )
    outs, out_down, sum_in_out = call(
        rows_out_kernel, [((2, unit, width), F32), (f_rest.shape, F32), ((1, ff // TEAM), F32)], owned, f_owned, us=1
    )
    out_attn = settle(jnp.moveaxis(out_attn, 0, 1))
    out_outputs = settle(jnp.moveaxis(outs, 0, 1))
    out_up, out_down = settle(out_up), settle(out_down)
    vectors = [settle(v) for v in (*vectors[:3], sum_in_out[0], vectors[3][0])]
    return (
        token_logprob[:, :length],
        grad_source[None, None],
        grad_passage[None, None],
        prior_grad,
        out_attn,
        out_outputs,
        out_up,
        out_down,
        vectors[0],
        vectors[1],
        vectors[2],
        vectors[3],
        vectors[4],
        made[-1],
    )


def solution(mesh):
    placed = (
        P("pb", "slot", None, None),
        P("pb", "slot", None, None),
        P("pb", None, None),
        P("pb", None, None),
        P("pb", None),
        P("pb", None),
        P(),
        P(),
        P(),
        P(),
        P(),
        P("pb", None),
        P(),
        P(),
        P("pb", None),
        P("pb", "slot"),
    )
    both = ("slot", "pb")
    return jax.shard_map(
        shards,
        mesh=mesh,
        in_specs=placed,
        out_specs=(
            P("pb", None),
            P("pb", "slot", None, None),
            P("pb", "slot", None, None),
            P("pb", "slot"),
            P(both, None, None),
            P(both, None, None),
            P(both, None),
            P(both, None),
            P(both, None),
            P(both, None),
            P(both, None),
            P(both),
            P(both),
            P("pb", None),
        ),
        check_vma=False,
    )
```

profile of v0, /device:TPU:2, one launch (start us, length us, event | category | flops | bytes accessed | tf_op | source)
XLA Modules:
  0.0 361.9 jit_solution(582075496533892904)
XLA Ops:
  8.5 11.8 %collective-permute-done.2.refs_3_.refs_7_ = bf16[1024,256]{1,0:T(8,128)(2,1)S(1)} collective-permute-done((bf16[1024,256]{1,0:T(8,128)(2,1)}, bf16[1024,256]{1,0:T(8,128)(2,1)S(1)}, u32[]{:S(2)}, u32[]{:S(2)}) %collective-permute-start.2) | collective-permute-done | bytes 524320 | tf_op jit(solution)/shard_map/ppermute | solution.py:26
  22.0 8.4 %collective-permute-done.refs_1_.refs_5_ = bf16[1024,256]{1,0:T(8,128)(2,1)S(1)} collective-permute-done((bf16[1024,256]{1,0:T(8,128)(2,1)}, bf16[1024,256]{1,0:T(8,128)(2,1)S(1)}, u32[]{:S(2)}, u32[]{:S(2)}) %collective-permute-start) | collective-permute-done | bytes 524320 | tf_op jit(solution)/shard_map/ppermute | solution.py:26
  33.1 4.1 %shard_map.264 = (bf16[256,1024]{1,0:T(8,128)(2,1)S(1)}, bf16[1024,768]{1,0:T(8,128)(2,1)S(1)}, bf16[256,256]{1,0:T(8,128)(2,1)S(1)}, bf16[256,256]{1,0:T(8,128)...) custom-call(bf16[1024,256]{1,0:T(8,128)(2,1)S(1)} %get-tuple-element, ...), custom_call_target="tpu_custom_call" | custom-call | flops 2000000000 | tf_op jit(solution)/shard_map/pallas_call | solution.py:97
  53.5 6.3 %collective-permute-done.15.refs_3_ = bf16[64,1024]{1,0:T(8,128)(2,1)S(1)} collective-permute-done((bf16[64,1024]{1,0:T(8,128)(2,1)S(1)}, bf16[64,1024]{1,0:T(8,128)(2,1)S(1)}, u32[]{:S(2)}, u32[]{:S(2)}) %collective-permute-start.15) | collective-permute-done | bytes 131104 | tf_op jit(solution)/shard_map/ppermute | solution.py:26
  79.4 6.1 %collective-permute-done.25.refs_3_ = bf16[128,1024]{1,0:T(8,128)(2,1)S(1)} collective-permute-done((bf16[128,1024]{1,0:T(8,128)(2,1)S(1)}, bf16[128,1024]{1,0:T(8,128)(2,1)S(1)}, u32[]{:S(2)}, u32[]{:S(2)}) %collective-permute-start.25) | collective-permute-done | bytes 262176 | tf_op jit(solution)/shard_map/ppermute | solution.py:26
  121.3 10.7 %shard_map.274 = (f32[4096,512]{1,0:T(8,128)}, f32[16,128]{1,0:T(8,128)S(1)}) custom-call(bf16[256,1024]{1,0:T(8,128)(2,1)S(1)} %get-tuple-element.282.h0_ref.own_ref, bf16[256,1024]{1,0:T(8,128)(2,1)S(1)} %collective-permute-done.34.h1_ref.pair_ref, s32[1,512]{1,0:T(1,128)S(1)} %concatenate.10.ids_ref, f32[1,128]{1,0:T(1,128)S(1)} %concatenate.11.own_ref, ...), custom_call_target="tpu_custom_call" | custom-call | flops 10000000000 | tf_op jit(solution)/shard_map/pallas_call | solution.py:386
  132.0 14.8 %all_to_all.25.all_ref = f32[32,16,128]{2,1,0:T(8,128)S(1)} all-to-all(f32[32,16,128]{2,1,0:T(8,128)S(1)} %broadcast_in_dim.29), channel_id=1, replica_groups=mesh['slot'=4,'pb'=8] {'slot','pb'}, dimensions={0} | all-to-all | bytes 524288 | tf_op jit(solution)/shard_map/all_to_all | solution.py:986
  146.9 3.9 %all-to-all-start.1 = ((bf16[4,256,1024]{2,1,0:T(8,128)(2,1)}), bf16[4,256,1024]{2,1,0:T(8,128)(2,1)S(1)}, u32[]{:S(2)}, u32[]{:S(2)}) async-start(bf16[4,256,1024]{2,1,0:T(8,128)(2,1)} %copy-done.4), calls=%async_computation.1 | async-start | bytes 4194304 | tf_op jit(solution)/shard_map/all_to_all | solution.py:56
  151.7 11.0 %shard_map.276 = (f32[256,1024]{1,0:T(8,128)S(1)}, bf16[256,1024]{1,0:T(8,128)(2,1)S(1)}, bf16[4096,512]{1,0:T(8,128)(2,1)}) custom-call(f32[4096,512]{1,0:T(8,128)} %get-tuple-element.288.l_ref, f32[1,2,8,256]{3,2,1,0:T(8,128)S(1)} %get-tuple-element.289.rows_ref, bf16[4096,1024]{1,0:T(8,128)(2,1)} %e_ref.11), custom_call_target="tpu_custom_call" | custom-call | flops 11000000512 | tf_op jit(solution)/shard_map/pallas_call | solution.py:507
  168.4 6.5 %shard_map.278.refs_0_ = f32[4096,1024]{1,0:T(8,128)} custom-call(bf16[4096,512]{1,0:T(8,128)(2,1)} %get-tuple-element.305.d_ref, bf16[256,1024]{1,0:T(8,128)(2,1)S(1)} %get-tuple-element.282.h0_ref.own_ref, bf16[256,1024]{1,0:T(8,128)(2,1)S(1)} %collective-permute-done.34.h1_ref.pair_ref), custom_call_target="tpu_custom_call" | custom-call | flops 1000000000 | tf_op jit(solution)/shard_map/pallas_call | solution.py:539
  179.8 6.5 %shard_map.280.held_ref = f32[4096,1024]{1,0:T(8,128)} custom-call(bf16[4096,512]{1,0:T(8,128)(2,1)} %get-tuple-element.305.d_ref, bf16[256,1024]{1,0:T(8,128)(2,1)S(1)} %get-tuple-element.282.h0_ref.own_ref, bf16[256,1024]{1,0:T(8,128)(2,1)S(1)} %collective-permute-done.34.h1_ref.pair_ref, ...), custom_call_target="tpu_custom_call", output_to_operand_aliasing={{}: (3, {})} | custom-call | flops 1000000000 | tf_op jit(solution)/shard_map/pallas_call | solution.py:539
  186.2 4.1 %shard_map.281 = (bf16[256,1024]{1,0:T(8,128)(2,1)S(1)}, bf16[256,1024]{1,0:T(8,128)(2,1)S(1)}, f32[1,1024]{1,0:T(1,128)S(1)}, f32[64,1024]{1,0:T(8,128)S(1)}, b...) custom-call(bf16[64,1024]{1,0:T(8,128)(2,1)S(1)} %get-tuple-element.304.refs_0_, ...), custom_call_target="tpu_custom_call" | custom-call | flops 2000000000 | tf_op jit(solution)/shard_map/pallas_call | solution.py:97
  211.6 4.8 %all-to-all-start.2 = ((bf16[4,256,1024]{2,1,0:T(8,128)(2,1)}), bf16[4,256,1024]{2,1,0:T(8,128)(2,1)}, u32[]{:S(2)}, u32[]{:S(2)}) async-start(bf16[4,256,1024]{2,1,0:T(8,128)(2,1)} %shard_map.284), calls=%async_computation.2 | async-start | bytes 4194304 | tf_op jit(solution)/shard_map/all_to_all | solution.py:56
  226.4 6.4 %shard_map.285 = (bf16[256,1024]{1,0:T(8,128)(2,1)}, bf16[256,256]{1,0:T(8,128)(2,1)}, bf16[512,256]{1,0:T(8,128)(2,1)}, bf16[512,256]{1,0:T(8,128)(2,1)}, f32[6...) custom-call(bf16[64,1024]{1,0:T(8,128)(2,1)} %get-tuple-element.335.refs_0_, ...), custom_call_target="tpu_custom_call" | custom-call | flops 5000000000 | tf_op jit(solution)/shard_map/pallas_call | solution.py:97
  239.5 7.3 %shard_map.287.held_ref = f32[4096,1024]{1,0:T(8,128)} custom-call(f32[4,2,8,256]{3,2,1,0:T(8,128)S(1)} %get-tuple-element.410.rows_ref, bf16[4,256,1024]{2,1,0:T(8,128)(2,1)S(1)} %all-to-all-done.1.own_ref, bf16[4,256,1024]{2,1,0:T(8,128)(2,1)S(1)} %copy-done.1, bf16[4096,1024]{1,0:T(8,128)(2,1)} %e_ref.11, ...), custom_call_target="tpu_custom_call", output_to_operand_aliasing={{}: (4, {})} | custom-call | flops 1500000000 | tf_op jit(solution)/shard_map/pallas_call | solution.py:575
  254.6 7.4 %shard_map.290.held_ref = f32[4096,1024]{1,0:T(8,128)} custom-call(f32[4,2,8,256]{3,2,1,0:T(8,128)S(1)} %get-tuple-element.410.rows_ref, bf16[4,256,1024]{2,1,0:T(8,128)(2,1)S(1)} %all-to-all-done.1.own_ref, bf16[4,256,1024]{2,1,0:T(8,128)(2,1)S(1)} %copy-done.1, bf16[4096,1024]{1,0:T(8,128)(2,1)} %e_ref.11, ...), custom_call_target="tpu_custom_call", output_to_operand_aliasing={{}: (4, {})} | custom-call | flops 1500000000 | tf_op jit(solution)/shard_map/pallas_call | solution.py:575
  265.1 5.2 %shard_map.291 = (bf16[256,1024]{1,0:T(8,128)(2,1)}, bf16[256,768]{1,0:T(8,128)(2,1)}) custom-call(bf16[64,1024]{1,0:T(8,128)(2,1)} %get-tuple-element.367.refs_0_, bf16[64,1024]{1,0:T(8,128)(2,1)} %copy-done.64, bf16[64,1024]{1,0:T(8,128)(2,1)} %copy-done.62, bf16[64,1024]{1,0:T(8,128)(2,1)} %copy-done.61, bf16[2,256,1024]{2,1,0:T(8,128)(2,1)} %copy-done.21, ...), custom_call_target="tpu_custom_call" | custom-call | flops 4000000000 | tf_op jit(solution)/shard_map/pallas_call | solution.py:97
  270.3 4.3 %all-to-all-start.3 = ((bf16[4,512,256]{2,1,0:T(8,128)(2,1)}), bf16[4,512,256]{2,1,0:T(8,128)(2,1)}, u32[]{:S(2)}, u32[]{:S(2)}) async-start(bf16[4,512,256]{2,1,0:T(8,128)(2,1)} %shard_map.289), calls=%async_computation.3 | async-start | bytes 2097152 | tf_op jit(solution)/shard_map/all_to_all | solution.py:56
  283.5 4.5 %shard_map.294 = (f32[192,1024]{1,0:T(8,128)}, bf16[192,1024]{1,0:T(8,128)(2,1)}, bf16[192,1024]{1,0:T(8,128)(2,1)}, bf16[192,1024]{1,0:T(8,128)(2,1)}) custom-call(bf16[256,768]{1,0:T(8,128)(2,1)} %get-tuple-element.388.d, bf16[1024,768]{1,0:T(8,128)(2,1)} %copy-done.19, bf16[512,256]{1,0:T(8,128)(2,1)} %get-tuple-element.345.dk, ...), custom_call_target="tpu_custom_call" | custom-call | flops 3000000000 | tf_op jit(solution)/shard_map/pallas_call | solution.py:97
  292.1 7.4 %shard_map.296.held_ref = f32[4096,1024]{1,0:T(8,128)} custom-call(f32[4,2,8,256]{3,2,1,0:T(8,128)S(1)} %get-tuple-element.410.rows_ref, bf16[4,256,1024]{2,1,0:T(8,128)(2,1)S(1)} %all-to-all-done.1.own_ref, bf16[4,256,1024]{2,1,0:T(8,128)(2,1)S(1)} %copy-done.2, bf16[4096,1024]{1,0:T(8,128)(2,1)} %e_ref.11, ...), custom_call_target="tpu_custom_call", output_to_operand_aliasing={{}: (4, {})} | custom-call | flops 1500000000 | tf_op jit(solution)/shard_map/pallas_call | solution.py:575
  299.9 4.8 %all-to-all-start.4 = ((bf16[4,544,256]{2,1,0:T(8,128)(2,1)}), bf16[4,544,256]{2,1,0:T(8,128)(2,1)}, u32[]{:S(2)}, u32[]{:S(2)}) async-start(bf16[4,544,256]{2,1,0:T(8,128)(2,1)} %shard_map.295), calls=%async_computation.4 | async-start | bytes 2228224 | tf_op jit(solution)/shard_map/all_to_all | solution.py:56
  304.7 5.5 %collective-permute-start.68 = (bf16[128,1024]{1,0:T(8,128)(2,1)S(1)}, bf16[128,1024]{1,0:T(8,128)(2,1)S(1)}, u32[]{:S(2)}, u32[]{:S(2)}) collective-permute-start(bf16[128,1024]{1,0:T(8,128)(2,1)S(1)} %get-tuple-element.387), channel_id=1, source_target_pairs={{0,0},{1,1},{2,8},{3,9},{4,16},{5,17},{6,24},{7,25},{8,2},{9,3},{1... | collective-permute-start | bytes 786440 | tf_op jit(solution)/shard_map/ppermute | solution.py:1043
  316.8 24.0 %shard_map.298 = f32[4096,1024]{1,0:T(8,128)} custom-call(f32[4,2,8,256]{3,2,1,0:T(8,128)S(1)} %get-tuple-element.410.rows_ref, bf16[4,256,1024]{2,1,0:T(8,128)(2,1)S(1)} %all-to-all-done.1.own_ref, bf16[4,256,1024]{2,1,0:T(8,128)(2,1)S(1)} %copy-done.3, bf16[4096,1024]{1,0:T(8,128)(2,1)} %e_ref.11, ...), custom_call_target="tpu_custom_call", output_to_operand_aliasing={{}: (4, {})} | custom-call | flops 7500000256 | tf_op jit(solution)/shard_map/pallas_call | solution.py:575
  352.8 4.1 %collective-permute-done.65.p1 = bf16[208,256]{1,0:T(8,128)(2,1)S(1)} collective-permute-done((bf16[208,256]{1,0:T(8,128)(2,1)S(1)}, bf16[208,256]{1,0:T(8,128)(2,1)S(1)}, u32[]{:S(2)}, u32[]{:S(2)}) %collective-permute-start.65) | collective-permute-done | bytes 106528 | tf_op jit(solution)/shard_map/ppermute | solution.py:26
  (326 shorter events, 180.0 us)
Async XLA Ops:
  4.3 16.0 %collective-permute-start.2 = (bf16[1024,256]{1,0:T(8,128)(2,1)}, bf16[1024,256]{1,0:T(8,128)(2,1)S(1)}, u32[]{:S(2)}, u32[]{:S(2)}) collective-permute-start(bf16[1024,256]{1,0:T(8,128)(2,1)} %get-tuple-element.232), channel_id=1, source_target_pairs={{0,6},{1,7},{2,4},{3,5},{4,2},{5,3},{6,0},{7,1},{8,14},{9,15},{10,... | collective-permute-start | bytes 1572872 | tf_op jit(solution)/shard_map/ppermute | solution.py:26
  5.8 24.6 %collective-permute-start = (bf16[1024,256]{1,0:T(8,128)(2,1)}, bf16[1024,256]{1,0:T(8,128)(2,1)S(1)}, u32[]{:S(2)}, u32[]{:S(2)}) collective-permute-start(bf16[1024,256]{1,0:T(8,128)(2,1)} %get-tuple-element.229), channel_id=1, source_target_pairs={{0,2},{1,3},{2,0},{3,1},{4,6},{5,7},{6,4},{7,5},{8,10},{9,11},{10,... | collective-permute-start | bytes 1572872 | tf_op jit(solution)/shard_map/ppermute | solution.py:26
  7.3 23.1 %collective-permute-start.1 = (bf16[1024,256]{1,0:T(8,128)(2,1)}, bf16[1024,256]{1,0:T(8,128)(2,1)S(1)}, u32[]{:S(2)}, u32[]{:S(2)}) collective-permute-start(bf16[1024,256]{1,0:T(8,128)(2,1)} %get-tuple-element.231), channel_id=1, source_target_pairs={{0,4},{1,5},{2,6},{3,7},{4,0},{5,1},{6,2},{7,3},{8,12},{9,13},{10,... | collective-permute-start | bytes 1572872 | tf_op jit(solution)/shard_map/ppermute | solution.py:26
  7.9 24.0 %collective-permute-start.7 = (bf16[2,128,1024]{2,1,0:T(8,128)(2,1)S(1)}, bf16[2,128,1024]{2,1,0:T(8,128)(2,1)}, u32[]{:S(2)}, u32[]{:S(2)}) collective-permute-start(bf16[2,128,1024]{2,1,0:T(8,128)(2,1)S(1)} %bitcast.21), channel_id=1, source_target_pairs={{0,1},{1,0},{2,3},{3,2},{4,5},{5,4},{6,7},{7,6},{8,9},{9,8},{10,11... | collective-permute-start | bytes 1572872 | tf_op jit(solution)/shard_map/ppermute | solution.py:30
  8.0 24.5 %collective-permute-start.3 = (bf16[1024,256]{1,0:T(8,128)(2,1)S(1)}, bf16[1024,256]{1,0:T(8,128)(2,1)S(1)}, u32[]{:S(2)}, u32[]{:S(2)}) collective-permute-start(bf16[1024,256]{1,0:T(8,128)(2,1)S(1)} %get-tuple-element.228.refs_0_.refs_4_), channel_id=1, source_target_pairs={{0,1},{1,0},{2,3},{3,2},{4,5},{5,4},{6,7},{7,6},{8,9},{9,8},{10,11... | collective-permute-start | bytes 1572872 | tf_op jit(solution)/shard_map/ppermute | solution.py:30
  30.9 16.4 %collective-permute-start.9 = (bf16[128,1024]{1,0:T(8,128)(2,1)S(1)}, bf16[128,1024]{1,0:T(8,128)(2,1)S(1)}, u32[]{:S(2)}, u32[]{:S(2)}) collective-permute-start(bf16[128,1024]{1,0:T(8,128)(2,1)S(1)} %bitcast.26), channel_id=1, source_target_pairs={{0,4},{1,5},{2,6},{3,7},{4,0},{5,1},{6,2},{7,3},{8,12},{9,13},{10,... | collective-permute-start | bytes 786440 | tf_op jit(solution)/shard_map/ppermute | solution.py:26
  31.9 15.5 %collective-permute-start.8 = (bf16[128,1024]{1,0:T(8,128)(2,1)S(1)}, bf16[128,1024]{1,0:T(8,128)(2,1)S(1)}, u32[]{:S(2)}, u32[]{:S(2)}) collective-permute-start(bf16[128,1024]{1,0:T(8,128)(2,1)S(1)} %bitcast.27), channel_id=1, source_target_pairs={{0,2},{1,3},{2,0},{3,1},{4,6},{5,7},{6,4},{7,5},{8,10},{9,11},{10,... | collective-permute-start | bytes 786440 | tf_op jit(solution)/shard_map/ppermute | solution.py:26
  47.4 15.8 %collective-permute-start.16 = (bf16[128,1024]{1,0:T(8,128)(2,1)S(1)}, bf16[128,1024]{1,0:T(8,128)(2,1)S(1)}, u32[]{:S(2)}, u32[]{:S(2)}) collective-permute-start(bf16[128,1024]{1,0:T(8,128)(2,1)S(1)} %bitcast.28), channel_id=1, source_target_pairs={{0,6},{1,7},{2,4},{3,5},{4,2},{5,3},{6,0},{7,1},{8,14},{9,15},{10,... | collective-permute-start | bytes 786440 | tf_op jit(solution)/shard_map/ppermute | solution.py:26
  61.1 11.8 %collective-permute-start.17 = (bf16[128,1024]{1,0:T(8,128)(2,1)S(1)}, bf16[128,1024]{1,0:T(8,128)(2,1)S(1)}, u32[]{:S(2)}, u32[]{:S(2)}) collective-permute-start(bf16[128,1024]{1,0:T(8,128)(2,1)S(1)} %get-tuple-element.260), channel_id=1, source_target_pairs={{0,2},{1,3},{2,0},{3,1},{4,6},{5,7},{6,4},{7,5},{8,10},{9,11},{10,... | collective-permute-start | bytes 786440 | tf_op jit(solution)/shard_map/ppermute | solution.py:26
  79.4 11.3 %collective-permute-start.27 = (bf16[512,1024]{1,0:T(8,128)(2,1)S(1)}, bf16[512,1024]{1,0:T(8,128)(2,1)S(1)}, u32[]{:S(2)}, u32[]{:S(2)}) collective-permute-start(bf16[512,1024]{1,0:T(8,128)(2,1)S(1)} %copy-done.10), channel_id=1, source_target_pairs={{0,1},{1,0},{2,3},{3,2},{4,5},{5,4},{6,7},{7,6},{8,9},{9,8},{10,11... | collective-permute-start | bytes 3145736 | tf_op jit(solution)/shard_map/ppermute | solution.py:30
  146.9 54.2 %all-to-all-start.1 = ((bf16[4,256,1024]{2,1,0:T(8,128)(2,1)}), bf16[4,256,1024]{2,1,0:T(8,128)(2,1)S(1)}, u32[]{:S(2)}, u32[]{:S(2)}) async-start(bf16[4,256,1024]{2,1,0:T(8,128)(2,1)} %copy-done.4), calls=%async_computation.1 | async-start | bytes 4194304 | tf_op jit(solution)/shard_map/all_to_all | solution.py:56
  211.6 53.5 %all-to-all-start.2 = ((bf16[4,256,1024]{2,1,0:T(8,128)(2,1)}), bf16[4,256,1024]{2,1,0:T(8,128)(2,1)}, u32[]{:S(2)}, u32[]{:S(2)}) async-start(bf16[4,256,1024]{2,1,0:T(8,128)(2,1)} %shard_map.284), calls=%async_computation.2 | async-start | bytes 4194304 | tf_op jit(solution)/shard_map/all_to_all | solution.py:56
  235.8 17.6 %collective-permute-start.56 = (bf16[4,512,256]{2,1,0:T(8,128)(2,1)S(1)}, bf16[4,512,256]{2,1,0:T(8,128)(2,1)S(1)}, u32[]{:S(2)}, u32[]{:S(2)}) collective-permute-start(bf16[4,512,256]{2,1,0:T(8,128)(2,1)S(1)} %get-tuple-element.360), channel_id=1, source_target_pairs={{0,1},{1,0},{2,3},{3,2},{4,5},{5,4},{6,7},{7,6},{8,9},{9,8},{10,11... | collective-permute-start | bytes 3145736 | tf_op jit(solution)/shard_map/ppermute | solution.py:30
  249.9 12.1 %collective-permute-start.55 = (bf16[64,1024]{1,0:T(8,128)(2,1)}, bf16[64,1024]{1,0:T(8,128)(2,1)S(1)}, u32[]{:S(2)}, u32[]{:S(2)}) collective-permute-start(bf16[64,1024]{1,0:T(8,128)(2,1)} %get-tuple-element.367.refs_0_), channel_id=1, source_target_pairs={{0,6},{1,7},{2,4},{3,5},{4,2},{5,3},{6,0},{7,1},{8,14},{9,15},{10,... | collective-permute-start | bytes 393224 | tf_op jit(solution)/shard_map/ppermute | solution.py:26
  270.3 29.6 %all-to-all-start.3 = ((bf16[4,512,256]{2,1,0:T(8,128)(2,1)}), bf16[4,512,256]{2,1,0:T(8,128)(2,1)}, u32[]{:S(2)}, u32[]{:S(2)}) async-start(bf16[4,512,256]{2,1,0:T(8,128)(2,1)} %shard_map.289), calls=%async_computation.3 | async-start | bytes 2097152 | tf_op jit(solution)/shard_map/all_to_all | solution.py:56
  280.0 19.5 %collective-permute-start.58 = (bf16[32,1024]{1,0:T(8,128)(2,1)S(1)}, bf16[32,1024]{1,0:T(8,128)(2,1)S(1)}, u32[]{:S(2)}, u32[]{:S(2)}) collective-permute-start(bf16[32,1024]{1,0:T(8,128)(2,1)S(1)} %get-tuple-element.396), channel_id=1, source_target_pairs={{0,2},{1,3},{2,0},{3,1},{4,6},{5,7},{6,4},{7,5},{8,10},{9,11},{10,... | collective-permute-start | bytes 196616 | tf_op jit(solution)/shard_map/ppermute | solution.py:26
  281.8 17.7 %collective-permute-start.59 = (bf16[32,1024]{1,0:T(8,128)(2,1)S(1)}, bf16[32,1024]{1,0:T(8,128)(2,1)S(1)}, u32[]{:S(2)}, u32[]{:S(2)}) collective-permute-start(bf16[32,1024]{1,0:T(8,128)(2,1)S(1)} %get-tuple-element.397), channel_id=1, source_target_pairs={{0,4},{1,5},{2,6},{3,7},{4,0},{5,1},{6,2},{7,3},{8,12},{9,13},{10,... | collective-permute-start | bytes 196616 | tf_op jit(solution)/shard_map/ppermute | solution.py:26
  282.7 16.8 %collective-permute-start.60 = (bf16[32,1024]{1,0:T(8,128)(2,1)S(1)}, bf16[32,1024]{1,0:T(8,128)(2,1)S(1)}, u32[]{:S(2)}, u32[]{:S(2)}) collective-permute-start(bf16[32,1024]{1,0:T(8,128)(2,1)S(1)} %get-tuple-element.398), channel_id=1, source_target_pairs={{0,6},{1,7},{2,4},{3,5},{4,2},{5,3},{6,0},{7,1},{8,14},{9,15},{10,... | collective-permute-start | bytes 196616 | tf_op jit(solution)/shard_map/ppermute | solution.py:26
  299.9 43.0 %all-to-all-start.4 = ((bf16[4,544,256]{2,1,0:T(8,128)(2,1)}), bf16[4,544,256]{2,1,0:T(8,128)(2,1)}, u32[]{:S(2)}, u32[]{:S(2)}) async-start(bf16[4,544,256]{2,1,0:T(8,128)(2,1)} %shard_map.295), calls=%async_computation.4 | async-start | bytes 2228224 | tf_op jit(solution)/shard_map/all_to_all | solution.py:56
  304.7 52.2 %collective-permute-start.68 = (bf16[128,1024]{1,0:T(8,128)(2,1)S(1)}, bf16[128,1024]{1,0:T(8,128)(2,1)S(1)}, u32[]{:S(2)}, u32[]{:S(2)}) collective-permute-start(bf16[128,1024]{1,0:T(8,128)(2,1)S(1)} %get-tuple-element.387), channel_id=1, source_target_pairs={{0,0},{1,1},{2,8},{3,9},{4,16},{5,17},{6,24},{7,25},{8,2},{9,3},{1... | collective-permute-start | bytes 786440 | tf_op jit(solution)/shard_map/ppermute | solution.py:1043
  310.2 30.6 %collective-permute-start.62 = (bf16[192,1024]{1,0:T(8,128)(2,1)}, bf16[192,1024]{1,0:T(8,128)(2,1)}, u32[]{:S(2)}, u32[]{:S(2)}) collective-permute-start(bf16[192,1024]{1,0:T(8,128)(2,1)} %get-tuple-element.404), channel_id=1, source_target_pairs={{0,4},{1,5},{2,6},{3,7},{4,0},{5,1},{6,2},{7,3},{8,12},{9,13},{10,... | collective-permute-start | bytes 1179656 | tf_op jit(solution)/shard_map/ppermute | solution.py:26
  313.5 27.3 %collective-permute-start.63 = (bf16[192,1024]{1,0:T(8,128)(2,1)}, bf16[192,1024]{1,0:T(8,128)(2,1)}, u32[]{:S(2)}, u32[]{:S(2)}) collective-permute-start(bf16[192,1024]{1,0:T(8,128)(2,1)} %get-tuple-element.405), channel_id=1, source_target_pairs={{0,6},{1,7},{2,4},{3,5},{4,2},{5,3},{6,0},{7,1},{8,14},{9,15},{10,... | collective-permute-start | bytes 1179656 | tf_op jit(solution)/shard_map/ppermute | solution.py:26
  313.5 29.4 %collective-permute-start.61 = (bf16[192,1024]{1,0:T(8,128)(2,1)S(1)}, bf16[192,1024]{1,0:T(8,128)(2,1)}, u32[]{:S(2)}, u32[]{:S(2)}) collective-permute-start(bf16[192,1024]{1,0:T(8,128)(2,1)S(1)} %copy-done.53), channel_id=1, source_target_pairs={{0,2},{1,3},{2,0},{3,1},{4,6},{5,7},{6,4},{7,5},{8,10},{9,11},{10,... | collective-permute-start | bytes 1179656 | tf_op jit(solution)/shard_map/ppermute | solution.py:26
  344.8 12.1 %collective-permute-start.64 = (bf16[272,256]{1,0:T(8,128)(2,1)S(1)}, bf16[272,256]{1,0:T(8,128)(2,1)S(1)}, u32[]{:S(2)}, u32[]{:S(2)}) collective-permute-start(bf16[272,256]{1,0:T(8,128)(2,1)S(1)} %get-tuple-element.414), channel_id=1, source_target_pairs={{0,0},{1,1},{2,8},{3,9},{4,16},{5,17},{6,24},{7,25},{8,2},{9,3},{1... | collective-permute-start | bytes 417800 | tf_op jit(solution)/shard_map/ppermute | solution.py:1043
  (123 other events, 998.9 us)
where the time goes:
time: 365 us; the launch traced here: 362 us
  Pallas kernels  146 us (40%)
  starting transfers between devices  91.7 us (25%)
  waiting for transfers between devices  81.6 us (22%)
  local copies, waits for them, and re-layouts  25.7 us (7%)
  blocking collectives  14.8 us (4%)
    ppermute x54, waiting for transfers between devices, from_chip(): return lax.ppermute(x, 'pb', pairs)  72.5 us
    pallas_call x31, Pallas kernels, call(): pl.pallas_call(kernel, out_shape=places, scratch_shapes=scratch, compiler...  64.6 us
    ppermute x54, starting transfers between devices, from_chip(): return lax.ppermute(x, 'pb', pairs)  63.9 us
    pallas_call x4, Pallas kernels, embedding_piece(): pl.pallas_call(functools.partial(embedding_kernel, first), grid=(steps,),...  46.1 us
    unnamed x153, local copies, waits for them, and re-layouts  23.7 us
    all_to_all x4, starting transfers between devices, across_slots(): return lax.all_to_all(x, 'slot', 0, 0, tiled=True)  17.8 us
    all_to_all x1, blocking collectives, shards(): lax.all_to_all(jnp.broadcast_to(payload[None], (n_all,) + payload.shape),...  14.8 us
    pallas_call x2, Pallas kernels, own_embedding(): pl.pallas_call(own_embedding_kernel, grid=(steps,), in_specs=[pl.BlockSpe...  12.9 us
  transfers between devices with their start and end apart: 73, of which 26 were waited for; matrix products, arithmetic and copies ran while one was open for 1% of the time, Pallas kernels for 34%

commit v1 on v0

--- a/solution.py
+++ b/solution.py
@@ -89,15 +89,16 @@
     return pl.CostEstimate(flops=int(us * 1e9), bytes_accessed=0, transcendentals=0)
 
 
-def call(kernel, outs, *args, us=2.0, far=False, scratch=()):
+def call(kernel, outs, *args, us=2.0, far=(), scratch=()):
     shapes = [jax.ShapeDtypeStruct(*o) for o in outs]
     held = sum(a.size * a.dtype.itemsize for a in (*args, *shapes))
     params = limit(8 + held * 5 // 4 // MIB)
-    places = [pltpu.HBM(*o) for o in outs] if far else shapes
+    far = range(len(outs)) if far is True else far
+    places = [pltpu.HBM(*o) if n in far else s for n, (o, s) in enumerate(zip(outs, shapes))]
     results = pl.pallas_call(
         kernel, out_shape=places, scratch_shapes=scratch, compiler_params=params, cost_estimate=work(us)
     )(*args)
-    return [in_hbm(r) for r in results] if far else results
+    return [in_hbm(r) if n in far else r for n, r in enumerate(results)]
 
 
 def in_hbm(x):
@@ -765,19 +766,38 @@
             out[s, top + SMALL : top + SMALL + 1, :wide] = jnp.where(first, ends[0], ends[1]).astype(BF)
 
 
-def input_back_kernel(d, w_self, dk, dv, w_cross, mine_out, *send):
+def input_back_kernel(d, w_self, dk, dv, w_cross, f_got, mine_out, rest_out, *send):
+    chip, _ = place()
     quarter = dk.shape[1]
     length, memory = d.shape[0] // CHIPS, dk.shape[0] // CHIPS
     y = dot(d[...], w_self[...], NT)
     m = dot(dk[...], w_cross[:, quarter : 2 * quarter], NT) + dot(dv[...], w_cross[:, 2 * quarter :], NT)
-    for k, out in enumerate((mine_out, *send)):
-        out[:length, :] = y[k * length : (k + 1) * length].astype(out.dtype)
-        out[length:, :] = m[k * memory : (k + 1) * memory].astype(out.dtype)
-
-
-def input_total_kernel(base, mine, r1, r2, r3, source_out, memory_out):
+    f = sum(f_got[n].astype(F32) for n in range(SLOTS)).astype(BF)
+    both = length + memory
+    unit = (send[0].shape[0] - both)
+    rest_out[...] = f[CHIPS * unit :]
+    mine_out[:length, :] = y[:length]
+    mine_out[length:, :] = m[:memory]
+    for k, out in enumerate(send):
+        if k:
+            out[:length, :] = y[k * length : (k + 1) * length].astype(BF)
+            out[length:both, :] = m[k * memory : (k + 1) * memory].astype(BF)
+        block = jnp.zeros((unit, f.shape[1]), BF)
+        for b in range(CHIPS):
+            block = jnp.where((chip ^ k) == b, f[b * unit : (b + 1) * unit], block)
+        out[both:, :] = block
+
+
+def input_total_kernel(base, mine, own, r1, r2, r3, source_out, memory_out, up_out):
+    chip, _ = place()
     length = base.shape[0]
-    y = mine[...] + r1[...].astype(F32) + r2[...].astype(F32) + r3[...].astype(F32)
+    both = mine.shape[0]
+    width = base.shape[1]
+    y = mine[...]
+    for k, r in enumerate((own, r1, r2, r3)):
+        if k:
+            y = y + r[:both, :].astype(F32)
+        up_out[:, rows_at((chip ^ k) * width, width, 128)] = r[both:, :].astype(F32)
     source_out[...] = base[...] + y[:length]
     memory_out[...] = y[length:]
 
@@ -785,22 +805,6 @@
 def core_sum_kernel(mine, got, out):
     for n in range(SLOTS):
         out[n] = (mine[n].astype(F32) + got[n].astype(F32)).astype(BF)
-
-
-def column_pieces_kernel(count, got, *outs):
-    *pieces, rest = outs
-    chip, _ = place()
-    unit = pieces[0].shape[0] // count
-    y = sum(got[n].astype(F32) for n in range(SLOTS))
-    top = count * CHIPS * unit
-    rest[...] = y[top:].astype(BF)
-    hold = y[:top].astype(BF).reshape(count, CHIPS, unit, y.shape[1])
-    for k in range(CHIPS):
-        for j in range(count):
-            block = jnp.zeros((unit, y.shape[1]), BF)
-            for b in range(CHIPS):
-                block = jnp.where((chip ^ k) == b, hold[j, b], block)
-            pieces[k][j * unit : (j + 1) * unit, :] = block
 
 
 def attn_pieces_kernel(s_got, c_got, *outs):
@@ -837,11 +841,10 @@
     mine = jnp.zeros((SMALL, unit), F32)
     for b in range(CHIPS):
         mine = jnp.where(chip == b, total[:, b * unit : (b + 1) * unit], mine)
-    columns = jnp.transpose(jnp.concatenate([mine, jnp.zeros((SMALL, 128 - unit), F32)], axis=1))
-    bias_out[...] = columns[:unit, 0:6]
-    gain_out[...] = columns[:unit, 6:9]
-    shift_out[...] = columns[:unit, 9:12]
-    last_out[...] = mine[12:13, :]
+    bias_out[...] = mine[0:6]
+    gain_out[...] = mine[6:9]
+    shift_out[...] = mine[9:12]
+    last_out[...] = mine[12:13]
 
 
 def rows_out_kernel(owned, f_owned, out, down_out, in_out):
@@ -852,13 +855,6 @@
             out[m, :, b * quarter : (b + 1) * quarter] = owned[m * n + b * unit : m * n + (b + 1) * unit, :].astype(F32)
     down_out[...] = f_owned[...].astype(F32)
     in_out[...] = owned[2 * n : 2 * n + 1, : in_out.shape[1]].astype(F32)
-
-
-def up_out_kernel(p0, p1, p2, p3, out):
-    chip, _ = place()
-    quarter = p0.shape[1]
-    for k, p in enumerate((p0, p1, p2, p3)):
-        out[:, rows_at((chip ^ k) * quarter, quarter, 128)] = p[...].astype(F32)
 
 
 def shards(
@@ -953,6 +949,7 @@
     got_low = [low_two] + others(low_two)
     third[3], got_third[1] = tie(third[3], got_third[1])
     got_third.append(from_chip(third[3], 3))
+    got_third[3], *got_low = tie(got_third[3], *got_low)
     (up_half,) = call(up_half_kernel, [((CHIPS, rows, ff), BF)], *got_third)
     up_half_pair = from_core(up_half)
     low_two_all, upward, active, w_up, w_down, mine, *send = call(
@@ -968,7 +965,7 @@
     )
 
     held, spread_held = call(
-        stack_kernel, [(every, BF), ((n_slot,) + every, BF)], final_low, *others(final_low), us=1
+        stack_kernel, [(every, BF), ((n_slot,) + every, BF)], final_low, *others(final_low), us=1, far=(1,) if teams == 1 else ()
     )
     pair = from_core(held)
 
@@ -1042,14 +1039,6 @@
                 pairs.append((s * n_pb + i, b * n_pb + t * TEAM + s * CORES + c))
         return lax.ppermute(g, ("slot", "pb"), pairs)
 
-    def column_pieces(count, got, n, cols):
-        rest = got.shape[1] - count * CHIPS * n
-        *piece, rest = call(
-            functools.partial(column_pieces_kernel, count),
-            [((count * n, cols), BF)] * CHIPS + [((rest, cols), BF)], got,
-        )
-        return [piece[0]] + give_far(piece[1:]), rest
-
     x_all, w_self, queries, keys, values, mixed, w_out, m_all, w_cross, cross_keys, cross_values = (
         in_hbm(v)
         for v in (x_all, w_self, queries, keys, values, mixed, w_out, m_all, w_cross, cross_keys, cross_values)
@@ -1072,10 +1061,10 @@
         [(every, BF), ((CHIPS * length, ff), BF), ((1, ff), F32), (block, F32)] + sends,
         e_three, *got_e, upward, w_up, w_down,
     )
-    got = give_far(send)
+    got = give(send)
     f_shape = (n_slot, CHIPS * unit + ff // TEAM, width)
     du, send[0] = tie(du, send[0])
-    f_mine, f_other = call(ffn_grads_kernel, [(f_shape, BF)] * 2, low_two_all, du, active, e_all, us=3)
+    f_mine, f_other = far_call(ffn_grads_kernel, [(f_shape, BF)] * 2, low_two_all, du, active, e_all, us=3)
     f_other, all_held, *got = tie(f_other, all_held, *got)
     all_pair = from_core(all_held)
     dr_two, e_two, sums_two = far_call(
@@ -1083,7 +1072,7 @@
     )
     got_e = give_far([e_two] * 3)
     f_got = from_core(f_other)
-    f_got, all_pair, e_two = tie(f_got, all_pair, e_two)
+    f_got, all_pair, got_e[2] = tie(f_got, all_pair, got_e[2])
     states = [jnp.stack([all_teams(h[n]) for n in range(n_slot)]) if teams > 1 else h for h in (all_held, all_pair)]
     (f_total,) = far_call(core_sum_kernel, [(f_shape, BF)], f_mine, f_got)
     f_got = across_slots(f_total)
@@ -1093,7 +1082,7 @@
         e_two, *got_e, w_out, w_cross, cross_queries, cross_keys, cross_values, us=5,
         scratch=[pltpu.VMEM(cols, BF)],
     )
-    got = give_far(send)
+    got = give(send)
     dqc, send[0] = tie(dqc, send[0])
     g_shape = (n_slot, 4 * CHIPS * unit, quarter)
     c_mine, c_other, c_sums = call(
@@ -1106,16 +1095,16 @@
     dr_one, e_one, sums_one = far_call(
         functools.partial(norm_back_kernel, 0, True), grads, dr_two, mine, *got, z_one, inv_one, vec, us=1
     )
-    got_e = give_far([e_one] * 3)
+    got_e = give([e_one] * 3)
     c_got, e_one = tie(c_got, e_one)
     (c_total,) = far_call(core_sum_kernel, [(g_shape, BF)], c_mine, c_got)
     (c_total,) = piece(c_total)
-    f_got, *got_e = then(f_got, *got_e)
+    got_e = then(*got_e)
     e_all_one, d_self = far_call(
         self_back_kernel, [(every, BF), ((CHIPS * length, 3 * quarter), BF)], e_one, *got_e, w_out, queries, keys, values, us=4,
         scratch=[pltpu.VMEM(cols, BF)],
     )
-    c_total, d_self = tie(c_total, d_self)
+    c_total, d_self, f_got = tie(c_total, d_self, f_got)
     c_got = across_slots(c_total)
     s_shape = (n_slot, g_shape[1] + 2 * SMALL, quarter)
     s_mine, s_other = far_call(
@@ -1123,20 +1112,21 @@
     )
     s_got = from_core(s_other)
     f_got, s_mine = tie(f_got, s_mine)
-    f_pieces, f_rest = column_pieces(1, f_got, unit, width)
+    both = (length + passage, width)
+    f_rest = (f_shape[1] - CHIPS * unit, width)
+    mine, f_rest, *send = far_call(
+        input_back_kernel, [(both, F32), (f_rest, BF)] + [((both[0] + unit, width), BF)] * CHIPS,
+        d_self, w_self, dkc, dvc, w_cross, f_got, us=3,
+    )
     f_owned = to_owner(f_rest)
-    d_self, f_rest = tie(d_self, f_rest)
-    both = (length + passage, width)
-    mine, *send = far_call(input_back_kernel, [(both, F32)] + [(both, BF)] * 3, d_self, w_self, dkc, dvc, w_cross, us=3)
     s_got, send[0] = tie(s_got, send[0])
     (s_total,) = far_call(core_sum_kernel, [(s_shape, BF)], s_mine, s_got)
     (s_total,) = pieces(1, s_total)
-    c_got, *f_pieces = then(c_got, *f_pieces)
+    (c_got,) = then(c_got)
     s_total, send[0], c_got = tie(s_total, send[0], c_got)
     s_got = across_slots(s_total)
-    got = give_far(send)
-    (out_up,) = call(up_out_kernel, [((unit, up_w.shape[1]), F32)], *f_pieces, us=1)
-    (out_up,) = pieces(len(parts) + 1 - len(made), out_up)
+    got = give(send[1:])
+    (send[0],) = pieces(len(parts) + 1 - len(made), send[0])
     s_got, *got = then(s_got, *got)
     *piece_parts, rest = call(
         attn_pieces_kernel,
@@ -1145,13 +1135,14 @@
     )
     last = give(piece_parts[1:])
     owned = to_owner(rest)
-    grad_source, grad_passage = call(
-        input_total_kernel, [(block, F32), ((passage, width), F32)], dr_one, mine, *got, us=1
+    grad_source, grad_passage, out_up = call(
+        input_total_kernel, [(block, F32), ((passage, width), F32), ((unit, up_w.shape[1]), F32)],
+        dr_one, mine, send[0], *got, us=1,
     )
     owned, grad_source, *last = tie(owned, grad_source, *last)
     out_attn, *vectors = call(
         attn_out_kernel,
-        [((6, unit, width), F32), ((unit, 6), F32), ((unit, 3), F32), ((unit, 3), F32), ((1, unit), F32)],
+        [((6, unit, width), F32), ((6, unit), F32), ((3, unit), F32), ((3, unit), F32), ((1, unit), F32)],
         piece_parts[0], *last, us=1,
     )
     outs, out_down, sum_in_out = call(
@@ -1160,7 +1151,7 @@
     out_attn = settle(jnp.moveaxis(out_attn, 0, 1))
     out_outputs = settle(jnp.moveaxis(outs, 0, 1))
     out_up, out_down = settle(out_up), settle(out_down)
-    vectors = [settle(v) for v in (*vectors[:3], sum_in_out[0], vectors[3][0])]
+    vectors = [settle(v) for v in (vectors[0].T, vectors[1].T, vectors[2].T, sum_in_out[0], vectors[3][0])]
     return (
         token_logprob[:, :length],
         grad_source[None, None],

time: 365 us -> 358 us (0.981)
  local copies, waits for them, and re-layouts: 25.7 us -> 11.2 us
  Pallas kernels: 146 us -> 155 us
    unnamed x153 -> x122, local copies, waits for them, and re-layouts: 23.7 us -> 10.7 us
    pallas_call x4, Pallas kernels: 46.1 us -> 51.1 us  [embedding_piece(): pl.pallas_call(functools.partial(embedding_kernel, first), grid=(steps,),...]
    pallas_call x31 -> x29, Pallas kernels: 64.6 us -> 68.9 us  [call(): pl.pallas_call(kernel, out_shape=places, scratch_shapes=scratch, compiler...]
    ppermute x54 -> x51, waiting for transfers between devices: 72.5 us -> 70.4 us  [from_chip(): return lax.ppermute(x, 'pb', pairs)]
    ppermute x54 -> x51, starting transfers between devices: 63.9 us -> 64 us  [from_chip(): return lax.ppermute(x, 'pb', pairs)]
  transfers between devices with their start and end apart: 73 -> 70, of which waited for: 26 -> 26; matrix products, arithmetic and copies ran while one was open for 1% -> 0% of each run, Pallas kernels for 34% -> 37%
where the time goes in v1:
time: 358 us; the launch traced here: 354 us
  Pallas kernels  155 us (43%)
  starting transfers between devices  90.6 us (25%)
  waiting for transfers between devices  80.1 us (22%)
  blocking collectives  14.4 us (4%)
  local copies, waits for them, and re-layouts  11.2 us (3%)
    ppermute x51, waiting for transfers between devices, from_chip(): return lax.ppermute(x, 'pb', pairs)  70.4 us
    pallas_call x29, Pallas kernels, call(): pl.pallas_call(kernel, out_shape=places, scratch_shapes=scratch, compiler...  68.9 us
    ppermute x51, starting transfers between devices, from_chip(): return lax.ppermute(x, 'pb', pairs)  64 us
    pallas_call x4, Pallas kernels, embedding_piece(): pl.pallas_call(functools.partial(embedding_kernel, first), grid=(steps,),...  51.1 us
    all_to_all x4, starting transfers between devices, across_slots(): return lax.all_to_all(x, 'slot', 0, 0, tiled=True)  17.6 us
    all_to_all x1, blocking collectives, shards(): lax.all_to_all(jnp.broadcast_to(payload[None], (n_all,) + payload.shape),...  14.4 us
    pallas_call x2, Pallas kernels, own_embedding(): pl.pallas_call(own_embedding_kernel, grid=(steps,), in_specs=[pl.BlockSpe...  12.9 us
    pallas_call x1, Pallas kernels, state_grad(): pl.pallas_call(state_grad_kernel, grid=(vocab // tile,), in_specs=[pl.Blo...  11 us
  transfers between devices with their start and end apart: 70, of which 26 were waited for; matrix products, arithmetic and copies ran while one was open for 0% of the time, Pallas kernels for 37%

profile of v1, /device:TPU:2, one launch (start us, length us, event | category | flops | bytes accessed | tf_op | source)
XLA Modules:
  0.0 353.9 jit_solution(17224242819054986317)
XLA Ops:
  8.5 11.8 %collective-permute-done.2.refs_3_.refs_7_ = bf16[1024,256]{1,0:T(8,128)(2,1)S(1)} collective-permute-done((bf16[1024,256]{1,0:T(8,128)(2,1)}, bf16[1024,256]{1,0:T(8,128)(2,1)S(1)}, u32[]{:S(2)}, u32[]{:S(2)}) %collective-permute-start.2) | collective-permute-done | bytes 524320 | tf_op jit(solution)/shard_map/ppermute | solution.py:26
  20.6 9.8 %collective-permute-done.refs_1_.refs_5_ = bf16[1024,256]{1,0:T(8,128)(2,1)S(1)} collective-permute-done((bf16[1024,256]{1,0:T(8,128)(2,1)}, bf16[1024,256]{1,0:T(8,128)(2,1)S(1)}, u32[]{:S(2)}, u32[]{:S(2)}) %collective-permute-start) | collective-permute-done | bytes 524320 | tf_op jit(solution)/shard_map/ppermute | solution.py:26
  33.1 4.3 %shard_map.264 = (bf16[256,1024]{1,0:T(8,128)(2,1)S(1)}, bf16[1024,768]{1,0:T(8,128)(2,1)S(1)}, bf16[256,256]{1,0:T(8,128)(2,1)S(1)}, bf16[256,256]{1,0:T(8,128)...) custom-call(bf16[1024,256]{1,0:T(8,128)(2,1)S(1)} %get-tuple-element, ...), custom_call_target="tpu_custom_call" | custom-call | flops 2000000000 | tf_op jit(solution)/shard_map/pallas_call | solution.py:98
  51.8 7.0 %collective-permute-done.15.refs_3_ = bf16[64,1024]{1,0:T(8,128)(2,1)S(1)} collective-permute-done((bf16[64,1024]{1,0:T(8,128)(2,1)S(1)}, bf16[64,1024]{1,0:T(8,128)(2,1)S(1)}, u32[]{:S(2)}, u32[]{:S(2)}) %collective-permute-start.15) | collective-permute-done | bytes 131104 | tf_op jit(solution)/shard_map/ppermute | solution.py:26
  80.8 6.0 %collective-permute-done.25.refs_3_ = bf16[64,1024]{1,0:T(8,128)(2,1)S(1)} collective-permute-done((bf16[64,1024]{1,0:T(8,128)(2,1)S(1)}, bf16[64,1024]{1,0:T(8,128)(2,1)S(1)}, u32[]{:S(2)}, u32[]{:S(2)}) %collective-permute-start.25) | collective-permute-done | bytes 131104 | tf_op jit(solution)/shard_map/ppermute | solution.py:26
  115.5 10.7 %shard_map.274 = (f32[4096,512]{1,0:T(8,128)}, f32[16,128]{1,0:T(8,128)S(1)}) custom-call(bf16[256,1024]{1,0:T(8,128)(2,1)S(1)} %get-tuple-element.285.h0_ref.own_ref, bf16[256,1024]{1,0:T(8,128)(2,1)S(1)} %collective-permute-done.34.h1_ref.pair_ref, s32[1,512]{1,0:T(1,128)S(1)} %concatenate.10.ids_ref, f32[1,128]{1,0:T(1,128)S(1)} %concatenate.11.own_ref, ...), custom_call_target="tpu_custom_call" | custom-call | flops 10000000000 | tf_op jit(solution)/shard_map/pallas_call | solution.py:387
  126.2 14.4 %all_to_all.25.all_ref = f32[32,16,128]{2,1,0:T(8,128)S(1)} all-to-all(f32[32,16,128]{2,1,0:T(8,128)S(1)} %broadcast_in_dim.29), channel_id=1, replica_groups=mesh['slot'=4,'pb'=8] {'slot','pb'}, dimensions={0} | all-to-all | bytes 524288 | tf_op jit(solution)/shard_map/all_to_all | solution.py:983
  140.6 4.8 %all-to-all-start.1 = ((bf16[4,256,1024]{2,1,0:T(8,128)(2,1)}), bf16[4,256,1024]{2,1,0:T(8,128)(2,1)}, u32[]{:S(2)}, u32[]{:S(2)}) async-start(bf16[4,256,1024]{2,1,0:T(8,128)(2,1)} %get-tuple-element.325), calls=%async_computation.1 | async-start | bytes 4194304 | tf_op jit(solution)/shard_map/all_to_all | solution.py:56
  146.2 11.0 %shard_map.276 = (f32[256,1024]{1,0:T(8,128)S(1)}, bf16[256,1024]{1,0:T(8,128)(2,1)S(1)}, bf16[4096,512]{1,0:T(8,128)(2,1)}) custom-call(f32[4096,512]{1,0:T(8,128)} %get-tuple-element.291.l_ref, f32[1,2,8,256]{3,2,1,0:T(8,128)S(1)} %get-tuple-element.292.rows_ref, bf16[4096,1024]{1,0:T(8,128)(2,1)} %e_ref.11), custom_call_target="tpu_custom_call" | custom-call | flops 11000000512 | tf_op jit(solution)/shard_map/pallas_call | solution.py:508
  163.0 6.4 %shard_map.278.refs_0_ = f32[4096,1024]{1,0:T(8,128)} custom-call(bf16[4096,512]{1,0:T(8,128)(2,1)} %get-tuple-element.309.d_ref, bf16[256,1024]{1,0:T(8,128)(2,1)S(1)} %get-tuple-element.285.h0_ref.own_ref, bf16[256,1024]{1,0:T(8,128)(2,1)S(1)} %collective-permute-done.34.h1_ref.pair_ref), custom_call_target="tpu_custom_call" | custom-call | flops 1000000000 | tf_op jit(solution)/shard_map/pallas_call | solution.py:540
  174.2 6.5 %shard_map.280.held_ref = f32[4096,1024]{1,0:T(8,128)} custom-call(bf16[4096,512]{1,0:T(8,128)(2,1)} %get-tuple-element.309.d_ref, bf16[256,1024]{1,0:T(8,128)(2,1)S(1)} %get-tuple-element.285.h0_ref.own_ref, bf16[256,1024]{1,0:T(8,128)(2,1)S(1)} %collective-permute-done.34.h1_ref.pair_ref, ...), custom_call_target="tpu_custom_call", output_to_operand_aliasing={{}: (3, {})} | custom-call | flops 1000000000 | tf_op jit(solution)/shard_map/pallas_call | solution.py:540
  180.7 4.2 %shard_map.281 = (bf16[256,1024]{1,0:T(8,128)(2,1)S(1)}, bf16[256,1024]{1,0:T(8,128)(2,1)S(1)}, f32[1,1024]{1,0:T(1,128)S(1)}, f32[64,1024]{1,0:T(8,128)S(1)}, b...) custom-call(bf16[64,1024]{1,0:T(8,128)(2,1)S(1)} %get-tuple-element.308.refs_0_, ...), custom_call_target="tpu_custom_call" | custom-call | flops 2000000000 | tf_op jit(solution)/shard_map/pallas_call | solution.py:98
  188.4 4.6 %shard_map.282 = (bf16[4,256,1024]{2,1,0:T(8,128)(2,1)}, bf16[4,256,1024]{2,1,0:T(8,128)(2,1)}) custom-call(bf16[256,1024]{1,0:T(8,128)(2,1)} %copy-done.14, bf16[256,1024]{1,0:T(8,128)(2,1)S(1)} %get-tuple-element.321.du, bf16[256,1024]{1,0:T(8,128)(2,1)} %copy-done.15, bf16[256,1024]{1,0:T(8,128)(2,1)S(1)} %get-tuple-element.323.e), custom_call_target="tpu_custom_call" | custom-call | flops 3000000000 | tf_op jit(solution)/shard_map/pallas_call | solution.py:98
  197.6 5.8 %collective-permute-done.49.refs_3_ = bf16[64,1024]{1,0:T(8,128)(2,1)S(1)} collective-permute-done((bf16[64,1024]{1,0:T(8,128)(2,1)}, bf16[64,1024]{1,0:T(8,128)(2,1)S(1)}, u32[]{:S(2)}, u32[]{:S(2)}) %collective-permute-start.49) | collective-permute-done | bytes 131104 | tf_op jit(solution)/shard_map/ppermute | solution.py:26
  219.9 6.4 %shard_map.284 = (bf16[256,1024]{1,0:T(8,128)(2,1)}, bf16[256,256]{1,0:T(8,128)(2,1)}, bf16[512,256]{1,0:T(8,128)(2,1)}, bf16[512,256]{1,0:T(8,128)(2,1)}, f32[6...) custom-call(bf16[64,1024]{1,0:T(8,128)(2,1)} %get-tuple-element.333.refs_0_, ...), custom_call_target="tpu_custom_call" | custom-call | flops 5000000000 | tf_op jit(solution)/shard_map/pallas_call | solution.py:98
  232.9 8.6 %shard_map.286.held_ref = f32[4096,1024]{1,0:T(8,128)} custom-call(f32[4,2,8,256]{3,2,1,0:T(8,128)S(1)} %get-tuple-element.404.rows_ref, bf16[4,256,1024]{2,1,0:T(8,128)(2,1)} %all-to-all-done.1.own_ref, bf16[4,256,1024]{2,1,0:T(8,128)(2,1)} %collective-permute-done.48.pair_ref, bf16[4096,1024]{1,0:T(8,128)(2,1)} %e_ref.11, ...), custom_call_target="tpu_custom_call", output_to_operand_aliasing={{}: (4, {})} | custom-call | flops 1500000000 | tf_op jit(solution)/shard_map/pallas_call | solution.py:576
  249.2 8.6 %shard_map.289.held_ref = f32[4096,1024]{1,0:T(8,128)} custom-call(f32[4,2,8,256]{3,2,1,0:T(8,128)S(1)} %get-tuple-element.404.rows_ref, bf16[4,256,1024]{2,1,0:T(8,128)(2,1)} %all-to-all-done.1.own_ref, bf16[4,256,1024]{2,1,0:T(8,128)(2,1)} %collective-permute-done.48.pair_ref, bf16[4096,1024]{1,0:T(8,128)(2,1)} %e_ref.11, ...), custom_call_target="tpu_custom_call", output_to_operand_aliasing={{}: (4, {})} | custom-call | flops 1500000000 | tf_op jit(solution)/shard_map/pallas_call | solution.py:576
  258.6 5.2 %shard_map.290 = (bf16[256,1024]{1,0:T(8,128)(2,1)}, bf16[256,768]{1,0:T(8,128)(2,1)}) custom-call(bf16[64,1024]{1,0:T(8,128)(2,1)} %get-tuple-element.364.refs_0_, bf16[64,1024]{1,0:T(8,128)(2,1)} %copy-done.55, bf16[64,1024]{1,0:T(8,128)(2,1)} %copy-done.53, bf16[64,1024]{1,0:T(8,128)(2,1)} %copy-done.51, bf16[2,256,1024]{2,1,0:T(8,128)(2,1)} %copy-done.11, ...), custom_call_target="tpu_custom_call" | custom-call | flops 4000000000 | tf_op jit(solution)/shard_map/pallas_call | solution.py:98
  263.8 5.1 %all-to-all-start.3 = ((bf16[4,512,256]{2,1,0:T(8,128)(2,1)}), bf16[4,512,256]{2,1,0:T(8,128)(2,1)S(1)}, u32[]{:S(2)}, u32[]{:S(2)}) async-start(bf16[4,512,256]{2,1,0:T(8,128)(2,1)} %shard_map.288), calls=%async_computation.3 | async-start | bytes 2097152 | tf_op jit(solution)/shard_map/all_to_all | solution.py:56
  272.4 5.6 %shard_map.293 = (f32[192,1024]{1,0:T(8,128)}, bf16[128,1024]{1,0:T(8,128)(2,1)}, bf16[224,1024]{1,0:T(8,128)(2,1)}, bf16[224,1024]{1,0:T(8,128)(2,1)}, bf16[224...) custom-call(bf16[256,768]{1,0:T(8,128)(2,1)} %get-tuple-element.378.d, bf16[1024,768]{1,0:T(8,128)(2,1)} %copy-done.9, ...), custom_call_target="tpu_custom_call" | custom-call | flops 3000000000 | tf_op jit(solution)/shard_map/pallas_call | solution.py:98
  281.9 8.6 %shard_map.295.held_ref = f32[4096,1024]{1,0:T(8,128)} custom-call(f32[4,2,8,256]{3,2,1,0:T(8,128)S(1)} %get-tuple-element.404.rows_ref, bf16[4,256,1024]{2,1,0:T(8,128)(2,1)} %all-to-all-done.1.own_ref, bf16[4,256,1024]{2,1,0:T(8,128)(2,1)} %collective-permute-done.48.pair_ref, bf16[4096,1024]{1,0:T(8,128)(2,1)} %e_ref.11, ...), custom_call_target="tpu_custom_call", output_to_operand_aliasing={{}: (4, {})} | custom-call | flops 1500000000 | tf_op jit(solution)/shard_map/pallas_call | solution.py:576
  298.1 4.4 %collective-permute-start.65 = (bf16[128,1024]{1,0:T(8,128)(2,1)S(1)}, bf16[128,1024]{1,0:T(8,128)(2,1)}, u32[]{:S(2)}, u32[]{:S(2)}) collective-permute-start(bf16[128,1024]{1,0:T(8,128)(2,1)S(1)} %copy-done.45), channel_id=1, source_target_pairs={{0,0},{1,1},{2,8},{3,9},{4,16},{5,17},{6,24},{7,25},{8,2},{9,3},{1... | collective-permute-start | bytes 786440 | tf_op jit(solution)/shard_map/ppermute | solution.py:1040
  307.3 25.3 %shard_map.296 = f32[4096,1024]{1,0:T(8,128)} custom-call(f32[4,2,8,256]{3,2,1,0:T(8,128)S(1)} %get-tuple-element.404.rows_ref, bf16[4,256,1024]{2,1,0:T(8,128)(2,1)} %all-to-all-done.1.own_ref, bf16[4,256,1024]{2,1,0:T(8,128)(2,1)} %collective-permute-done.48.pair_ref, bf16[4096,1024]{1,0:T(8,128)(2,1)} %e_ref.11, ...), custom_call_target="tpu_custom_call", output_to_operand_aliasing={{}: (4, {})} | custom-call | flops 7500000256 | tf_op jit(solution)/shard_map/pallas_call | solution.py:576
  338.0 6.5 %collective-permute-start.63 = (bf16[208,256]{1,0:T(8,128)(2,1)S(1)}, bf16[208,256]{1,0:T(8,128)(2,1)S(1)}, u32[]{:S(2)}, u32[]{:S(2)}) collective-permute-start(bf16[208,256]{1,0:T(8,128)(2,1)S(1)} %get-tuple-element.417), channel_id=1, source_target_pairs={{0,4},{1,5},{2,6},{3,7},{4,0},{5,1},{6,2},{7,3},{8,12},{9,13},{10,... | collective-permute-start | bytes 319496 | tf_op jit(solution)/shard_map/ppermute | solution.py:26
  (287 shorter events, 160.1 us)
Async XLA Ops:
  4.3 16.0 %collective-permute-start.2 = (bf16[1024,256]{1,0:T(8,128)(2,1)}, bf16[1024,256]{1,0:T(8,128)(2,1)S(1)}, u32[]{:S(2)}, u32[]{:S(2)}) collective-permute-start(bf16[1024,256]{1,0:T(8,128)(2,1)} %get-tuple-element.230), channel_id=1, source_target_pairs={{0,6},{1,7},{2,4},{3,5},{4,2},{5,3},{6,0},{7,1},{8,14},{9,15},{10,... | collective-permute-start | bytes 1572872 | tf_op jit(solution)/shard_map/ppermute | solution.py:26
  5.8 24.6 %collective-permute-start = (bf16[1024,256]{1,0:T(8,128)(2,1)}, bf16[1024,256]{1,0:T(8,128)(2,1)S(1)}, u32[]{:S(2)}, u32[]{:S(2)}) collective-permute-start(bf16[1024,256]{1,0:T(8,128)(2,1)} %get-tuple-element.227), channel_id=1, source_target_pairs={{0,2},{1,3},{2,0},{3,1},{4,6},{5,7},{6,4},{7,5},{8,10},{9,11},{10,... | collective-permute-start | bytes 1572872 | tf_op jit(solution)/shard_map/ppermute | solution.py:26
  7.3 23.1 %collective-permute-start.1 = (bf16[1024,256]{1,0:T(8,128)(2,1)}, bf16[1024,256]{1,0:T(8,128)(2,1)S(1)}, u32[]{:S(2)}, u32[]{:S(2)}) collective-permute-start(bf16[1024,256]{1,0:T(8,128)(2,1)} %get-tuple-element.229), channel_id=1, source_target_pairs={{0,4},{1,5},{2,6},{3,7},{4,0},{5,1},{6,2},{7,3},{8,12},{9,13},{10,... | collective-permute-start | bytes 1572872 | tf_op jit(solution)/shard_map/ppermute | solution.py:26
  7.9 24.0 %collective-permute-start.7 = (bf16[2,128,1024]{2,1,0:T(8,128)(2,1)S(1)}, bf16[2,128,1024]{2,1,0:T(8,128)(2,1)}, u32[]{:S(2)}, u32[]{:S(2)}) collective-permute-start(bf16[2,128,1024]{2,1,0:T(8,128)(2,1)S(1)} %bitcast.24), channel_id=1, source_target_pairs={{0,1},{1,0},{2,3},{3,2},{4,5},{5,4},{6,7},{7,6},{8,9},{9,8},{10,11... | collective-permute-start | bytes 1572872 | tf_op jit(solution)/shard_map/ppermute | solution.py:30
  8.0 24.5 %collective-permute-start.3 = (bf16[1024,256]{1,0:T(8,128)(2,1)S(1)}, bf16[1024,256]{1,0:T(8,128)(2,1)}, u32[]{:S(2)}, u32[]{:S(2)}) collective-permute-start(bf16[1024,256]{1,0:T(8,128)(2,1)S(1)} %get-tuple-element.226.refs_0_.refs_4_), channel_id=1, source_target_pairs={{0,1},{1,0},{2,3},{3,2},{4,5},{5,4},{6,7},{7,6},{8,9},{9,8},{10,11... | collective-permute-start | bytes 1572872 | tf_op jit(solution)/shard_map/ppermute | solution.py:30
  31.0 15.3 %collective-permute-start.9 = (bf16[128,1024]{1,0:T(8,128)(2,1)S(1)}, bf16[128,1024]{1,0:T(8,128)(2,1)S(1)}, u32[]{:S(2)}, u32[]{:S(2)}) collective-permute-start(bf16[128,1024]{1,0:T(8,128)(2,1)S(1)} %bitcast.29), channel_id=1, source_target_pairs={{0,4},{1,5},{2,6},{3,7},{4,0},{5,1},{6,2},{7,3},{8,12},{9,13},{10,... | collective-permute-start | bytes 786440 | tf_op jit(solution)/shard_map/ppermute | solution.py:26
  32.0 14.4 %collective-permute-start.8 = (bf16[128,1024]{1,0:T(8,128)(2,1)S(1)}, bf16[128,1024]{1,0:T(8,128)(2,1)S(1)}, u32[]{:S(2)}, u32[]{:S(2)}) collective-permute-start(bf16[128,1024]{1,0:T(8,128)(2,1)S(1)} %bitcast.30), channel_id=1, source_target_pairs={{0,2},{1,3},{2,0},{3,1},{4,6},{5,7},{6,4},{7,5},{8,10},{9,11},{10,... | collective-permute-start | bytes 786440 | tf_op jit(solution)/shard_map/ppermute | solution.py:26
  46.3 15.8 %collective-permute-start.16 = (bf16[128,1024]{1,0:T(8,128)(2,1)S(1)}, bf16[128,1024]{1,0:T(8,128)(2,1)S(1)}, u32[]{:S(2)}, u32[]{:S(2)}) collective-permute-start(bf16[128,1024]{1,0:T(8,128)(2,1)S(1)} %bitcast.31), channel_id=1, source_target_pairs={{0,6},{1,7},{2,4},{3,5},{4,2},{5,3},{6,0},{7,1},{8,14},{9,15},{10,... | collective-permute-start | bytes 786440 | tf_op jit(solution)/shard_map/ppermute | solution.py:26
  75.8 12.2 %collective-permute-start.22 = (bf16[128,1024]{1,0:T(8,128)(2,1)S(1)}, bf16[128,1024]{1,0:T(8,128)(2,1)S(1)}, u32[]{:S(2)}, u32[]{:S(2)}) collective-permute-start(bf16[128,1024]{1,0:T(8,128)(2,1)S(1)} %get-tuple-element.269), channel_id=1, source_target_pairs={{0,6},{1,7},{2,4},{3,5},{4,2},{5,3},{6,0},{7,1},{8,14},{9,15},{10,... | collective-permute-start | bytes 786440 | tf_op jit(solution)/shard_map/ppermute | solution.py:26
  140.6 53.9 %all-to-all-start.1 = ((bf16[4,256,1024]{2,1,0:T(8,128)(2,1)}), bf16[4,256,1024]{2,1,0:T(8,128)(2,1)}, u32[]{:S(2)}, u32[]{:S(2)}) async-start(bf16[4,256,1024]{2,1,0:T(8,128)(2,1)} %get-tuple-element.325), calls=%async_computation.1 | async-start | bytes 4194304 | tf_op jit(solution)/shard_map/all_to_all | solution.py:56
  208.9 54.9 %all-to-all-start.2 = ((bf16[4,256,1024]{2,1,0:T(8,128)(2,1)}), bf16[4,256,1024]{2,1,0:T(8,128)(2,1)S(1)}, u32[]{:S(2)}, u32[]{:S(2)}) async-start(bf16[4,256,1024]{2,1,0:T(8,128)(2,1)} %shard_map.291), calls=%async_computation.2 | async-start | bytes 4194304 | tf_op jit(solution)/shard_map/all_to_all | solution.py:56
  229.2 18.8 %collective-permute-start.50 = (bf16[4,512,256]{2,1,0:T(8,128)(2,1)S(1)}, bf16[4,512,256]{2,1,0:T(8,128)(2,1)S(1)}, u32[]{:S(2)}, u32[]{:S(2)}) collective-permute-start(bf16[4,512,256]{2,1,0:T(8,128)(2,1)S(1)} %get-tuple-element.348), channel_id=1, source_target_pairs={{0,1},{1,0},{2,3},{3,2},{4,5},{5,4},{6,7},{7,6},{8,9},{9,8},{10,11... | collective-permute-start | bytes 3145736 | tf_op jit(solution)/shard_map/ppermute | solution.py:30
  229.3 12.2 %collective-permute-start.51 = (bf16[64,1024]{1,0:T(8,128)(2,1)S(1)}, bf16[64,1024]{1,0:T(8,128)(2,1)S(1)}, u32[]{:S(2)}, u32[]{:S(2)}) collective-permute-start(bf16[64,1024]{1,0:T(8,128)(2,1)S(1)} %copy-done.47), channel_id=1, source_target_pairs={{0,2},{1,3},{2,0},{3,1},{4,6},{5,7},{6,4},{7,5},{8,10},{9,11},{10,... | collective-permute-start | bytes 393224 | tf_op jit(solution)/shard_map/ppermute | solution.py:26
  230.2 11.3 %collective-permute-start.52 = (bf16[64,1024]{1,0:T(8,128)(2,1)S(1)}, bf16[64,1024]{1,0:T(8,128)(2,1)S(1)}, u32[]{:S(2)}, u32[]{:S(2)}) collective-permute-start(bf16[64,1024]{1,0:T(8,128)(2,1)S(1)} %copy-done.50), channel_id=1, source_target_pairs={{0,4},{1,5},{2,6},{3,7},{4,0},{5,1},{6,2},{7,3},{8,12},{9,13},{10,... | collective-permute-start | bytes 393224 | tf_op jit(solution)/shard_map/ppermute | solution.py:26
  244.5 13.3 %collective-permute-start.56 = (bf16[64,1024]{1,0:T(8,128)(2,1)}, bf16[64,1024]{1,0:T(8,128)(2,1)S(1)}, u32[]{:S(2)}, u32[]{:S(2)}) collective-permute-start(bf16[64,1024]{1,0:T(8,128)(2,1)} %get-tuple-element.364.refs_0_), channel_id=1, source_target_pairs={{0,6},{1,7},{2,4},{3,5},{4,2},{5,3},{6,0},{7,1},{8,14},{9,15},{10,... | collective-permute-start | bytes 393224 | tf_op jit(solution)/shard_map/ppermute | solution.py:26
  245.9 11.9 %collective-permute-start.55 = (bf16[64,1024]{1,0:T(8,128)(2,1)}, bf16[64,1024]{1,0:T(8,128)(2,1)S(1)}, u32[]{:S(2)}, u32[]{:S(2)}) collective-permute-start(bf16[64,1024]{1,0:T(8,128)(2,1)} %get-tuple-element.364.refs_0_), channel_id=1, source_target_pairs={{0,4},{1,5},{2,6},{3,7},{4,0},{5,1},{6,2},{7,3},{8,12},{9,13},{10,... | collective-permute-start | bytes 393224 | tf_op jit(solution)/shard_map/ppermute | solution.py:26
  263.8 29.8 %all-to-all-start.3 = ((bf16[4,512,256]{2,1,0:T(8,128)(2,1)}), bf16[4,512,256]{2,1,0:T(8,128)(2,1)S(1)}, u32[]{:S(2)}, u32[]{:S(2)}) async-start(bf16[4,512,256]{2,1,0:T(8,128)(2,1)} %shard_map.288), calls=%async_computation.3 | async-start | bytes 2097152 | tf_op jit(solution)/shard_map/all_to_all | solution.py:56
  294.6 38.1 %all-to-all-start.4 = ((bf16[4,544,256]{2,1,0:T(8,128)(2,1)}), bf16[4,544,256]{2,1,0:T(8,128)(2,1)S(1)}, u32[]{:S(2)}, u32[]{:S(2)}) async-start(bf16[4,544,256]{2,1,0:T(8,128)(2,1)} %shard_map.294), calls=%async_computation.4 | async-start | bytes 2228224 | tf_op jit(solution)/shard_map/all_to_all | solution.py:56
  298.1 52.0 %collective-permute-start.65 = (bf16[128,1024]{1,0:T(8,128)(2,1)S(1)}, bf16[128,1024]{1,0:T(8,128)(2,1)}, u32[]{:S(2)}, u32[]{:S(2)}) collective-permute-start(bf16[128,1024]{1,0:T(8,128)(2,1)S(1)} %copy-done.45), channel_id=1, source_target_pairs={{0,0},{1,1},{2,8},{3,9},{4,16},{5,17},{6,24},{7,25},{8,2},{9,3},{1... | collective-permute-start | bytes 786440 | tf_op jit(solution)/shard_map/ppermute | solution.py:1040
  302.5 30.1 %collective-permute-start.58 = (bf16[224,1024]{1,0:T(8,128)(2,1)}, bf16[224,1024]{1,0:T(8,128)(2,1)S(1)}, u32[]{:S(2)}, u32[]{:S(2)}) collective-permute-start(bf16[224,1024]{1,0:T(8,128)(2,1)} %get-tuple-element.400), channel_id=1, source_target_pairs={{0,2},{1,3},{2,0},{3,1},{4,6},{5,7},{6,4},{7,5},{8,10},{9,11},{10,... | collective-permute-start | bytes 1376264 | tf_op jit(solution)/shard_map/ppermute | solution.py:26
  302.6 30.0 %collective-permute-start.59 = (bf16[224,1024]{1,0:T(8,128)(2,1)}, bf16[224,1024]{1,0:T(8,128)(2,1)S(1)}, u32[]{:S(2)}, u32[]{:S(2)}) collective-permute-start(bf16[224,1024]{1,0:T(8,128)(2,1)} %get-tuple-element.401), channel_id=1, source_target_pairs={{0,4},{1,5},{2,6},{3,7},{4,0},{5,1},{6,2},{7,3},{8,12},{9,13},{10,... | collective-permute-start | bytes 1376264 | tf_op jit(solution)/shard_map/ppermute | solution.py:26
  305.9 26.7 %collective-permute-start.60 = (bf16[224,1024]{1,0:T(8,128)(2,1)S(1)}, bf16[224,1024]{1,0:T(8,128)(2,1)S(1)}, u32[]{:S(2)}, u32[]{:S(2)}) collective-permute-start(bf16[224,1024]{1,0:T(8,128)(2,1)S(1)} %copy-done.43), channel_id=1, source_target_pairs={{0,6},{1,7},{2,4},{3,5},{4,2},{5,3},{6,0},{7,1},{8,14},{9,15},{10,... | collective-permute-start | bytes 1376264 | tf_op jit(solution)/shard_map/ppermute | solution.py:26
  335.6 14.5 %collective-permute-start.61 = (bf16[272,256]{1,0:T(8,128)(2,1)S(1)}, bf16[272,256]{1,0:T(8,128)(2,1)S(1)}, u32[]{:S(2)}, u32[]{:S(2)}) collective-permute-start(bf16[272,256]{1,0:T(8,128)(2,1)S(1)} %get-tuple-element.408), channel_id=1, source_target_pairs={{0,0},{1,1},{2,8},{3,9},{4,16},{5,17},{6,24},{7,25},{8,2},{9,3},{1... | collective-permute-start | bytes 417800 | tf_op jit(solution)/shard_map/ppermute | solution.py:1040
  338.0 11.9 %collective-permute-start.63 = (bf16[208,256]{1,0:T(8,128)(2,1)S(1)}, bf16[208,256]{1,0:T(8,128)(2,1)S(1)}, u32[]{:S(2)}, u32[]{:S(2)}) collective-permute-start(bf16[208,256]{1,0:T(8,128)(2,1)S(1)} %get-tuple-element.417), channel_id=1, source_target_pairs={{0,4},{1,5},{2,6},{3,7},{4,0},{5,1},{6,2},{7,3},{8,12},{9,13},{10,... | collective-permute-start | bytes 319496 | tf_op jit(solution)/shard_map/ppermute | solution.py:26
  (106 other events, 934.3 us)

commit v2 on v1

--- a/solution.py
+++ b/solution.py
@@ -338,7 +338,7 @@
             spread_out[slot, k * n : (k + 1) * n, :] = part[...]
 
 
-def logits_kernel(length, h0_ref, h1_ref, ids_ref, own_ref, e_ref, l_ref, pay_ref, h_ref, m_ref, s_ref, p_ref):
+def logits_kernel(length, h0_ref, h1_ref, ids_ref, e_ref, l_ref, pay_ref, h_ref, m_ref, s_ref, p_ref):
     i = pl.program_id(0)
     half = h0_ref.shape[0]
 
@@ -361,7 +361,6 @@
     @pl.when(i == pl.num_programs(0) - 1)
     def _():
         pay_ref[...] = jnp.zeros_like(pay_ref)
-        pay_ref[pay_ref.shape[0] - 8 : pay_ref.shape[0] - 7, :] = own_ref[...]
         norm = peak + jnp.log(total)
         lane = lax.broadcasted_iota(jnp.int32, (1, 2 * length), 1)
         chip, core = place()
@@ -379,7 +378,7 @@
                 pay_ref[pl.ds(q, 1), :] = rows[j]
 
 
-def logits(held, pair, ids, own_row, embedding, length, questions):
+def logits(held, pair, ids, embedding, length, questions):
     half, vocab, width = held.shape[0], embedding.shape[0], embedding.shape[1]
     tile = min(2 * VOCAB_TILE, vocab)
     stat = pltpu.VMEM((8, 2 * half), F32)
@@ -387,22 +386,22 @@
     return pl.pallas_call(
         functools.partial(logits_kernel, length),
         grid=(vocab // tile,),
-        in_specs=[whole, whole, whole, whole, pl.BlockSpec((tile, width), lambda i: (i, 0))],
+        in_specs=[whole, whole, whole, pl.BlockSpec((tile, width), lambda i: (i, 0))],
         out_specs=[
             pl.BlockSpec((tile, 2 * half), lambda i: (i, 0)),
-            pl.BlockSpec((questions + 8, 2 * length), lambda i: (0, 0)),
+            pl.BlockSpec((questions, 2 * length), lambda i: (0, 0)),
         ],
         out_shape=[
             pltpu.HBM((vocab, 2 * half), F32),
-            jax.ShapeDtypeStruct((questions + 8, 2 * length), F32),
+            jax.ShapeDtypeStruct((questions, 2 * length), F32),
         ],
         scratch_shapes=[pltpu.VMEM((2 * half, width), BF), stat, stat, stat],
         compiler_params=limit(14 + 24 * half * tile // MIB),
         cost_estimate=work(10),
-    )(held, pair, ids, own_row, embedding)
-
-
-def merge_kernel(length, all_ref, counts_ref, ids_ref, rows_out, own_out, logp_out, prior_out, n_ref, g_ref):
+    )(held, pair, ids, embedding)
+
+
+def merge_kernel(length, all_ref, info_ref, counts_ref, ids_ref, rows_out, own_out, logp_out, prior_out, n_ref, g_ref):
     n_slot, n_pb = n_ref.shape[0], n_ref.shape[1]
     chip, core = place()
     me, slot = lax.axis_index("pb"), lax.axis_index("slot")
@@ -420,7 +419,7 @@
             pick = pick + b
         norm = peak + jnp.log(total)
         n_ref[s] = norm
-        own = jnp.concatenate([all_ref[s * n_pb + j, n_pb : n_pb + 1, :] for j in range(n_pb)], axis=0)
+        own = info_ref[s * n_pb : (s + 1) * n_pb, :]
         mask = own
         prior = pltpu.roll(own, length, 1)
         logp = pltpu.roll(pick, length, 1) - norm + prior
@@ -458,7 +457,7 @@
     own_out[0] = rows_out[slot]
 
 
-def merge(everyone, counts, ids, length, n_slot, n_pb, half):
+def merge(everyone, info, counts, ids, length, n_slot, n_pb, half):
     held = pltpu.VMEM((n_slot, n_pb, 2 * length), F32)
     return pl.pallas_call(
         functools.partial(merge_kernel, length),
@@ -471,7 +470,7 @@
         scratch_shapes=[held, held],
         compiler_params=limit(16 + 2 * everyone.size * 4 // MIB),
         cost_estimate=work(2),
-    )(everyone, counts, ids)
+    )(everyone, info, counts, ids)
 
 
 def logit_gradient(x, rows, first):
@@ -683,15 +682,12 @@
     g = dot(e, w_mine[1], NT).astype(BF)
     g_ref[...] = g
 
-    def pair(i, carry):
-        for j in range(2):
-            s, t = rows_at((2 * i + j) * length, length, 16), rows_at((2 * i + j) * memory, memory, 16)
-            dq_out[s, :], dk_out[t, :], dv_out[t, :] = attend_back(
-                g_ref[s, :], q_ref[s, :], k_ref[t, :], v_ref[t, :], False
-            )
+    def question(i, carry):
+        s, t = rows_at(i * length, length, 16), rows_at(i * memory, memory, 16)
+        dq_out[s, :], dk_out[t, :], dv_out[t, :] = attend_back(g_ref[s, :], q_ref[s, :], k_ref[t, :], v_ref[t, :], False)
         return carry
 
-    lax.fori_loop(0, CHIPS // 2, pair, 0)
+    lax.fori_loop(0, CHIPS, question, 0)
     split_rows(dot(dq_out[...], w_cols[:, :quarter], NT), mine_out, send)
 
 
@@ -891,6 +887,9 @@
     )
     ids = (targets - me * vocab_rows).astype(jnp.int32)
     own_row = jnp.concatenate([pad_mask.astype(F32), jnp.broadcast_to(log_prior, (1, length))], axis=1)
+    own_rows_all = lax.all_to_all(
+        jnp.broadcast_to(own_row[None], (n_all,) + own_row.shape), ("slot", "pb"), 0, 0, tiled=True
+    ).reshape(n_all, 2 * length)
 
     block = (length, width)
     every = (CHIPS * length, width)
@@ -908,7 +907,8 @@
 
     first = call(functools.partial(pack_kernel, 6, 0), [((CHIPS * length + 6 * rows, quarter), BF)] * CHIPS, x, attn_w)
     got_first = [first[0]] + give(first[1:])
-    got_first[1], vec = tie(got_first[1], vec)
+    got_first[3], vec = tie(got_first[3], vec)
+    got_first[1], own_rows_all = tie(got_first[1], own_rows_all)
     pair_first = [from_core(g) for g in got_first]
     out_pair = from_core(out_w)
     down_pair = from_core(down_w)
@@ -922,34 +922,33 @@
         + sends,
         *got_first, *pair_first, out_w, out_pair, vec,
     )
+    got_memory[1], send[0] = tie(got_memory[1], send[0])
     got = give(send)
-    got_memory[1], got_memory[2], *got = tie(got_memory[1], got_memory[2], *got)
+    got_memory.append(from_chip(got_memory[1], 2))
+    *got_memory, got[0], got[1], got[2] = tie(*got_memory, *got)
     norm_outs = [(block, F32), (block, BF), (block, F32), ((length, 1), F32)]
     hidden_one, low_one, z_one, inv_one = call(
         functools.partial(norm_kernel, (2, 6, 9)), norm_outs, x, mine, *got, vec, us=1
     )
     got_low = [low_one] + others(low_one)
-    m_send, got_memory[1] = tie(m, got_memory[1])
-    got_memory.append(from_chip(m_send, 3))
+    got_third = [third[0], from_chip(third[1], 1), from_chip(third[2], 2)]
     m_all, w_cross, cross_keys, cross_values = call(
         memory_kernel, [((CHIPS * passage, width), BF), ((width, 3 * quarter), BF)] + [(m_cols, BF)] * 2,
         *got_memory, *got_first, *pair_first, vec,
     )
-    third[1], third[2], *got_low = tie(third[1], third[2], *got_low)
-    got_third = [third[0], from_chip(third[1], 1), from_chip(third[2], 2)]
+    got_third[1], got_third[2], *got_low = tie(got_third[1], got_third[2], *got_low)
     low_one_all, cross_queries, cross_mixed, mine, *send = call(
         cross_kernel, [(every, BF), (cols, BF), (cols, BF), (block, F32)] + sends,
         *got_low, w_out, w_cross, cross_keys, cross_values, vec,
     )
     got = give(send)
-    got_third[1], got_third[2], *got = tie(got_third[1], got_third[2], *got)
+    third[3], got_third[1] = tie(third[3], got_third[1])
+    got_third.append(from_chip(third[3], 3))
+    got_third[3], *got = tie(got_third[3], *got)
     hidden_two, low_two, z_two, inv_two = call(
         functools.partial(norm_kernel, (5, 7, 10)), norm_outs, hidden_one, mine, *got, vec, us=1
     )
     got_low = [low_two] + others(low_two)
-    third[3], got_third[1] = tie(third[3], got_third[1])
-    got_third.append(from_chip(third[3], 3))
-    got_third[3], *got_low = tie(got_third[3], *got_low)
     (up_half,) = call(up_half_kernel, [((CHIPS, rows, ff), BF)], *got_third)
     up_half_pair = from_core(up_half)
     low_two_all, upward, active, w_up, w_down, mine, *send = call(
@@ -979,7 +978,7 @@
     ]
     ids_row = jnp.concatenate([lax.dynamic_slice_in_dim(ids, q, 1) for q in order], axis=1)
     states = [all_teams(held), all_teams(pair)]
-    scores, payload = logits(*states, ids_row, own_row, embedding, length, n_pb)
+    scores, payload = logits(*states, ids_row, embedding, length, n_pb)
     everyone = lax.all_to_all(
         jnp.broadcast_to(payload[None], (n_all,) + payload.shape), ("slot", "pb"), 0, 0, tiled=True
     )
@@ -987,7 +986,7 @@
     spread_held, everyone = tie(spread_held, everyone)
     all_held = across_slots(spread_held)
     token_rows, own_rows, token_logprob, prior_grad = merge(
-        everyone, slot_counts.astype(jnp.int32)[:, None], ids_wide, length, n_slot, n_pb, half
+        everyone, own_rows_all, slot_counts.astype(jnp.int32)[:, None], ids_wide, length, n_slot, n_pb, half
     )
     def home(partial):
         if teams == 1:

time: 358 us -> 354 us (0.989)
  waiting for transfers between devices: 80.1 us -> 68.9 us
  starting transfers between devices: 90.6 us -> 96.8 us
  local copies, waits for them, and re-layouts: 11.2 us -> 16.4 us
  blocking collectives: 14.4 us -> 9.81 us
    ppermute x51, waiting for transfers between devices: 70.4 us -> 57.4 us  [from_chip(): return lax.ppermute(x, 'pb', pairs)]
    all_to_all x0 -> x1, starting transfers between devices: none -> 6.24 us  [shards(): lax.all_to_all(jnp.broadcast_to(own_row[None], (n_all,) + own_row.shape),...]
    all_to_all x1, blocking collectives: 14.4 us -> 9.81 us  [shards(): lax.all_to_all(jnp.broadcast_to(payload[None], (n_all,) + payload.shape),...]
    unnamed x122 -> x120, local copies, waits for them, and re-layouts: 10.7 us -> 15.3 us
    all_to_all x0 -> x1, waiting for transfers between devices: none -> 4.1 us  [shards(): lax.all_to_all(jnp.broadcast_to(own_row[None], (n_all,) + own_row.shape),...]
  transfers between devices with their start and end apart: 70 -> 71, of which waited for: 26 -> 26; matrix products, arithmetic and copies ran while one was open for 0% -> 1% of each run, Pallas kernels for 37% -> 38%
where the time goes in v2:
time: 354 us; the launch traced here: 349 us
  Pallas kernels  155 us (44%)
  starting transfers between devices  96.8 us (27%)
  waiting for transfers between devices  68.9 us (19%)
  local copies, waits for them, and re-layouts  16.4 us (5%)
  blocking collectives  9.81 us (3%)
    pallas_call x29, Pallas kernels, call(): pl.pallas_call(kernel, out_shape=places, scratch_shapes=scratch, compiler...  68.9 us
    ppermute x51, starting transfers between devices, from_chip(): return lax.ppermute(x, 'pb', pairs)  64.2 us
    ppermute x51, waiting for transfers between devices, from_chip(): return lax.ppermute(x, 'pb', pairs)  57.4 us
    pallas_call x4, Pallas kernels, embedding_piece(): pl.pallas_call(functools.partial(embedding_kernel, first), grid=(steps,),...  51.1 us
    all_to_all x4, starting transfers between devices, across_slots(): return lax.all_to_all(x, 'slot', 0, 0, tiled=True)  17.7 us
    unnamed x120, local copies, waits for them, and re-layouts  15.3 us
    pallas_call x2, Pallas kernels, own_embedding(): pl.pallas_call(own_embedding_kernel, grid=(steps,), in_specs=[pl.BlockSpe...  12.9 us
    pallas_call x1, Pallas kernels, state_grad(): pl.pallas_call(state_grad_kernel, grid=(vocab // tile,), in_specs=[pl.Blo...  11 us
  transfers between devices with their start and end apart: 71, of which 26 were waited for; matrix products, arithmetic and copies ran while one was open for 1% of the time, Pallas kernels for 38%

profile of v2, /device:TPU:2, one launch (start us, length us, event | category | flops | bytes accessed | tf_op | source)
XLA Modules:
  0.0 349.4 jit_solution(4394248350035978125)
XLA Ops:
  8.7 11.3 %collective-permute-done.2.refs_3_.refs_7_ = bf16[1024,256]{1,0:T(8,128)(2,1)S(1)} collective-permute-done((bf16[1024,256]{1,0:T(8,128)(2,1)S(1)}, bf16[1024,256]{1,0:T(8,128)(2,1)S(1)}, u32[]{:S(2)}, u32[]{:S(2)}) %collective-permute-start.2) | collective-permute-done | bytes 524320 | tf_op jit(solution)/shard_map/ppermute | solution.py:26
  20.6 6.2 %all-to-all-start = ((f32[32,1,128]{2,1,0:T(1,128)}), f32[32,1,128]{2,1,0:T(1,128)S(1)}, u32[]{:S(2)}, u32[]{:S(2)}) async-start(f32[32,1,128]{2,1,0:T(1,128)} %broadcast_in_dim.36), calls=%async_computation | async-start | bytes 32768 | tf_op jit(solution)/shard_map/all_to_all | solution.py:890
  35.3 4.1 %shard_map.264 = (bf16[256,1024]{1,0:T(8,128)(2,1)S(1)}, bf16[1024,768]{1,0:T(8,128)(2,1)S(1)}, bf16[256,256]{1,0:T(8,128)(2,1)S(1)}, bf16[256,256]{1,0:T(8,128)...) custom-call(bf16[1024,256]{1,0:T(8,128)(2,1)S(1)} %get-tuple-element, ...), custom_call_target="tpu_custom_call" | custom-call | flops 2000000000 | tf_op jit(solution)/shard_map/pallas_call | solution.py:98
  45.8 8.9 %collective-permute-done.12.refs_3_ = bf16[64,1024]{1,0:T(8,128)(2,1)S(1)} collective-permute-done((bf16[64,1024]{1,0:T(8,128)(2,1)S(1)}, bf16[64,1024]{1,0:T(8,128)(2,1)S(1)}, u32[]{:S(2)}, u32[]{:S(2)}) %collective-permute-start.12) | collective-permute-done | bytes 131104 | tf_op jit(solution)/shard_map/ppermute | solution.py:26
  115.3 10.7 %shard_map.274 = (f32[4096,512]{1,0:T(8,128)}, f32[8,128]{1,0:T(8,128)S(1)}) custom-call(bf16[256,1024]{1,0:T(8,128)(2,1)S(1)} %get-tuple-element.280.h0_ref.own_ref, bf16[256,1024]{1,0:T(8,128)(2,1)S(1)} %collective-permute-done.34.h1_ref.pair_ref, s32[1,512]{1,0:T(1,128)S(1)} %concatenate.11.ids_ref, bf16[4096,1024]{1,0:T(8,128)(2,1)} %e_ref.11), custom_call_target="tpu_custom_call" | custom-call | flops 10000000000 | tf_op jit(solution)/shard_map/pallas_call | solution.py:386
  126.0 9.8 %all_to_all.30.all_ref = f32[32,8,128]{2,1,0:T(8,128)S(1)} all-to-all(f32[32,8,128]{2,1,0:T(8,128)S(1)} %broadcast_in_dim.39), channel_id=1, replica_groups=mesh['slot'=4,'pb'=8] {'slot','pb'}, dimensions={0} | all-to-all | bytes 262144 | tf_op jit(solution)/shard_map/all_to_all | solution.py:982
  135.8 4.8 %all-to-all-start.2 = ((bf16[4,256,1024]{2,1,0:T(8,128)(2,1)}), bf16[4,256,1024]{2,1,0:T(8,128)(2,1)}, u32[]{:S(2)}, u32[]{:S(2)}) async-start(bf16[4,256,1024]{2,1,0:T(8,128)(2,1)} %get-tuple-element.321), calls=%async_computation.2 | async-start | bytes 4194304 | tf_op jit(solution)/shard_map/all_to_all | solution.py:56
  141.4 11.0 %shard_map.276 = (f32[256,1024]{1,0:T(8,128)S(1)}, bf16[256,1024]{1,0:T(8,128)(2,1)S(1)}, bf16[4096,512]{1,0:T(8,128)(2,1)}) custom-call(f32[4096,512]{1,0:T(8,128)} %get-tuple-element.287.l_ref, f32[1,2,8,256]{3,2,1,0:T(8,128)S(1)} %get-tuple-element.288.rows_ref, bf16[4096,1024]{1,0:T(8,128)(2,1)} %e_ref.11), custom_call_target="tpu_custom_call" | custom-call | flops 11000000512 | tf_op jit(solution)/shard_map/pallas_call | solution.py:507
  158.0 6.4 %shard_map.278.refs_0_ = f32[4096,1024]{1,0:T(8,128)} custom-call(bf16[4096,512]{1,0:T(8,128)(2,1)} %get-tuple-element.305.d_ref, bf16[256,1024]{1,0:T(8,128)(2,1)S(1)} %get-tuple-element.280.h0_ref.own_ref, bf16[256,1024]{1,0:T(8,128)(2,1)S(1)} %collective-permute-done.34.h1_ref.pair_ref), custom_call_target="tpu_custom_call" | custom-call | flops 1000000000 | tf_op jit(solution)/shard_map/pallas_call | solution.py:539
  169.3 6.5 %shard_map.280.held_ref = f32[4096,1024]{1,0:T(8,128)} custom-call(bf16[4096,512]{1,0:T(8,128)(2,1)} %get-tuple-element.305.d_ref, bf16[256,1024]{1,0:T(8,128)(2,1)S(1)} %get-tuple-element.280.h0_ref.own_ref, bf16[256,1024]{1,0:T(8,128)(2,1)S(1)} %collective-permute-done.34.h1_ref.pair_ref, ...), custom_call_target="tpu_custom_call", output_to_operand_aliasing={{}: (3, {})} | custom-call | flops 1000000000 | tf_op jit(solution)/shard_map/pallas_call | solution.py:539
  175.7 4.2 %shard_map.281 = (bf16[256,1024]{1,0:T(8,128)(2,1)S(1)}, bf16[256,1024]{1,0:T(8,128)(2,1)S(1)}, f32[1,1024]{1,0:T(1,128)S(1)}, f32[64,1024]{1,0:T(8,128)S(1)}, b...) custom-call(bf16[64,1024]{1,0:T(8,128)(2,1)S(1)} %get-tuple-element.304.refs_0_, ...), custom_call_target="tpu_custom_call" | custom-call | flops 2000000000 | tf_op jit(solution)/shard_map/pallas_call | solution.py:98
  183.5 4.6 %shard_map.282 = (bf16[4,256,1024]{2,1,0:T(8,128)(2,1)}, bf16[4,256,1024]{2,1,0:T(8,128)(2,1)}) custom-call(bf16[256,1024]{1,0:T(8,128)(2,1)} %copy-done.14, bf16[256,1024]{1,0:T(8,128)(2,1)S(1)} %get-tuple-element.317.du, bf16[256,1024]{1,0:T(8,128)(2,1)} %copy-done.15, bf16[256,1024]{1,0:T(8,128)(2,1)S(1)} %get-tuple-element.319.e), custom_call_target="tpu_custom_call" | custom-call | flops 3000000000 | tf_op jit(solution)/shard_map/pallas_call | solution.py:98
  193.2 5.1 %collective-permute-done.49.refs_3_ = bf16[64,1024]{1,0:T(8,128)(2,1)S(1)} collective-permute-done((bf16[64,1024]{1,0:T(8,128)(2,1)}, bf16[64,1024]{1,0:T(8,128)(2,1)S(1)}, u32[]{:S(2)}, u32[]{:S(2)}) %collective-permute-start.49) | collective-permute-done | bytes 131104 | tf_op jit(solution)/shard_map/ppermute | solution.py:26
  203.8 4.4 %all-to-all-start.3 = ((bf16[4,256,1024]{2,1,0:T(8,128)(2,1)}), bf16[4,256,1024]{2,1,0:T(8,128)(2,1)S(1)}, u32[]{:S(2)}, u32[]{:S(2)}) async-start(bf16[4,256,1024]{2,1,0:T(8,128)(2,1)} %shard_map.291), calls=%async_computation.3 | async-start | bytes 4194304 | tf_op jit(solution)/shard_map/all_to_all | solution.py:56
  214.9 6.8 %shard_map.284 = (bf16[256,1024]{1,0:T(8,128)(2,1)}, bf16[256,256]{1,0:T(8,128)(2,1)}, bf16[512,256]{1,0:T(8,128)(2,1)}, bf16[512,256]{1,0:T(8,128)(2,1)}, f32[6...) custom-call(bf16[64,1024]{1,0:T(8,128)(2,1)} %get-tuple-element.329.refs_0_, ...), custom_call_target="tpu_custom_call" | custom-call | flops 5000000000 | tf_op jit(solution)/shard_map/pallas_call | solution.py:98
  228.3 8.6 %shard_map.286.held_ref = f32[4096,1024]{1,0:T(8,128)} custom-call(f32[4,2,8,256]{3,2,1,0:T(8,128)S(1)} %get-tuple-element.400.rows_ref, bf16[4,256,1024]{2,1,0:T(8,128)(2,1)} %all-to-all-done.2.own_ref, bf16[4,256,1024]{2,1,0:T(8,128)(2,1)} %collective-permute-done.48.pair_ref, bf16[4096,1024]{1,0:T(8,128)(2,1)} %e_ref.11, ...), custom_call_target="tpu_custom_call", output_to_operand_aliasing={{}: (4, {})} | custom-call | flops 1500000000 | tf_op jit(solution)/shard_map/pallas_call | solution.py:575
  244.6 8.6 %shard_map.289.held_ref = f32[4096,1024]{1,0:T(8,128)} custom-call(f32[4,2,8,256]{3,2,1,0:T(8,128)S(1)} %get-tuple-element.400.rows_ref, bf16[4,256,1024]{2,1,0:T(8,128)(2,1)} %all-to-all-done.2.own_ref, bf16[4,256,1024]{2,1,0:T(8,128)(2,1)} %collective-permute-done.48.pair_ref, bf16[4096,1024]{1,0:T(8,128)(2,1)} %e_ref.11, ...), custom_call_target="tpu_custom_call", output_to_operand_aliasing={{}: (4, {})} | custom-call | flops 1500000000 | tf_op jit(solution)/shard_map/pallas_call | solution.py:575
  254.0 5.2 %shard_map.290 = (bf16[256,1024]{1,0:T(8,128)(2,1)}, bf16[256,768]{1,0:T(8,128)(2,1)}) custom-call(bf16[64,1024]{1,0:T(8,128)(2,1)} %get-tuple-element.360.refs_0_, bf16[64,1024]{1,0:T(8,128)(2,1)} %copy-done.54, bf16[64,1024]{1,0:T(8,128)(2,1)} %copy-done.52, bf16[64,1024]{1,0:T(8,128)(2,1)} %copy-done.50, bf16[2,256,1024]{2,1,0:T(8,128)(2,1)} %copy-done.11, ...), custom_call_target="tpu_custom_call" | custom-call | flops 4000000000 | tf_op jit(solution)/shard_map/pallas_call | solution.py:98
  259.2 5.1 %all-to-all-start.4 = ((bf16[4,512,256]{2,1,0:T(8,128)(2,1)}), bf16[4,512,256]{2,1,0:T(8,128)(2,1)S(1)}, u32[]{:S(2)}, u32[]{:S(2)}) async-start(bf16[4,512,256]{2,1,0:T(8,128)(2,1)} %shard_map.288), calls=%async_computation.4 | async-start | bytes 2097152 | tf_op jit(solution)/shard_map/all_to_all | solution.py:56
  267.8 5.6 %shard_map.293 = (f32[192,1024]{1,0:T(8,128)}, bf16[128,1024]{1,0:T(8,128)(2,1)}, bf16[224,1024]{1,0:T(8,128)(2,1)}, bf16[224,1024]{1,0:T(8,128)(2,1)}, bf16[224...) custom-call(bf16[256,768]{1,0:T(8,128)(2,1)} %get-tuple-element.374.d, bf16[1024,768]{1,0:T(8,128)(2,1)} %copy-done.9, ...), custom_call_target="tpu_custom_call" | custom-call | flops 3000000000 | tf_op jit(solution)/shard_map/pallas_call | solution.py:98
  277.3 8.6 %shard_map.295.held_ref = f32[4096,1024]{1,0:T(8,128)} custom-call(f32[4,2,8,256]{3,2,1,0:T(8,128)S(1)} %get-tuple-element.400.rows_ref, bf16[4,256,1024]{2,1,0:T(8,128)(2,1)} %all-to-all-done.2.own_ref, bf16[4,256,1024]{2,1,0:T(8,128)(2,1)} %collective-permute-done.48.pair_ref, bf16[4096,1024]{1,0:T(8,128)(2,1)} %e_ref.11, ...), custom_call_target="tpu_custom_call", output_to_operand_aliasing={{}: (4, {})} | custom-call | flops 1500000000 | tf_op jit(solution)/shard_map/pallas_call | solution.py:575
  293.5 4.3 %collective-permute-start.65 = (bf16[128,1024]{1,0:T(8,128)(2,1)S(1)}, bf16[128,1024]{1,0:T(8,128)(2,1)}, u32[]{:S(2)}, u32[]{:S(2)}) collective-permute-start(bf16[128,1024]{1,0:T(8,128)(2,1)S(1)} %copy-done.44), channel_id=1, source_target_pairs={{0,0},{1,1},{2,8},{3,9},{4,16},{5,17},{6,24},{7,25},{8,2},{9,3},{1... | collective-permute-start | bytes 786440 | tf_op jit(solution)/shard_map/ppermute | solution.py:1039
  302.6 25.3 %shard_map.296 = f32[4096,1024]{1,0:T(8,128)} custom-call(f32[4,2,8,256]{3,2,1,0:T(8,128)S(1)} %get-tuple-element.400.rows_ref, bf16[4,256,1024]{2,1,0:T(8,128)(2,1)} %all-to-all-done.2.own_ref, bf16[4,256,1024]{2,1,0:T(8,128)(2,1)} %collective-permute-done.48.pair_ref, bf16[4096,1024]{1,0:T(8,128)(2,1)} %e_ref.11, ...), custom_call_target="tpu_custom_call", output_to_operand_aliasing={{}: (4, {})} | custom-call | flops 7500000256 | tf_op jit(solution)/shard_map/pallas_call | solution.py:575
  333.3 6.6 %collective-permute-start.63 = (bf16[208,256]{1,0:T(8,128)(2,1)S(1)}, bf16[208,256]{1,0:T(8,128)(2,1)S(1)}, u32[]{:S(2)}, u32[]{:S(2)}) collective-permute-start(bf16[208,256]{1,0:T(8,128)(2,1)S(1)} %get-tuple-element.413), channel_id=1, source_target_pairs={{0,4},{1,5},{2,6},{3,7},{4,0},{5,1},{6,2},{7,3},{8,12},{9,13},{10,... | collective-permute-start | bytes 319496 | tf_op jit(solution)/shard_map/ppermute | solution.py:26
  (288 shorter events, 164.7 us)
Async XLA Ops:
  4.2 15.8 %collective-permute-start.2 = (bf16[1024,256]{1,0:T(8,128)(2,1)S(1)}, bf16[1024,256]{1,0:T(8,128)(2,1)S(1)}, u32[]{:S(2)}, u32[]{:S(2)}) collective-permute-start(bf16[1024,256]{1,0:T(8,128)(2,1)S(1)} %get-tuple-element.228), channel_id=1, source_target_pairs={{0,6},{1,7},{2,4},{3,5},{4,2},{5,3},{6,0},{7,1},{8,14},{9,15},{10,... | collective-permute-start | bytes 1572872 | tf_op jit(solution)/shard_map/ppermute | solution.py:26
  5.7 27.0 %collective-permute-start = (bf16[1024,256]{1,0:T(8,128)(2,1)}, bf16[1024,256]{1,0:T(8,128)(2,1)S(1)}, u32[]{:S(2)}, u32[]{:S(2)}) collective-permute-start(bf16[1024,256]{1,0:T(8,128)(2,1)} %get-tuple-element.225), channel_id=1, source_target_pairs={{0,2},{1,3},{2,0},{3,1},{4,6},{5,7},{6,4},{7,5},{8,10},{9,11},{10,... | collective-permute-start | bytes 1572872 | tf_op jit(solution)/shard_map/ppermute | solution.py:26
  7.2 25.5 %collective-permute-start.1 = (bf16[1024,256]{1,0:T(8,128)(2,1)}, bf16[1024,256]{1,0:T(8,128)(2,1)S(1)}, u32[]{:S(2)}, u32[]{:S(2)}) collective-permute-start(bf16[1024,256]{1,0:T(8,128)(2,1)} %get-tuple-element.227), channel_id=1, source_target_pairs={{0,4},{1,5},{2,6},{3,7},{4,0},{5,1},{6,2},{7,3},{8,12},{9,13},{10,... | collective-permute-start | bytes 1572872 | tf_op jit(solution)/shard_map/ppermute | solution.py:26
  20.0 13.2 %collective-permute-start.6 = (bf16[1024,256]{1,0:T(8,128)(2,1)S(1)}, bf16[1024,256]{1,0:T(8,128)(2,1)S(1)}, u32[]{:S(2)}, u32[]{:S(2)}) collective-permute-start(bf16[1024,256]{1,0:T(8,128)(2,1)S(1)} %collective-permute-done.2.refs_3_.refs_7_), channel_id=1, source_target_pairs={{0,1},{1,0},{2,3},{3,2},{4,5},{5,4},{6,7},{7,6},{8,9},{9,8},{10,11... | collective-permute-start | bytes 1572872 | tf_op jit(solution)/shard_map/ppermute | solution.py:30
  20.6 12.1 %all-to-all-start = ((f32[32,1,128]{2,1,0:T(1,128)}), f32[32,1,128]{2,1,0:T(1,128)S(1)}, u32[]{:S(2)}, u32[]{:S(2)}) async-start(f32[32,1,128]{2,1,0:T(1,128)} %broadcast_in_dim.36), calls=%async_computation | async-start | bytes 32768 | tf_op jit(solution)/shard_map/all_to_all | solution.py:890
  34.8 22.0 %collective-permute-start.9 = (bf16[128,1024]{1,0:T(8,128)(2,1)S(1)}, bf16[128,1024]{1,0:T(8,128)(2,1)S(1)}, u32[]{:S(2)}, u32[]{:S(2)}) collective-permute-start(bf16[128,1024]{1,0:T(8,128)(2,1)S(1)} %bitcast.34), channel_id=1, source_target_pairs={{0,4},{1,5},{2,6},{3,7},{4,0},{5,1},{6,2},{7,3},{8,12},{9,13},{10,... | collective-permute-start | bytes 786440 | tf_op jit(solution)/shard_map/ppermute | solution.py:26
  41.5 15.2 %collective-permute-start.10 = (bf16[128,1024]{1,0:T(8,128)(2,1)S(1)}, bf16[128,1024]{1,0:T(8,128)(2,1)S(1)}, u32[]{:S(2)}, u32[]{:S(2)}) collective-permute-start(bf16[128,1024]{1,0:T(8,128)(2,1)S(1)} %collective-permute-done.8.refs_1_), channel_id=1, source_target_pairs={{0,4},{1,5},{2,6},{3,7},{4,0},{5,1},{6,2},{7,3},{8,12},{9,13},{10,... | collective-permute-start | bytes 786440 | tf_op jit(solution)/shard_map/ppermute | solution.py:26
  42.2 12.5 %collective-permute-start.12 = (bf16[64,1024]{1,0:T(8,128)(2,1)S(1)}, bf16[64,1024]{1,0:T(8,128)(2,1)S(1)}, u32[]{:S(2)}, u32[]{:S(2)}) collective-permute-start(bf16[64,1024]{1,0:T(8,128)(2,1)S(1)} %get-tuple-element.237), channel_id=1, source_target_pairs={{0,4},{1,5},{2,6},{3,7},{4,0},{5,1},{6,2},{7,3},{8,12},{9,13},{10,... | collective-permute-start | bytes 393224 | tf_op jit(solution)/shard_map/ppermute | solution.py:26
  43.6 12.6 %collective-permute-start.13 = (bf16[64,1024]{1,0:T(8,128)(2,1)S(1)}, bf16[64,1024]{1,0:T(8,128)(2,1)S(1)}, u32[]{:S(2)}, u32[]{:S(2)}) collective-permute-start(bf16[64,1024]{1,0:T(8,128)(2,1)S(1)} %get-tuple-element.238), channel_id=1, source_target_pairs={{0,6},{1,7},{2,4},{3,5},{4,2},{5,3},{6,0},{7,1},{8,14},{9,15},{10,... | collective-permute-start | bytes 393224 | tf_op jit(solution)/shard_map/ppermute | solution.py:26
  45.1 11.7 %collective-permute-start.11 = (bf16[64,1024]{1,0:T(8,128)(2,1)S(1)}, bf16[64,1024]{1,0:T(8,128)(2,1)S(1)}, u32[]{:S(2)}, u32[]{:S(2)}) collective-permute-start(bf16[64,1024]{1,0:T(8,128)(2,1)S(1)} %get-tuple-element.236), channel_id=1, source_target_pairs={{0,2},{1,3},{2,0},{3,1},{4,6},{5,7},{6,4},{7,5},{8,10},{9,11},{10,... | collective-permute-start | bytes 393224 | tf_op jit(solution)/shard_map/ppermute | solution.py:26
  68.1 12.0 %collective-permute-start.19 = (bf16[128,1024]{1,0:T(8,128)(2,1)S(1)}, bf16[128,1024]{1,0:T(8,128)(2,1)S(1)}, u32[]{:S(2)}, u32[]{:S(2)}) collective-permute-start(bf16[128,1024]{1,0:T(8,128)(2,1)S(1)} %get-tuple-element.261), channel_id=1, source_target_pairs={{0,6},{1,7},{2,4},{3,5},{4,2},{5,3},{6,0},{7,1},{8,14},{9,15},{10,... | collective-permute-start | bytes 786440 | tf_op jit(solution)/shard_map/ppermute | solution.py:26
  135.8 53.4 %all-to-all-start.2 = ((bf16[4,256,1024]{2,1,0:T(8,128)(2,1)}), bf16[4,256,1024]{2,1,0:T(8,128)(2,1)}, u32[]{:S(2)}, u32[]{:S(2)}) async-start(bf16[4,256,1024]{2,1,0:T(8,128)(2,1)} %get-tuple-element.321), calls=%async_computation.2 | async-start | bytes 4194304 | tf_op jit(solution)/shard_map/all_to_all | solution.py:56
  203.8 55.4 %all-to-all-start.3 = ((bf16[4,256,1024]{2,1,0:T(8,128)(2,1)}), bf16[4,256,1024]{2,1,0:T(8,128)(2,1)S(1)}, u32[]{:S(2)}, u32[]{:S(2)}) async-start(bf16[4,256,1024]{2,1,0:T(8,128)(2,1)} %shard_map.291), calls=%async_computation.3 | async-start | bytes 4194304 | tf_op jit(solution)/shard_map/all_to_all | solution.py:56
  224.6 18.8 %collective-permute-start.50 = (bf16[4,512,256]{2,1,0:T(8,128)(2,1)S(1)}, bf16[4,512,256]{2,1,0:T(8,128)(2,1)S(1)}, u32[]{:S(2)}, u32[]{:S(2)}) collective-permute-start(bf16[4,512,256]{2,1,0:T(8,128)(2,1)S(1)} %get-tuple-element.344), channel_id=1, source_target_pairs={{0,1},{1,0},{2,3},{3,2},{4,5},{5,4},{6,7},{7,6},{8,9},{9,8},{10,11... | collective-permute-start | bytes 3145736 | tf_op jit(solution)/shard_map/ppermute | solution.py:30
  224.7 12.2 %collective-permute-start.51 = (bf16[64,1024]{1,0:T(8,128)(2,1)S(1)}, bf16[64,1024]{1,0:T(8,128)(2,1)S(1)}, u32[]{:S(2)}, u32[]{:S(2)}) collective-permute-start(bf16[64,1024]{1,0:T(8,128)(2,1)S(1)} %copy-done.46), channel_id=1, source_target_pairs={{0,2},{1,3},{2,0},{3,1},{4,6},{5,7},{6,4},{7,5},{8,10},{9,11},{10,... | collective-permute-start | bytes 393224 | tf_op jit(solution)/shard_map/ppermute | solution.py:26
  239.9 13.3 %collective-permute-start.56 = (bf16[64,1024]{1,0:T(8,128)(2,1)}, bf16[64,1024]{1,0:T(8,128)(2,1)S(1)}, u32[]{:S(2)}, u32[]{:S(2)}) collective-permute-start(bf16[64,1024]{1,0:T(8,128)(2,1)} %get-tuple-element.360.refs_0_), channel_id=1, source_target_pairs={{0,6},{1,7},{2,4},{3,5},{4,2},{5,3},{6,0},{7,1},{8,14},{9,15},{10,... | collective-permute-start | bytes 393224 | tf_op jit(solution)/shard_map/ppermute | solution.py:26
  259.2 29.8 %all-to-all-start.4 = ((bf16[4,512,256]{2,1,0:T(8,128)(2,1)}), bf16[4,512,256]{2,1,0:T(8,128)(2,1)S(1)}, u32[]{:S(2)}, u32[]{:S(2)}) async-start(bf16[4,512,256]{2,1,0:T(8,128)(2,1)} %shard_map.288), calls=%async_computation.4 | async-start | bytes 2097152 | tf_op jit(solution)/shard_map/all_to_all | solution.py:56
  290.0 37.9 %all-to-all-start.5 = ((bf16[4,544,256]{2,1,0:T(8,128)(2,1)}), bf16[4,544,256]{2,1,0:T(8,128)(2,1)S(1)}, u32[]{:S(2)}, u32[]{:S(2)}) async-start(bf16[4,544,256]{2,1,0:T(8,128)(2,1)} %shard_map.294), calls=%async_computation.5 | async-start | bytes 2228224 | tf_op jit(solution)/shard_map/all_to_all | solution.py:56
  293.5 52.1 %collective-permute-start.65 = (bf16[128,1024]{1,0:T(8,128)(2,1)S(1)}, bf16[128,1024]{1,0:T(8,128)(2,1)}, u32[]{:S(2)}, u32[]{:S(2)}) collective-permute-start(bf16[128,1024]{1,0:T(8,128)(2,1)S(1)} %copy-done.44), channel_id=1, source_target_pairs={{0,0},{1,1},{2,8},{3,9},{4,16},{5,17},{6,24},{7,25},{8,2},{9,3},{1... | collective-permute-start | bytes 786440 | tf_op jit(solution)/shard_map/ppermute | solution.py:1039
  297.8 30.1 %collective-permute-start.58 = (bf16[224,1024]{1,0:T(8,128)(2,1)}, bf16[224,1024]{1,0:T(8,128)(2,1)S(1)}, u32[]{:S(2)}, u32[]{:S(2)}) collective-permute-start(bf16[224,1024]{1,0:T(8,128)(2,1)} %get-tuple-element.396), channel_id=1, source_target_pairs={{0,2},{1,3},{2,0},{3,1},{4,6},{5,7},{6,4},{7,5},{8,10},{9,11},{10,... | collective-permute-start | bytes 1376264 | tf_op jit(solution)/shard_map/ppermute | solution.py:26
  297.9 30.0 %collective-permute-start.59 = (bf16[224,1024]{1,0:T(8,128)(2,1)}, bf16[224,1024]{1,0:T(8,128)(2,1)S(1)}, u32[]{:S(2)}, u32[]{:S(2)}) collective-permute-start(bf16[224,1024]{1,0:T(8,128)(2,1)} %get-tuple-element.397), channel_id=1, source_target_pairs={{0,4},{1,5},{2,6},{3,7},{4,0},{5,1},{6,2},{7,3},{8,12},{9,13},{10,... | collective-permute-start | bytes 1376264 | tf_op jit(solution)/shard_map/ppermute | solution.py:26
  301.2 26.7 %collective-permute-start.60 = (bf16[224,1024]{1,0:T(8,128)(2,1)S(1)}, bf16[224,1024]{1,0:T(8,128)(2,1)S(1)}, u32[]{:S(2)}, u32[]{:S(2)}) collective-permute-start(bf16[224,1024]{1,0:T(8,128)(2,1)S(1)} %copy-done.42), channel_id=1, source_target_pairs={{0,6},{1,7},{2,4},{3,5},{4,2},{5,3},{6,0},{7,1},{8,14},{9,15},{10,... | collective-permute-start | bytes 1376264 | tf_op jit(solution)/shard_map/ppermute | solution.py:26
  330.9 14.7 %collective-permute-start.61 = (bf16[272,256]{1,0:T(8,128)(2,1)S(1)}, bf16[272,256]{1,0:T(8,128)(2,1)S(1)}, u32[]{:S(2)}, u32[]{:S(2)}) collective-permute-start(bf16[272,256]{1,0:T(8,128)(2,1)S(1)} %get-tuple-element.404), channel_id=1, source_target_pairs={{0,0},{1,1},{2,8},{3,9},{4,16},{5,17},{6,24},{7,25},{8,2},{9,3},{1... | collective-permute-start | bytes 417800 | tf_op jit(solution)/shard_map/ppermute | solution.py:1039
  333.3 11.9 %collective-permute-start.63 = (bf16[208,256]{1,0:T(8,128)(2,1)S(1)}, bf16[208,256]{1,0:T(8,128)(2,1)S(1)}, u32[]{:S(2)}, u32[]{:S(2)}) collective-permute-start(bf16[208,256]{1,0:T(8,128)(2,1)S(1)} %get-tuple-element.413), channel_id=1, source_target_pairs={{0,4},{1,5},{2,6},{3,7},{4,0},{5,1},{6,2},{7,3},{8,12},{9,13},{10,... | collective-permute-start | bytes 319496 | tf_op jit(solution)/shard_map/ppermute | solution.py:26
  (106 other events, 785.9 us)

commit v3 on v2

--- a/solution.py
+++ b/solution.py
@@ -1098,13 +1098,12 @@
     c_got, e_one = tie(c_got, e_one)
     (c_total,) = far_call(core_sum_kernel, [(g_shape, BF)], c_mine, c_got)
     (c_total,) = piece(c_total)
-    got_e = then(*got_e)
+    c_total, f_got, *got_e = then(c_total, f_got, *got_e)
+    c_got = across_slots(c_total)
     e_all_one, d_self = far_call(
         self_back_kernel, [(every, BF), ((CHIPS * length, 3 * quarter), BF)], e_one, *got_e, w_out, queries, keys, values, us=4,
         scratch=[pltpu.VMEM(cols, BF)],
     )
-    c_total, d_self, f_got = tie(c_total, d_self, f_got)
-    c_got = across_slots(c_total)
     s_shape = (n_slot, g_shape[1] + 2 * SMALL, quarter)
     s_mine, s_other = far_call(
         self_grads_kernel, [(s_shape, BF)] * 2, x_all, d_self, mixed, e_all_one, c_sums, sum_in, sums_one, sums_two, sums_three

time: 354 us -> 354 us (level)
    unnamed x120 -> x118, local copies, waits for them, and re-layouts: 15.3 us -> 15.3 us
  transfers between devices with their start and end apart: 71 -> 71, of which waited for: 26 -> 25; matrix products, arithmetic and copies ran while one was open for 1% -> 1% of each run, Pallas kernels for 38% -> 38%
where the time goes in v3:
time: 354 us; the launch traced here: 350 us
  Pallas kernels  155 us (44%)
  starting transfers between devices  98.2 us (28%)
  waiting for transfers between devices  68.1 us (19%)
  local copies, waits for them, and re-layouts  16.4 us (5%)
  blocking collectives  9.81 us (3%)
    pallas_call x29, Pallas kernels, call(): pl.pallas_call(kernel, out_shape=places, scratch_shapes=scratch, compiler...  68.9 us
    ppermute x51, starting transfers between devices, from_chip(): return lax.ppermute(x, 'pb', pairs)  65.5 us
    ppermute x51, waiting for transfers between devices, from_chip(): return lax.ppermute(x, 'pb', pairs)  58 us
    pallas_call x4, Pallas kernels, embedding_piece(): pl.pallas_call(functools.partial(embedding_kernel, first), grid=(steps,),...  51.1 us
    all_to_all x4, starting transfers between devices, across_slots(): return lax.all_to_all(x, 'slot', 0, 0, tiled=True)  17.7 us
    unnamed x118, local copies, waits for them, and re-layouts  15.3 us
    pallas_call x2, Pallas kernels, own_embedding(): pl.pallas_call(own_embedding_kernel, grid=(steps,), in_specs=[pl.BlockSpe...  12.9 us
    pallas_call x1, Pallas kernels, state_grad(): pl.pallas_call(state_grad_kernel, grid=(vocab // tile,), in_specs=[pl.Blo...  11 us
  transfers between devices with their start and end apart: 71, of which 25 were waited for; matrix products, arithmetic and copies ran while one was open for 1% of the time, Pallas kernels for 38%

profile of v3, /device:TPU:2, one launch (start us, length us, event | category | flops | bytes accessed | tf_op | source)
XLA Modules:
  0.0 350.0 jit_solution(10933708655257805402)
XLA Ops:
  8.7 11.3 %collective-permute-done.2.refs_3_.refs_7_ = bf16[1024,256]{1,0:T(8,128)(2,1)S(1)} collective-permute-done((bf16[1024,256]{1,0:T(8,128)(2,1)S(1)}, bf16[1024,256]{1,0:T(8,128)(2,1)S(1)}, u32[]{:S(2)}, u32[]{:S(2)}) %collective-permute-start.2) | collective-permute-done | bytes 524320 | tf_op jit(solution)/shard_map/ppermute | solution.py:26
  20.6 6.2 %all-to-all-start = ((f32[32,1,128]{2,1,0:T(1,128)}), f32[32,1,128]{2,1,0:T(1,128)S(1)}, u32[]{:S(2)}, u32[]{:S(2)}) async-start(f32[32,1,128]{2,1,0:T(1,128)} %broadcast_in_dim.36), calls=%async_computation | async-start | bytes 32768 | tf_op jit(solution)/shard_map/all_to_all | solution.py:890
  35.3 4.1 %shard_map.264 = (bf16[256,1024]{1,0:T(8,128)(2,1)S(1)}, bf16[1024,768]{1,0:T(8,128)(2,1)S(1)}, bf16[256,256]{1,0:T(8,128)(2,1)S(1)}, bf16[256,256]{1,0:T(8,128)...) custom-call(bf16[1024,256]{1,0:T(8,128)(2,1)S(1)} %get-tuple-element, ...), custom_call_target="tpu_custom_call" | custom-call | flops 2000000000 | tf_op jit(solution)/shard_map/pallas_call | solution.py:98
  45.8 8.9 %collective-permute-done.12.refs_3_ = bf16[64,1024]{1,0:T(8,128)(2,1)S(1)} collective-permute-done((bf16[64,1024]{1,0:T(8,128)(2,1)S(1)}, bf16[64,1024]{1,0:T(8,128)(2,1)S(1)}, u32[]{:S(2)}, u32[]{:S(2)}) %collective-permute-start.12) | collective-permute-done | bytes 131104 | tf_op jit(solution)/shard_map/ppermute | solution.py:26
  115.3 10.7 %shard_map.274 = (f32[4096,512]{1,0:T(8,128)}, f32[8,128]{1,0:T(8,128)S(1)}) custom-call(bf16[256,1024]{1,0:T(8,128)(2,1)S(1)} %get-tuple-element.279.h0_ref.own_ref, bf16[256,1024]{1,0:T(8,128)(2,1)S(1)} %collective-permute-done.34.h1_ref.pair_ref, s32[1,512]{1,0:T(1,128)S(1)} %concatenate.11.ids_ref, bf16[4096,1024]{1,0:T(8,128)(2,1)} %e_ref.11), custom_call_target="tpu_custom_call" | custom-call | flops 10000000000 | tf_op jit(solution)/shard_map/pallas_call | solution.py:386
  126.0 9.8 %all_to_all.30.all_ref = f32[32,8,128]{2,1,0:T(8,128)S(1)} all-to-all(f32[32,8,128]{2,1,0:T(8,128)S(1)} %broadcast_in_dim.39), channel_id=1, replica_groups=mesh['slot'=4,'pb'=8] {'slot','pb'}, dimensions={0} | all-to-all | bytes 262144 | tf_op jit(solution)/shard_map/all_to_all | solution.py:982
  135.8 4.8 %all-to-all-start.2 = ((bf16[4,256,1024]{2,1,0:T(8,128)(2,1)}), bf16[4,256,1024]{2,1,0:T(8,128)(2,1)}, u32[]{:S(2)}, u32[]{:S(2)}) async-start(bf16[4,256,1024]{2,1,0:T(8,128)(2,1)} %get-tuple-element.320), calls=%async_computation.2 | async-start | bytes 4194304 | tf_op jit(solution)/shard_map/all_to_all | solution.py:56
  141.4 11.0 %shard_map.276 = (f32[256,1024]{1,0:T(8,128)S(1)}, bf16[256,1024]{1,0:T(8,128)(2,1)S(1)}, bf16[4096,512]{1,0:T(8,128)(2,1)}) custom-call(f32[4096,512]{1,0:T(8,128)} %get-tuple-element.286.l_ref, f32[1,2,8,256]{3,2,1,0:T(8,128)S(1)} %get-tuple-element.287.rows_ref, bf16[4096,1024]{1,0:T(8,128)(2,1)} %e_ref.11), custom_call_target="tpu_custom_call" | custom-call | flops 11000000512 | tf_op jit(solution)/shard_map/pallas_call | solution.py:507
  158.0 6.4 %shard_map.278.refs_0_ = f32[4096,1024]{1,0:T(8,128)} custom-call(bf16[4096,512]{1,0:T(8,128)(2,1)} %get-tuple-element.304.d_ref, bf16[256,1024]{1,0:T(8,128)(2,1)S(1)} %get-tuple-element.279.h0_ref.own_ref, bf16[256,1024]{1,0:T(8,128)(2,1)S(1)} %collective-permute-done.34.h1_ref.pair_ref), custom_call_target="tpu_custom_call" | custom-call | flops 1000000000 | tf_op jit(solution)/shard_map/pallas_call | solution.py:539
  169.3 6.5 %shard_map.280.held_ref = f32[4096,1024]{1,0:T(8,128)} custom-call(bf16[4096,512]{1,0:T(8,128)(2,1)} %get-tuple-element.304.d_ref, bf16[256,1024]{1,0:T(8,128)(2,1)S(1)} %get-tuple-element.279.h0_ref.own_ref, bf16[256,1024]{1,0:T(8,128)(2,1)S(1)} %collective-permute-done.34.h1_ref.pair_ref, ...), custom_call_target="tpu_custom_call", output_to_operand_aliasing={{}: (3, {})} | custom-call | flops 1000000000 | tf_op jit(solution)/shard_map/pallas_call | solution.py:539
  175.7 4.2 %shard_map.281 = (bf16[256,1024]{1,0:T(8,128)(2,1)S(1)}, bf16[256,1024]{1,0:T(8,128)(2,1)S(1)}, f32[1,1024]{1,0:T(1,128)S(1)}, f32[64,1024]{1,0:T(8,128)S(1)}, b...) custom-call(bf16[64,1024]{1,0:T(8,128)(2,1)S(1)} %get-tuple-element.303.refs_0_, ...), custom_call_target="tpu_custom_call" | custom-call | flops 2000000000 | tf_op jit(solution)/shard_map/pallas_call | solution.py:98
  183.4 4.6 %shard_map.282 = (bf16[4,256,1024]{2,1,0:T(8,128)(2,1)}, bf16[4,256,1024]{2,1,0:T(8,128)(2,1)}) custom-call(bf16[256,1024]{1,0:T(8,128)(2,1)} %copy-done.14, bf16[256,1024]{1,0:T(8,128)(2,1)S(1)} %get-tuple-element.316.du, bf16[256,1024]{1,0:T(8,128)(2,1)} %copy-done.15, bf16[256,1024]{1,0:T(8,128)(2,1)S(1)} %get-tuple-element.318.e), custom_call_target="tpu_custom_call" | custom-call | flops 3000000000 | tf_op jit(solution)/shard_map/pallas_call | solution.py:98
  193.2 5.1 %collective-permute-done.49.refs_3_ = bf16[64,1024]{1,0:T(8,128)(2,1)S(1)} collective-permute-done((bf16[64,1024]{1,0:T(8,128)(2,1)}, bf16[64,1024]{1,0:T(8,128)(2,1)S(1)}, u32[]{:S(2)}, u32[]{:S(2)}) %collective-permute-start.49) | collective-permute-done | bytes 131104 | tf_op jit(solution)/shard_map/ppermute | solution.py:26
  203.7 4.3 %all-to-all-start.3 = ((bf16[4,256,1024]{2,1,0:T(8,128)(2,1)}), bf16[4,256,1024]{2,1,0:T(8,128)(2,1)S(1)}, u32[]{:S(2)}, u32[]{:S(2)}) async-start(bf16[4,256,1024]{2,1,0:T(8,128)(2,1)} %shard_map.289), calls=%async_computation.3 | async-start | bytes 4194304 | tf_op jit(solution)/shard_map/all_to_all | solution.py:56
  214.8 6.8 %shard_map.284 = (bf16[256,1024]{1,0:T(8,128)(2,1)}, bf16[256,256]{1,0:T(8,128)(2,1)}, bf16[512,256]{1,0:T(8,128)(2,1)}, bf16[512,256]{1,0:T(8,128)(2,1)}, f32[6...) custom-call(bf16[64,1024]{1,0:T(8,128)(2,1)} %get-tuple-element.328.refs_0_, ...), custom_call_target="tpu_custom_call" | custom-call | flops 5000000000 | tf_op jit(solution)/shard_map/pallas_call | solution.py:98
  228.2 8.6 %shard_map.286.held_ref = f32[4096,1024]{1,0:T(8,128)} custom-call(f32[4,2,8,256]{3,2,1,0:T(8,128)S(1)} %get-tuple-element.398.rows_ref, bf16[4,256,1024]{2,1,0:T(8,128)(2,1)} %all-to-all-done.2.own_ref, bf16[4,256,1024]{2,1,0:T(8,128)(2,1)} %collective-permute-done.48.pair_ref, bf16[4096,1024]{1,0:T(8,128)(2,1)} %e_ref.11, ...), custom_call_target="tpu_custom_call", output_to_operand_aliasing={{}: (4, {})} | custom-call | flops 1500000000 | tf_op jit(solution)/shard_map/pallas_call | solution.py:575
  244.6 8.6 %shard_map.290.held_ref = f32[4096,1024]{1,0:T(8,128)} custom-call(f32[4,2,8,256]{3,2,1,0:T(8,128)S(1)} %get-tuple-element.398.rows_ref, bf16[4,256,1024]{2,1,0:T(8,128)(2,1)} %all-to-all-done.2.own_ref, bf16[4,256,1024]{2,1,0:T(8,128)(2,1)} %collective-permute-done.48.pair_ref, bf16[4096,1024]{1,0:T(8,128)(2,1)} %e_ref.11, ...), custom_call_target="tpu_custom_call", output_to_operand_aliasing={{}: (4, {})} | custom-call | flops 1500000000 | tf_op jit(solution)/shard_map/pallas_call | solution.py:575
  259.2 5.2 %shard_map.291 = (bf16[256,1024]{1,0:T(8,128)(2,1)}, bf16[256,768]{1,0:T(8,128)(2,1)}) custom-call(bf16[64,1024]{1,0:T(8,128)(2,1)} %get-tuple-element.365.refs_0_, bf16[64,1024]{1,0:T(8,128)(2,1)} %collective-permute-done.54.refs_1_, bf16[64,1024]{1,0:T(8,128)(2,1)} %copy-done.51, bf16[64,1024]{1,0:T(8,128)(2,1)} %copy-done.49, ...), custom_call_target="tpu_custom_call" | custom-call | flops 4000000000 | tf_op jit(solution)/shard_map/pallas_call | solution.py:98
  267.9 5.6 %shard_map.293 = (f32[192,1024]{1,0:T(8,128)}, bf16[128,1024]{1,0:T(8,128)(2,1)}, bf16[224,1024]{1,0:T(8,128)(2,1)}, bf16[224,1024]{1,0:T(8,128)(2,1)}, bf16[224...) custom-call(bf16[256,768]{1,0:T(8,128)(2,1)} %get-tuple-element.372.d, bf16[1024,768]{1,0:T(8,128)(2,1)} %copy-done.9, ...), custom_call_target="tpu_custom_call" | custom-call | flops 3000000000 | tf_op jit(solution)/shard_map/pallas_call | solution.py:98
  277.4 8.6 %shard_map.295.held_ref = f32[4096,1024]{1,0:T(8,128)} custom-call(f32[4,2,8,256]{3,2,1,0:T(8,128)S(1)} %get-tuple-element.398.rows_ref, bf16[4,256,1024]{2,1,0:T(8,128)(2,1)} %all-to-all-done.2.own_ref, bf16[4,256,1024]{2,1,0:T(8,128)(2,1)} %collective-permute-done.48.pair_ref, bf16[4096,1024]{1,0:T(8,128)(2,1)} %e_ref.11, ...), custom_call_target="tpu_custom_call", output_to_operand_aliasing={{}: (4, {})} | custom-call | flops 1500000000 | tf_op jit(solution)/shard_map/pallas_call | solution.py:575
  287.0 5.1 %all-to-all-start.5 = ((bf16[4,544,256]{2,1,0:T(8,128)(2,1)}), bf16[4,544,256]{2,1,0:T(8,128)(2,1)S(1)}, u32[]{:S(2)}, u32[]{:S(2)}) async-start(bf16[4,544,256]{2,1,0:T(8,128)(2,1)} %shard_map.294), calls=%async_computation.5 | async-start | bytes 2228224 | tf_op jit(solution)/shard_map/all_to_all | solution.py:56
  292.1 4.9 %collective-permute-start.65 = (bf16[128,1024]{1,0:T(8,128)(2,1)S(1)}, bf16[128,1024]{1,0:T(8,128)(2,1)}, u32[]{:S(2)}, u32[]{:S(2)}) collective-permute-start(bf16[128,1024]{1,0:T(8,128)(2,1)S(1)} %copy-done.44), channel_id=1, source_target_pairs={{0,0},{1,1},{2,8},{3,9},{4,16},{5,17},{6,24},{7,25},{8,2},{9,3},{1... | collective-permute-start | bytes 786440 | tf_op jit(solution)/shard_map/ppermute | solution.py:1039
  301.7 25.3 %shard_map.296 = f32[4096,1024]{1,0:T(8,128)} custom-call(f32[4,2,8,256]{3,2,1,0:T(8,128)S(1)} %get-tuple-element.398.rows_ref, bf16[4,256,1024]{2,1,0:T(8,128)(2,1)} %all-to-all-done.2.own_ref, bf16[4,256,1024]{2,1,0:T(8,128)(2,1)} %collective-permute-done.48.pair_ref, bf16[4096,1024]{1,0:T(8,128)(2,1)} %e_ref.11, ...), custom_call_target="tpu_custom_call", output_to_operand_aliasing={{}: (4, {})} | custom-call | flops 7500000256 | tf_op jit(solution)/shard_map/pallas_call | solution.py:575
  333.6 6.4 %collective-permute-start.63 = (bf16[208,256]{1,0:T(8,128)(2,1)S(1)}, bf16[208,256]{1,0:T(8,128)(2,1)S(1)}, u32[]{:S(2)}, u32[]{:S(2)}) collective-permute-start(bf16[208,256]{1,0:T(8,128)(2,1)S(1)} %get-tuple-element.411), channel_id=1, source_target_pairs={{0,4},{1,5},{2,6},{3,7},{4,0},{5,1},{6,2},{7,3},{8,12},{9,13},{10,... | collective-permute-start | bytes 319496 | tf_op jit(solution)/shard_map/ppermute | solution.py:26
  (286 shorter events, 165.1 us)
Async XLA Ops:
  4.2 15.8 %collective-permute-start.2 = (bf16[1024,256]{1,0:T(8,128)(2,1)S(1)}, bf16[1024,256]{1,0:T(8,128)(2,1)S(1)}, u32[]{:S(2)}, u32[]{:S(2)}) collective-permute-start(bf16[1024,256]{1,0:T(8,128)(2,1)S(1)} %get-tuple-element.227), channel_id=1, source_target_pairs={{0,6},{1,7},{2,4},{3,5},{4,2},{5,3},{6,0},{7,1},{8,14},{9,15},{10,... | collective-permute-start | bytes 1572872 | tf_op jit(solution)/shard_map/ppermute | solution.py:26
  5.7 27.0 %collective-permute-start = (bf16[1024,256]{1,0:T(8,128)(2,1)}, bf16[1024,256]{1,0:T(8,128)(2,1)S(1)}, u32[]{:S(2)}, u32[]{:S(2)}) collective-permute-start(bf16[1024,256]{1,0:T(8,128)(2,1)} %get-tuple-element.224), channel_id=1, source_target_pairs={{0,2},{1,3},{2,0},{3,1},{4,6},{5,7},{6,4},{7,5},{8,10},{9,11},{10,... | collective-permute-start | bytes 1572872 | tf_op jit(solution)/shard_map/ppermute | solution.py:26
  7.2 25.5 %collective-permute-start.1 = (bf16[1024,256]{1,0:T(8,128)(2,1)}, bf16[1024,256]{1,0:T(8,128)(2,1)S(1)}, u32[]{:S(2)}, u32[]{:S(2)}) collective-permute-start(bf16[1024,256]{1,0:T(8,128)(2,1)} %get-tuple-element.226), channel_id=1, source_target_pairs={{0,4},{1,5},{2,6},{3,7},{4,0},{5,1},{6,2},{7,3},{8,12},{9,13},{10,... | collective-permute-start | bytes 1572872 | tf_op jit(solution)/shard_map/ppermute | solution.py:26
  20.0 13.2 %collective-permute-start.6 = (bf16[1024,256]{1,0:T(8,128)(2,1)S(1)}, bf16[1024,256]{1,0:T(8,128)(2,1)S(1)}, u32[]{:S(2)}, u32[]{:S(2)}) collective-permute-start(bf16[1024,256]{1,0:T(8,128)(2,1)S(1)} %collective-permute-done.2.refs_3_.refs_7_), channel_id=1, source_target_pairs={{0,1},{1,0},{2,3},{3,2},{4,5},{5,4},{6,7},{7,6},{8,9},{9,8},{10,11... | collective-permute-start | bytes 1572872 | tf_op jit(solution)/shard_map/ppermute | solution.py:30
  20.6 12.1 %all-to-all-start = ((f32[32,1,128]{2,1,0:T(1,128)}), f32[32,1,128]{2,1,0:T(1,128)S(1)}, u32[]{:S(2)}, u32[]{:S(2)}) async-start(f32[32,1,128]{2,1,0:T(1,128)} %broadcast_in_dim.36), calls=%async_computation | async-start | bytes 32768 | tf_op jit(solution)/shard_map/all_to_all | solution.py:890
  34.8 22.0 %collective-permute-start.9 = (bf16[128,1024]{1,0:T(8,128)(2,1)S(1)}, bf16[128,1024]{1,0:T(8,128)(2,1)S(1)}, u32[]{:S(2)}, u32[]{:S(2)}) collective-permute-start(bf16[128,1024]{1,0:T(8,128)(2,1)S(1)} %bitcast.34), channel_id=1, source_target_pairs={{0,4},{1,5},{2,6},{3,7},{4,0},{5,1},{6,2},{7,3},{8,12},{9,13},{10,... | collective-permute-start | bytes 786440 | tf_op jit(solution)/shard_map/ppermute | solution.py:26
  41.5 15.2 %collective-permute-start.10 = (bf16[128,1024]{1,0:T(8,128)(2,1)S(1)}, bf16[128,1024]{1,0:T(8,128)(2,1)S(1)}, u32[]{:S(2)}, u32[]{:S(2)}) collective-permute-start(bf16[128,1024]{1,0:T(8,128)(2,1)S(1)} %collective-permute-done.8.refs_1_), channel_id=1, source_target_pairs={{0,4},{1,5},{2,6},{3,7},{4,0},{5,1},{6,2},{7,3},{8,12},{9,13},{10,... | collective-permute-start | bytes 786440 | tf_op jit(solution)/shard_map/ppermute | solution.py:26
  42.2 12.5 %collective-permute-start.12 = (bf16[64,1024]{1,0:T(8,128)(2,1)S(1)}, bf16[64,1024]{1,0:T(8,128)(2,1)S(1)}, u32[]{:S(2)}, u32[]{:S(2)}) collective-permute-start(bf16[64,1024]{1,0:T(8,128)(2,1)S(1)} %get-tuple-element.236), channel_id=1, source_target_pairs={{0,4},{1,5},{2,6},{3,7},{4,0},{5,1},{6,2},{7,3},{8,12},{9,13},{10,... | collective-permute-start | bytes 393224 | tf_op jit(solution)/shard_map/ppermute | solution.py:26
  43.6 12.6 %collective-permute-start.13 = (bf16[64,1024]{1,0:T(8,128)(2,1)S(1)}, bf16[64,1024]{1,0:T(8,128)(2,1)S(1)}, u32[]{:S(2)}, u32[]{:S(2)}) collective-permute-start(bf16[64,1024]{1,0:T(8,128)(2,1)S(1)} %get-tuple-element.237), channel_id=1, source_target_pairs={{0,6},{1,7},{2,4},{3,5},{4,2},{5,3},{6,0},{7,1},{8,14},{9,15},{10,... | collective-permute-start | bytes 393224 | tf_op jit(solution)/shard_map/ppermute | solution.py:26
  68.1 12.0 %collective-permute-start.19 = (bf16[128,1024]{1,0:T(8,128)(2,1)S(1)}, bf16[128,1024]{1,0:T(8,128)(2,1)S(1)}, u32[]{:S(2)}, u32[]{:S(2)}) collective-permute-start(bf16[128,1024]{1,0:T(8,128)(2,1)S(1)} %get-tuple-element.260), channel_id=1, source_target_pairs={{0,6},{1,7},{2,4},{3,5},{4,2},{5,3},{6,0},{7,1},{8,14},{9,15},{10,... | collective-permute-start | bytes 786440 | tf_op jit(solution)/shard_map/ppermute | solution.py:26
  135.8 53.4 %all-to-all-start.2 = ((bf16[4,256,1024]{2,1,0:T(8,128)(2,1)}), bf16[4,256,1024]{2,1,0:T(8,128)(2,1)}, u32[]{:S(2)}, u32[]{:S(2)}) async-start(bf16[4,256,1024]{2,1,0:T(8,128)(2,1)} %get-tuple-element.320), calls=%async_computation.2 | async-start | bytes 4194304 | tf_op jit(solution)/shard_map/all_to_all | solution.py:56
  203.7 51.9 %all-to-all-start.3 = ((bf16[4,256,1024]{2,1,0:T(8,128)(2,1)}), bf16[4,256,1024]{2,1,0:T(8,128)(2,1)S(1)}, u32[]{:S(2)}, u32[]{:S(2)}) async-start(bf16[4,256,1024]{2,1,0:T(8,128)(2,1)} %shard_map.289), calls=%async_computation.3 | async-start | bytes 4194304 | tf_op jit(solution)/shard_map/all_to_all | solution.py:56
  224.6 18.8 %collective-permute-start.50 = (bf16[4,512,256]{2,1,0:T(8,128)(2,1)S(1)}, bf16[4,512,256]{2,1,0:T(8,128)(2,1)S(1)}, u32[]{:S(2)}, u32[]{:S(2)}) collective-permute-start(bf16[4,512,256]{2,1,0:T(8,128)(2,1)S(1)} %get-tuple-element.343), channel_id=1, source_target_pairs={{0,1},{1,0},{2,3},{3,2},{4,5},{5,4},{6,7},{7,6},{8,9},{9,8},{10,11... | collective-permute-start | bytes 3145736 | tf_op jit(solution)/shard_map/ppermute | solution.py:30
  224.6 12.2 %collective-permute-start.51 = (bf16[64,1024]{1,0:T(8,128)(2,1)S(1)}, bf16[64,1024]{1,0:T(8,128)(2,1)S(1)}, u32[]{:S(2)}, u32[]{:S(2)}) collective-permute-start(bf16[64,1024]{1,0:T(8,128)(2,1)S(1)} %copy-done.46), channel_id=1, source_target_pairs={{0,2},{1,3},{2,0},{3,1},{4,6},{5,7},{6,4},{7,5},{8,10},{9,11},{10,... | collective-permute-start | bytes 393224 | tf_op jit(solution)/shard_map/ppermute | solution.py:26
  239.9 13.3 %collective-permute-start.56 = (bf16[64,1024]{1,0:T(8,128)(2,1)}, bf16[64,1024]{1,0:T(8,128)(2,1)S(1)}, u32[]{:S(2)}, u32[]{:S(2)}) collective-permute-start(bf16[64,1024]{1,0:T(8,128)(2,1)} %get-tuple-element.365.refs_0_), channel_id=1, source_target_pairs={{0,6},{1,7},{2,4},{3,5},{4,2},{5,3},{6,0},{7,1},{8,14},{9,15},{10,... | collective-permute-start | bytes 393224 | tf_op jit(solution)/shard_map/ppermute | solution.py:26
  255.6 30.3 %all-to-all-start.4 = ((bf16[4,512,256]{2,1,0:T(8,128)(2,1)}), bf16[4,512,256]{2,1,0:T(8,128)(2,1)S(1)}, u32[]{:S(2)}, u32[]{:S(2)}) async-start(bf16[4,512,256]{2,1,0:T(8,128)(2,1)} %shard_map.288), calls=%async_computation.4 | async-start | bytes 2097152 | tf_op jit(solution)/shard_map/all_to_all | solution.py:56
  287.0 40.1 %all-to-all-start.5 = ((bf16[4,544,256]{2,1,0:T(8,128)(2,1)}), bf16[4,544,256]{2,1,0:T(8,128)(2,1)S(1)}, u32[]{:S(2)}, u32[]{:S(2)}) async-start(bf16[4,544,256]{2,1,0:T(8,128)(2,1)} %shard_map.294), calls=%async_computation.5 | async-start | bytes 2228224 | tf_op jit(solution)/shard_map/all_to_all | solution.py:56
  292.1 54.1 %collective-permute-start.65 = (bf16[128,1024]{1,0:T(8,128)(2,1)S(1)}, bf16[128,1024]{1,0:T(8,128)(2,1)}, u32[]{:S(2)}, u32[]{:S(2)}) collective-permute-start(bf16[128,1024]{1,0:T(8,128)(2,1)S(1)} %copy-done.44), channel_id=1, source_target_pairs={{0,0},{1,1},{2,8},{3,9},{4,16},{5,17},{6,24},{7,25},{8,2},{9,3},{1... | collective-permute-start | bytes 786440 | tf_op jit(solution)/shard_map/ppermute | solution.py:1039
  296.9 30.1 %collective-permute-start.58 = (bf16[224,1024]{1,0:T(8,128)(2,1)}, bf16[224,1024]{1,0:T(8,128)(2,1)S(1)}, u32[]{:S(2)}, u32[]{:S(2)}) collective-permute-start(bf16[224,1024]{1,0:T(8,128)(2,1)} %get-tuple-element.394), channel_id=1, source_target_pairs={{0,2},{1,3},{2,0},{3,1},{4,6},{5,7},{6,4},{7,5},{8,10},{9,11},{10,... | collective-permute-start | bytes 1376264 | tf_op jit(solution)/shard_map/ppermute | solution.py:26
  297.0 30.0 %collective-permute-start.59 = (bf16[224,1024]{1,0:T(8,128)(2,1)}, bf16[224,1024]{1,0:T(8,128)(2,1)S(1)}, u32[]{:S(2)}, u32[]{:S(2)}) collective-permute-start(bf16[224,1024]{1,0:T(8,128)(2,1)} %get-tuple-element.395), channel_id=1, source_target_pairs={{0,4},{1,5},{2,6},{3,7},{4,0},{5,1},{6,2},{7,3},{8,12},{9,13},{10,... | collective-permute-start | bytes 1376264 | tf_op jit(solution)/shard_map/ppermute | solution.py:26
  300.4 26.7 %collective-permute-start.60 = (bf16[224,1024]{1,0:T(8,128)(2,1)S(1)}, bf16[224,1024]{1,0:T(8,128)(2,1)S(1)}, u32[]{:S(2)}, u32[]{:S(2)}) collective-permute-start(bf16[224,1024]{1,0:T(8,128)(2,1)S(1)} %copy-done.42), channel_id=1, source_target_pairs={{0,6},{1,7},{2,4},{3,5},{4,2},{5,3},{6,0},{7,1},{8,14},{9,15},{10,... | collective-permute-start | bytes 1376264 | tf_op jit(solution)/shard_map/ppermute | solution.py:26
  330.0 16.1 %collective-permute-start.61 = (bf16[272,256]{1,0:T(8,128)(2,1)S(1)}, bf16[272,256]{1,0:T(8,128)(2,1)S(1)}, u32[]{:S(2)}, u32[]{:S(2)}) collective-permute-start(bf16[272,256]{1,0:T(8,128)(2,1)S(1)} %get-tuple-element.402), channel_id=1, source_target_pairs={{0,0},{1,1},{2,8},{3,9},{4,16},{5,17},{6,24},{7,25},{8,2},{9,3},{1... | collective-permute-start | bytes 417800 | tf_op jit(solution)/shard_map/ppermute | solution.py:1039
  332.0 12.4 %collective-permute-start.62 = (bf16[208,256]{1,0:T(8,128)(2,1)S(1)}, bf16[208,256]{1,0:T(8,128)(2,1)S(1)}, u32[]{:S(2)}, u32[]{:S(2)}) collective-permute-start(bf16[208,256]{1,0:T(8,128)(2,1)S(1)} %get-tuple-element.410), channel_id=1, source_target_pairs={{0,2},{1,3},{2,0},{3,1},{4,6},{5,7},{6,4},{7,5},{8,10},{9,11},{10,... | collective-permute-start | bytes 319496 | tf_op jit(solution)/shard_map/ppermute | solution.py:26
  333.6 12.5 %collective-permute-start.63 = (bf16[208,256]{1,0:T(8,128)(2,1)S(1)}, bf16[208,256]{1,0:T(8,128)(2,1)S(1)}, u32[]{:S(2)}, u32[]{:S(2)}) collective-permute-start(bf16[208,256]{1,0:T(8,128)(2,1)S(1)} %get-tuple-element.411), channel_id=1, source_target_pairs={{0,4},{1,5},{2,6},{3,7},{4,0},{5,1},{6,2},{7,3},{8,12},{9,13},{10,... | collective-permute-start | bytes 319496 | tf_op jit(solution)/shard_map/ppermute | solution.py:26
  (105 other events, 792.6 us)
